TPU v7x, 512 devices: a whole 4x8x8 slice. The times are simulated.
512 devices in a mesh: fsdp: 32 (over y, x_hi, core), tensor: 16 (over x_lo, z).
Axes of the slice: x: 4 (x_hi: 2, x_lo: 2; x = x_hi * 2 + x_lo), y: 8, z: 8, core: 2. Of those that a mesh axis runs over, the one named last changes fastest.
Arguments:
- out_grad: bfloat16 [4096, 8192], P(('fsdp', 'tensor')), may hold values from -24 to 24
- live_rows: int32 [512], P(('fsdp', 'tensor')), may hold values from 1 to 8, as said below
- gate_pre: bfloat16 [4096, 12288], P('fsdp', 'tensor'), may hold values from -8 to 8
- up_pre: bfloat16 [4096, 12288], P('fsdp', 'tensor'), may hold values from -6 to 6
- down_weight: bfloat16 [12288, 8192], P('tensor', 'fsdp'), may hold values from -0.15625 to 0.15625
- tile_mask: int32 [96, 64], P('tensor'), may hold values from 0 to 1, as said below
Outputs:
- d_gate: bfloat16 [4096, 12288], P('fsdp', 'tensor')
- d_up: bfloat16 [4096, 12288], P('fsdp', 'tensor')
- d_weight: bfloat16 [12288, 8192], P('tensor', 'fsdp')
Inputs may be any that keep to these rules, and one draw needn't show every extreme that they name: `tile_mask`: each device's shard of 6 x 2 tiles holds 1 to 4 kept tiles; in every draw the shards of some tensor index all hold exactly 4, and every tensor index has a shard holding 4. `live_rows`: some device has all 8 rows live in every draw.
All inputs are finite; a program needn't handle non-finite values.
Results may differ from a plain program's by a relative error of at most 0.015.
Values may be sent and summed in bfloat16 or wider, within the bound.
No kernel may reach another device: no remote copies, remote signals or barrier semaphores. Data moves between devices by JAX's collectives and lax.ppermute only.
A program may use at most 64 MiB of HBM per device.

v0:
```python
import math

import jax
import jax.numpy as jnp
from jax import lax
from jax.experimental import pallas as pl
from jax.experimental.pallas import tpu as pltpu
from jax.sharding import PartitionSpec as P


BLK = 128
CAP = 4
TAB = 8


VMEM = pl.BlockSpec(memory_space=pltpu.VMEM)
SMEM = pl.BlockSpec(memory_space=pltpu.SMEM)


def prep_kernel(f_ref, live_ref, mask_ref, grad_ref, weight_ref, masked_ref, packed_ref):
    row_blocks = mask_ref.shape[0]
    rows = lax.broadcasted_iota(jnp.int32, grad_ref.shape, 0)
    value = grad_ref[...].astype(jnp.float32)
    masked_ref[...] = jnp.where(rows < live_ref[0], value, 0.0).astype(jnp.bfloat16)
    packed_ref[...] = jnp.zeros_like(packed_ref)
    count = jnp.int32(0)
    for r in range(row_blocks):
        for c in range(2):
            kept = mask_ref[r, 2 * f_ref[0] + c]

            @pl.when(kept == 1)
            def _(r=r, c=c, count=count):
                packed_ref[count] = weight_ref[
                    r * BLK : (r + 1) * BLK, c * BLK : (c + 1) * BLK
                ]

            count = count + kept


def table_kernel(f_ref, mask_ref, gate_ref, up_ref, table_ref, hidden_ref):
    row_blocks = mask_ref.shape[0]
    core = lax.rem(f_ref[0], 2)

    def one_shard(s, carry):
        f = 2 * s + core
        base = s * TAB
        for k in range(TAB):
            table_ref[base + k] = 0
        count = jnp.int32(0)
        for r in range(row_blocks):
            for c in range(2):
                table_ref[base + count] = 2 * r + c
                count = count + mask_ref[r, 2 * f + c]
        return carry

    lax.fori_loop(0, table_ref.shape[0] // TAB, one_shard, 0)
    gate = gate_ref[...].astype(jnp.float32)
    up = up_ref[...].astype(jnp.float32)
    hidden = gate * jax.nn.sigmoid(gate) * up
    hidden_ref[...] = hidden.T.astype(jnp.bfloat16)


def partial_kernel(scale, dest_ref, table_ref, core_ref, own_h, other_h, own_p, other_p, out_ref):
    dest = dest_ref[pl.program_id(0)]
    wide = 2 * BLK
    for xh in range(2):
        s = 2 * dest + xh
        at = pl.multiple_of((2 * xh + core_ref[0]) * wide, wide)
        right = jnp.concatenate([own_p[:, pl.ds(at, wide)], other_p[:, pl.ds(at, wide)]], axis=0)
        places = [table_ref[s * TAB + k] for k in range(CAP)]
        rows = [pl.multiple_of((b >> 1) * BLK, BLK) for b in places]
        left = jnp.concatenate(
            [
                jnp.concatenate([own_h[pl.ds(r, BLK), :], other_h[pl.ds(r, BLK), :]], axis=1)
                for r in rows
            ],
            axis=0,
        )
        term = jnp.dot(left, right, preferred_element_type=jnp.float32) * scale
        for k, b in enumerate(places):
            tile = term[k * BLK : (k + 1) * BLK]
            kept = jnp.where((b & 1) == 0, tile[:, :BLK], tile[:, BLK:])
            out_ref[0, xh, k] = kept.astype(jnp.bfloat16)


def hidden_grad_kernel(
    table_ref, core_ref, own_p, other_p, weight_ref, own_ref, other_ref
):
    group = pl.program_id(0)
    shards = weight_ref.shape[0]
    wide = 2 * BLK
    rows = own_p.shape[0]

    @pl.when(group == 0)
    def _():
        own_ref[...] = jnp.zeros_like(own_ref)
        other_ref[...] = jnp.zeros_like(other_ref)

    for i in range(shards):
        s = group * shards + i
        at = pl.multiple_of((2 * i + core_ref[0]) * wide, wide)
        left = jnp.concatenate([own_p[:, pl.ds(at, wide)], other_p[:, pl.ds(at, wide)]], axis=0)
        places = [table_ref[s * TAB + k] for k in range(CAP)]
        halves = []
        for k, b in enumerate(places):
            tile = weight_ref[i, k].astype(jnp.float32)
            second = (b & 1) == 1
            zero = jnp.zeros_like(tile)
            halves.append(
                jnp.concatenate(
                    [jnp.where(second, zero, tile), jnp.where(second, tile, zero)], axis=1
                ).astype(jnp.bfloat16)
            )
        term = lax.dot_general(
            left,
            jnp.concatenate(halves, axis=0),
            (((1,), (1,)), ((), ())),
            preferred_element_type=jnp.float32,
        )
        for k, b in enumerate(places):
            r = pl.multiple_of((b >> 1) * BLK, BLK)
            part = term[:, k * BLK : (k + 1) * BLK]
            own_ref[:, pl.ds(r, BLK)] += part[:rows]
            other_ref[:, pl.ds(r, BLK)] += part[rows:]


def combine_kernel(xh_ref, part_ref, up_ref, down_ref, own_ref, send_ref):
    def total(i):
        return (
            part_ref[0, i].astype(jnp.float32)
            + up_ref[i].astype(jnp.float32)
            + down_ref[i].astype(jnp.float32)
        )

    own_ref[...] = total(xh_ref[0])
    send_ref[...] = total(1 - xh_ref[0]).astype(jnp.bfloat16)


def gates_kernel(own_ref, other_ref, gate_ref, up_ref, d_gate_ref, d_up_ref):
    d_hidden = own_ref[...] + other_ref[...]
    gate = gate_ref[...].astype(jnp.float32)
    up = up_ref[...].astype(jnp.float32)
    s = jax.nn.sigmoid(gate)
    d_up_ref[...] = (d_hidden * gate * s).astype(jnp.bfloat16)
    d_gate_ref[...] = (d_hidden * up * s * (1.0 + gate * (1.0 - s))).astype(jnp.bfloat16)


def place_kernel(f_ref, mask_ref, own_ref, other_ref, out_ref):
    row_blocks = mask_ref.shape[0]
    out_ref[...] = jnp.zeros_like(out_ref)
    count = jnp.int32(0)
    for r in range(row_blocks):
        for c in range(2):
            kept = mask_ref[r, 2 * f_ref[0] + c]

            @pl.when(kept == 1)
            def _(r=r, c=c, count=count):
                total = own_ref[count] + other_ref[count].astype(jnp.float32)
                out_ref[r * BLK : (r + 1) * BLK, c * BLK : (c + 1) * BLK] = total.astype(
                    jnp.bfloat16
                )

            count = count + kept


def shape(dims, dtype=jnp.bfloat16):
    return jax.ShapeDtypeStruct(dims, dtype)


def cost(flops, size):
    return pl.CostEstimate(flops=flops, bytes_accessed=size, transcendentals=0)


def per_device(out_grad, live_rows, gate_pre, up_pre, down_weight, tile_mask):
    fsdp_count = lax.axis_size("fsdp")
    tensor_count = lax.axis_size("tensor")
    f = lax.axis_index("fsdp")
    t = lax.axis_index("tensor")
    ring_y = fsdp_count // 4
    ring_z = tensor_count // 2
    y, xh = f >> 2, (f >> 1) & 1
    xl, z = t >> (ring_z.bit_length() - 1), t & (ring_z - 1)
    tok, width = out_grad.shape
    rows, units = gate_pre.shape
    scale = 1.0 / math.sqrt(rows * fsdp_count)
    f_arr = f.reshape(1).astype(jnp.int32)

    def over_f(x, move):
        return lax.ppermute(x, "fsdp", [(i, move(i)) for i in range(fsdp_count)])

    def over_t(x, move):
        return lax.ppermute(x, "tensor", [(i, move(i)) for i in range(tensor_count)])

    def y_step(x, d):
        return over_f(x, lambda i: (i + 4 * d) % fsdp_count)

    def z_step(x, d):
        return over_t(x, lambda i: (i // ring_z) * ring_z + (i + d) % ring_z)

    def swap_core(x):
        return over_f(x, lambda i: i ^ 1)

    def swap_xh(x):
        return over_f(x, lambda i: i ^ 2)

    def swap_xl(x):
        return over_t(x, lambda i: (i + ring_z) % tensor_count)

    masked, packed = pl.pallas_call(
        prep_kernel,
        out_shape=(shape((tok, width)), shape((CAP, BLK, BLK))),
        in_specs=[SMEM, SMEM, SMEM, VMEM, VMEM],
        out_specs=(VMEM, VMEM),
        name="prep",
        cost_estimate=cost(1000, 1 << 20),
    )(f_arr, live_rows, tile_mask, out_grad, down_weight)
    masked_other = swap_xl(masked)
    packed_other = swap_xh(packed)

    shard_count = fsdp_count // 2
    table, hidden_t = pl.pallas_call(
        table_kernel,
        out_shape=(shape((shard_count * TAB,), jnp.int32), shape((units, rows))),
        in_specs=[SMEM, SMEM, VMEM, VMEM],
        out_specs=(SMEM, VMEM),
        name="hidden",
        cost_estimate=cost(1000, 1 << 20),
    )(f_arr, tile_mask, gate_pre, up_pre)
    hidden_other = swap_core(hidden_t)

    def pair(own, other, index):
        first = jnp.where(index == 0, own, other)
        second = jnp.where(index == 0, other, own)
        return jnp.stack([first, second])

    def gather(block, step, index, count):
        full = jnp.zeros((2, count) + block.shape[1:], block.dtype)

        def put(full, piece, at):
            start = (0, at & (count - 1)) + (0,) * (block.ndim - 1)
            return lax.dynamic_update_slice(full, piece[:, None], start)

        full = put(full, block, index)
        up = down = block
        for d in range(1, count // 2 + 1):
            up = step(up, 1)
            full = put(full, up, index - d + count)
            if d < count // 2:
                down = step(down, -1)
                full = put(full, down, index + d)
        return full

    panel = gather(pair(masked, masked_other, xl), z_step, z, ring_z).reshape(rows, width)
    weights = gather(pair(packed, packed_other, xh), y_step, y, ring_y)
    weights = weights.transpose(1, 0, 2, 3, 4).reshape(shard_count, CAP, BLK, BLK)
    panel_other = swap_core(panel)
    core_arr = (f & 1).reshape(1).astype(jnp.int32)

    def partials(*offsets):
        count = len(offsets)
        dests = jnp.stack([(y + d + ring_y) & (ring_y - 1) for d in offsets]).astype(jnp.int32)
        panel_spec = pl.BlockSpec((rows, width // ring_y), lambda i, ds, tab, cr: (0, ds[i]))
        whole = pl.BlockSpec((units, rows), lambda i, ds, tab, cr: (0, 0))

        def body(*refs):
            partial_kernel(scale, *refs)

        return pl.pallas_call(
            body,
            out_shape=shape((count, 2, CAP, BLK, BLK)),
            grid_spec=pltpu.PrefetchScalarGridSpec(
                num_scalar_prefetch=3,
                grid=(count,),
                in_specs=[whole, whole, panel_spec, panel_spec],
                out_specs=pl.BlockSpec(
                    (1, 2, CAP, BLK, BLK), lambda i, ds, tab, cr: (i, 0, 0, 0, 0)
                ),
            ),
            name="partial",
            cost_estimate=cost(count * 8 * 2 * BLK * BLK * 2 * rows, count << 18),
        )(dests, table, core_arr, hidden_t, hidden_other, panel, panel_other)

    def added(part, running):
        return (part.astype(jnp.float32) + running.astype(jnp.float32)).astype(jnp.bfloat16)

    half = ring_y // 2
    send_up = partials(half)[0]
    down = None
    for d in range(half, 0, -1):
        up = y_step(send_up, 1)
        if d == half:
            part = partials(d - 1, 1 - d)
            send_down = part[1]
            send_up = added(part[0], up)
            continue
        down = y_step(send_down, -1)
        if d > 1:
            part = partials(d - 1, 1 - d)
            send_up = added(part[0], up)
            send_down = added(part[1], down)
    here = partials(0)
    own_sum, send_sum = pl.pallas_call(
        combine_kernel,
        out_shape=(shape((CAP, BLK, BLK), jnp.float32), shape((CAP, BLK, BLK))),
        in_specs=[SMEM, VMEM, VMEM, VMEM],
        out_specs=(VMEM, VMEM),
        name="combine",
        cost_estimate=cost(1000, 1 << 20),
    )(xh.reshape(1).astype(jnp.int32), here, up, down)
    other_sum = swap_xh(send_sum)

    groups = 4
    per_group = shard_count // groups
    acc_spec = pl.BlockSpec((rows, units), lambda i, tab, cr: (0, 0))
    panel_spec = pl.BlockSpec((rows, width // groups), lambda i, tab, cr: (0, i))
    own_part, sent_part = pl.pallas_call(
        hidden_grad_kernel,
        out_shape=(shape((rows, units), jnp.float32), shape((rows, units), jnp.float32)),
        grid_spec=pltpu.PrefetchScalarGridSpec(
            num_scalar_prefetch=2,
            grid=(groups,),
            in_specs=[
                panel_spec,
                panel_spec,
                pl.BlockSpec((per_group, CAP, BLK, BLK), lambda i, tab, cr: (i, 0, 0, 0)),
            ],
            out_specs=(acc_spec, acc_spec),
        ),
        name="hidden_grad",
        cost_estimate=cost(shard_count * CAP * 4 * rows * BLK * BLK, 6 << 20),
    )(table, core_arr, panel, panel_other, weights)
    other_part = swap_core(sent_part)
    d_gate, d_up = pl.pallas_call(
        gates_kernel,
        out_shape=(shape((rows, units)), shape((rows, units))),
        in_specs=[VMEM] * 4,
        out_specs=(VMEM, VMEM),
        name="gates",
        cost_estimate=cost(1000, 3 << 19),
    )(own_part, other_part, gate_pre, up_pre)
    d_weight = pl.pallas_call(
        place_kernel,
        out_shape=shape(down_weight.shape),
        in_specs=[SMEM, SMEM, VMEM, VMEM],
        out_specs=VMEM,
        name="place",
        cost_estimate=cost(1000, 1 << 20),
    )(f_arr, tile_mask, own_sum, other_sum)
    return (d_gate, d_up, d_weight)


def solution(mesh):
    return jax.shard_map(
        per_device,
        mesh=mesh,
        in_specs=(
            P(("fsdp", "tensor"), None),
            P(("fsdp", "tensor")),
            P("fsdp", "tensor"),
            P("fsdp", "tensor"),
            P("tensor", "fsdp"),
            P("tensor", None),
        ),
        out_specs=(P("fsdp", "tensor"), P("fsdp", "tensor"), P("tensor", "fsdp")),
        check_vma=False,
    )
```

profile of v0, /device:TPU:24, one launch (start us, length us, event | category | flops | bytes accessed | tf_op | source)
XLA Modules:
  0.0 173.6 jit_solution(10504902458558648319)
XLA Ops:
  3.3 3.4 %collective-permute-start = (bf16[8,8192]{1,0:T(8,128)(2,1)}, bf16[8,8192]{1,0:T(8,128)(2,1)S(1)}, u32[]{:S(2)}, u32[]{:S(2)}) collective-permute-start(bf16[8,8192]{1,0:T(8,128)(2,1)} %get-tuple-element.14), channel_id=1, source_target_pairs={{0,8},{1,9},{2,10},{3,11},{4,12},{5,13},{6,14},{7,15},{8,0},{9,1},... | collective-permute-start | bytes 393224 | tf_op jit(solution)/shard_map/ppermute | solution.py:192
  6.7 3.9 %collective-permute-done = bf16[8,8192]{1,0:T(8,128)(2,1)S(1)} collective-permute-done((bf16[8,8192]{1,0:T(8,128)(2,1)}, bf16[8,8192]{1,0:T(8,128)(2,1)S(1)}, u32[]{:S(2)}, u32[]{:S(2)}) %collective-permute-start) | collective-permute-done | bytes 131104 | tf_op jit(solution)/shard_map/ppermute | solution.py:192
  11.5 4.3 %collective-permute-start.1 = (bf16[2,8,8192]{2,1,0:T(8,128)(2,1)S(1)}, bf16[2,8,8192]{2,1,0:T(8,128)(2,1)S(1)}, u32[]{:S(2)}, u32[]{:S(2)}) collective-permute-start(bf16[2,8,8192]{2,1,0:T(8,128)(2,1)S(1)} %pad_maximum_fusion), channel_id=1, source_target_pairs={{0,1},{1,2},{2,3},{3,4},{4,5},{5,6},{6,7},{7,0},{8,9},{9,10},{10,1... | collective-permute-start | bytes 786440 | tf_op jit(solution)/shard_map/ppermute | solution.py:192
  15.8 8.6 %collective-permute-start.2 = (bf16[2,8,8192]{2,1,0:T(8,128)(2,1)S(1)}, bf16[2,8,8192]{2,1,0:T(8,128)(2,1)S(1)}, u32[]{:S(2)}, u32[]{:S(2)}) collective-permute-start(bf16[2,8,8192]{2,1,0:T(8,128)(2,1)S(1)} %pad_maximum_fusion), channel_id=1, source_target_pairs={{0,7},{1,0},{2,1},{3,2},{4,3},{5,4},{6,5},{7,6},{8,15},{9,8},{10,9... | collective-permute-start | bytes 786440 | tf_op jit(solution)/shard_map/ppermute | solution.py:192
  24.7 3.3 %collective-permute-done.1 = bf16[2,8,8192]{2,1,0:T(8,128)(2,1)S(1)} collective-permute-done((bf16[2,8,8192]{2,1,0:T(8,128)(2,1)S(1)}, bf16[2,8,8192]{2,1,0:T(8,128)(2,1)S(1)}, u32[]{:S(2)}, u32[]{:S(2)}) %collective-permute-start.1) | collective-permute-done | bytes 262176 | tf_op jit(solution)/shard_map/ppermute | solution.py:192
  29.9 5.1 %collective-permute-start.4 = (bf16[2,8,8192]{2,1,0:T(8,128)(2,1)S(1)}, bf16[2,8,8192]{2,1,0:T(8,128)(2,1)S(1)}, u32[]{:S(2)}, u32[]{:S(2)}) collective-permute-start(bf16[2,8,8192]{2,1,0:T(8,128)(2,1)S(1)} %collective-permute-done.2), channel_id=1, source_target_pairs={{0,7},{1,0},{2,1},{3,2},{4,3},{5,4},{6,5},{7,6},{8,15},{9,8},{10,9... | collective-permute-start | bytes 786440 | tf_op jit(solution)/shard_map/ppermute | solution.py:192
  39.6 5.1 %collective-permute-start.6 = (bf16[2,8,8192]{2,1,0:T(8,128)(2,1)S(1)}, bf16[2,8,8192]{2,1,0:T(8,128)(2,1)S(1)}, u32[]{:S(2)}, u32[]{:S(2)}) collective-permute-start(bf16[2,8,8192]{2,1,0:T(8,128)(2,1)S(1)} %collective-permute-done.4), channel_id=1, source_target_pairs={{0,7},{1,0},{2,1},{3,2},{4,3},{5,4},{6,5},{7,6},{8,15},{9,8},{10,9... | collective-permute-start | bytes 786440 | tf_op jit(solution)/shard_map/ppermute | solution.py:192
  49.1 7.5 %collective-permute-done.7 = bf16[2,8,8192]{2,1,0:T(8,128)(2,1)S(1)} collective-permute-done((bf16[2,8,8192]{2,1,0:T(8,128)(2,1)S(1)}, bf16[2,8,8192]{2,1,0:T(8,128)(2,1)S(1)}, u32[]{:S(2)}, u32[]{:S(2)}) %collective-permute-start.7) | collective-permute-done | bytes 262176 | tf_op jit(solution)/shard_map/ppermute | solution.py:192
  58.6 4.9 %collective-permute-start.9 = (bf16[4,128,128]{2,1,0:T(8,128)(2,1)S(1)}, bf16[4,128,128]{2,1,0:T(8,128)(2,1)S(1)}, u32[]{:S(2)}, u32[]{:S(2)}) collective-permute-start(bf16[4,128,128]{2,1,0:T(8,128)(2,1)S(1)} %copy-done.7), channel_id=1, source_target_pairs={{0,32},{16,48},{32,0},{48,16},{64,96},{80,112},{96,64},{112,80},{1... | collective-permute-start | bytes 393224 | tf_op jit(solution)/shard_map/ppermute | solution.py:189
  68.8 4.7 %collective-permute-start.10 = (bf16[2,4,128,128]{3,2,1,0:T(8,128)(2,1)S(1)}, bf16[2,4,128,128]{3,2,1,0:T(8,128)(2,1)S(1)}, u32[]{:S(2)}, u32[]{:S(2)}) collective-permute-start(bf16[2,4,128,128]{3,2,1,0:T(8,128)(2,1)S(1)} %pad_maximum_fusion.1), channel_id=1, source_target_pairs={{0,64},{16,80},{32,96},{48,112},{64,128},{80,144},{96,160},{112,17... | collective-permute-start | bytes 786440 | tf_op jit(solution)/shard_map/ppermute | solution.py:189
  79.5 5.6 %collective-permute-start.12 = (bf16[2,4,128,128]{3,2,1,0:T(8,128)(2,1)S(1)}, bf16[2,4,128,128]{3,2,1,0:T(8,128)(2,1)}, u32[]{:S(2)}, u32[]{:S(2)}) collective-permute-start(bf16[2,4,128,128]{3,2,1,0:T(8,128)(2,1)S(1)} %collective-permute-done.10), channel_id=1, source_target_pairs={{0,64},{16,80},{32,96},{48,112},{64,128},{80,144},{96,160},{112,17... | collective-permute-start | bytes 786440 | tf_op jit(solution)/shard_map/ppermute | solution.py:189
  87.1 3.1 %collective-permute-done.12 = bf16[2,4,128,128]{3,2,1,0:T(8,128)(2,1)} collective-permute-done((bf16[2,4,128,128]{3,2,1,0:T(8,128)(2,1)S(1)}, bf16[2,4,128,128]{3,2,1,0:T(8,128)(2,1)}, u32[]{:S(2)}, u32[]{:S(2)}) %collective-permute-start.12) | collective-permute-done | bytes 262176 | tf_op jit(solution)/shard_map/ppermute | solution.py:189
  90.2 5.7 %collective-permute-start.14 = (bf16[2,4,128,128]{3,2,1,0:T(8,128)(2,1)}, bf16[2,4,128,128]{3,2,1,0:T(8,128)(2,1)S(1)}, u32[]{:S(2)}, u32[]{:S(2)}) collective-permute-start(bf16[2,4,128,128]{3,2,1,0:T(8,128)(2,1)} %collective-permute-done.12), channel_id=1, source_target_pairs={{0,64},{16,80},{32,96},{48,112},{64,128},{80,144},{96,160},{112,17... | collective-permute-start | bytes 786440 | tf_op jit(solution)/shard_map/ppermute | solution.py:189
  103.1 5.1 %collective-permute-start.19 = (bf16[2,4,128,128]{3,2,1,0:T(8,128)(2,1)}, bf16[2,4,128,128]{3,2,1,0:T(8,128)(2,1)S(1)}, u32[]{:S(2)}, u32[]{:S(2)}) collective-permute-start(bf16[2,4,128,128]{3,2,1,0:T(8,128)(2,1)} %bitcast.107), channel_id=1, source_target_pairs={{0,64},{16,80},{32,96},{48,112},{64,128},{80,144},{96,160},{112,17... | collective-permute-start | bytes 786440 | tf_op jit(solution)/shard_map/ppermute | solution.py:189
  110.9 3.2 %partial.8 = bf16[2,2,4,128,128]{4,3,2,1,0:T(8,128)(2,1)} custom-call(s32[2]{0:T(128)} %pad_add_fusion.2.refs_0_, s32[128]{0:T(128)} %get-tuple-element.13.table_ref.refs_1_, s32[1]{0:T(128)} %bitcast.1.core_ref.refs_2_, bf16[768,128]{1,0:T(8,128)(2,1)} %get-tuple-element.20.refs_3_, bf16[768,128]{1,0:T(8,128)(2,1)} %copy-done.2, ...), custom_call_target="tpu_custom_call" | custom-call | flops 134217728 | bytes 524288 | tf_op jit(solution)/shard_map/partial/pallas_call | solution.py:268
  115.1 3.9 %collective-permute-start.23 = (bf16[2,4,128,128]{3,2,1,0:T(8,128)(2,1)S(1)}, bf16[2,4,128,128]{3,2,1,0:T(8,128)(2,1)S(1)}, u32[]{:S(2)}, u32[]{:S(2)}) collective-permute-start(bf16[2,4,128,128]{3,2,1,0:T(8,128)(2,1)S(1)} %slice_bitcast_fusion), channel_id=1, source_target_pairs={{0,448},{16,464},{32,480},{48,496},{64,0},{80,16},{96,32},{112,48}... | collective-permute-start | bytes 786440 | tf_op jit(solution)/shard_map/ppermute | solution.py:189
  120.1 3.1 %collective-permute-start.20 = (bf16[2,4,128,128]{3,2,1,0:T(8,128)(2,1)S(1)}, bf16[2,4,128,128]{3,2,1,0:T(8,128)(2,1)S(1)}, u32[]{:S(2)}, u32[]{:S(2)}) collective-permute-start(bf16[2,4,128,128]{3,2,1,0:T(8,128)(2,1)S(1)} %fusion.2), channel_id=1, source_target_pairs={{0,64},{16,80},{32,96},{48,112},{64,128},{80,144},{96,160},{112,17... | collective-permute-start | bytes 786440 | tf_op jit(solution)/shard_map/ppermute | solution.py:189
  124.7 3.2 %partial.7 = bf16[2,2,4,128,128]{4,3,2,1,0:T(8,128)(2,1)} custom-call(s32[2]{0:T(128)} %pad_add_fusion.1.refs_0_, s32[128]{0:T(128)} %get-tuple-element.13.table_ref.refs_1_, s32[1]{0:T(128)} %bitcast.1.core_ref.refs_2_, bf16[768,128]{1,0:T(8,128)(2,1)} %get-tuple-element.20.refs_3_, bf16[768,128]{1,0:T(8,128)(2,1)} %copy-done.2, ...), custom_call_target="tpu_custom_call" | custom-call | flops 134217728 | bytes 524288 | tf_op jit(solution)/shard_map/partial/pallas_call | solution.py:268
  131.8 4.8 %collective-permute-start.21 = (bf16[2,4,128,128]{3,2,1,0:T(8,128)(2,1)S(1)}, bf16[2,4,128,128]{3,2,1,0:T(8,128)(2,1)S(1)}, u32[]{:S(2)}, u32[]{:S(2)}) collective-permute-start(bf16[2,4,128,128]{3,2,1,0:T(8,128)(2,1)S(1)} %get-tuple-element.26), channel_id=1, source_target_pairs={{0,64},{16,80},{32,96},{48,112},{64,128},{80,144},{96,160},{112,17... | collective-permute-start | bytes 786440 | tf_op jit(solution)/shard_map/ppermute | solution.py:189
  137.3 3.2 %partial.6 = bf16[2,2,4,128,128]{4,3,2,1,0:T(8,128)(2,1)} custom-call(s32[2]{0:T(128)} %pad_add_fusion.refs_0_, s32[128]{0:T(128)} %get-tuple-element.13.table_ref.refs_1_, s32[1]{0:T(128)} %bitcast.1.core_ref.refs_2_, bf16[768,128]{1,0:T(8,128)(2,1)} %get-tuple-element.20.refs_3_, bf16[768,128]{1,0:T(8,128)(2,1)} %copy-done.2, bf16[128,8192]{1,0:T(8,128)(2,1)} %bitcast.103, ...), custom_call_target="tpu_custom_call" | custom-call | flops 134217728 | bytes 524288 | tf_op jit(solution)/shard_map/partial/pallas_call | solution.py:268
  140.6 6.1 %hidden_grad.1 = (f32[128,768]{1,0:T(8,128)}, f32[128,768]{1,0:T(8,128)}) custom-call(s32[128]{0:T(128)} %get-tuple-element.13.table_ref.refs_1_, s32[1]{0:T(128)} %bitcast.1.core_ref.refs_2_, bf16[128,8192]{1,0:T(8,128)(2,1)} %bitcast.104, bf16[128,8192]{1,0:T(8,128)(2,1)} %collective-permute-done.8.other_p.refs_6_, bf16[16,4,128,128]{3,2,1,0:T(8,128)(2,1)} %bitcast.106), custom_call_target="tpu_custom_call" | custom-call | flops 536870912 | bytes 6291456 | tf_op jit(solution)/shard_map/hidden_grad/pallas_call | solution.py:316
  148.7 5.1 %collective-permute-start.22 = (bf16[2,4,128,128]{3,2,1,0:T(8,128)(2,1)S(1)}, bf16[2,4,128,128]{3,2,1,0:T(8,128)(2,1)S(1)}, u32[]{:S(2)}, u32[]{:S(2)}) collective-permute-start(bf16[2,4,128,128]{3,2,1,0:T(8,128)(2,1)S(1)} %get-tuple-element.24), channel_id=1, source_target_pairs={{0,64},{16,80},{32,96},{48,112},{64,128},{80,144},{96,160},{112,17... | collective-permute-start | bytes 786440 | tf_op jit(solution)/shard_map/ppermute | solution.py:189
  155.8 2.9 %partial.5.part_ref = bf16[1,2,4,128,128]{4,3,2,1,0:T(8,128)(2,1)} custom-call(s32[1]{0:T(128)} %bitcast.34.refs_0_, s32[128]{0:T(128)} %get-tuple-element.13.table_ref.refs_1_, s32[1]{0:T(128)} %bitcast.1.core_ref.refs_2_, bf16[768,128]{1,0:T(8,128)(2,1)} %get-tuple-element.20.refs_3_, bf16[768,128]{1,0:T(8,128)(2,1)} %copy-done.2, ...), custom_call_target="tpu_custom_call" | custom-call | flops 67108864 | bytes 262144 | tf_op jit(solution)/shard_map/partial/pallas_call | solution.py:268
  167.1 3.9 %collective-permute-done.26.other_ref = bf16[4,128,128]{2,1,0:T(8,128)(2,1)S(1)} collective-permute-done((bf16[4,128,128]{2,1,0:T(8,128)(2,1)}, bf16[4,128,128]{2,1,0:T(8,128)(2,1)S(1)}, u32[]{:S(2)}, u32[]{:S(2)}) %collective-permute-start.26) | collective-permute-done | bytes 131104 | tf_op jit(solution)/shard_map/ppermute | solution.py:189
  (88 shorter events, 61.9 us)
Async XLA Ops:
  11.5 16.4 %collective-permute-start.1 = (bf16[2,8,8192]{2,1,0:T(8,128)(2,1)S(1)}, bf16[2,8,8192]{2,1,0:T(8,128)(2,1)S(1)}, u32[]{:S(2)}, u32[]{:S(2)}) collective-permute-start(bf16[2,8,8192]{2,1,0:T(8,128)(2,1)S(1)} %pad_maximum_fusion), channel_id=1, source_target_pairs={{0,1},{1,2},{2,3},{3,4},{4,5},{5,6},{6,7},{7,0},{8,9},{9,10},{10,1... | collective-permute-start | bytes 786440 | tf_op jit(solution)/shard_map/ppermute | solution.py:192
  15.8 14.0 %collective-permute-start.2 = (bf16[2,8,8192]{2,1,0:T(8,128)(2,1)S(1)}, bf16[2,8,8192]{2,1,0:T(8,128)(2,1)S(1)}, u32[]{:S(2)}, u32[]{:S(2)}) collective-permute-start(bf16[2,8,8192]{2,1,0:T(8,128)(2,1)S(1)} %pad_maximum_fusion), channel_id=1, source_target_pairs={{0,7},{1,0},{2,1},{3,2},{4,3},{5,4},{6,5},{7,6},{8,15},{9,8},{10,9... | collective-permute-start | bytes 786440 | tf_op jit(solution)/shard_map/ppermute | solution.py:192
  27.9 9.7 %collective-permute-start.3 = (bf16[2,8,8192]{2,1,0:T(8,128)(2,1)S(1)}, bf16[2,8,8192]{2,1,0:T(8,128)(2,1)S(1)}, u32[]{:S(2)}, u32[]{:S(2)}) collective-permute-start(bf16[2,8,8192]{2,1,0:T(8,128)(2,1)S(1)} %collective-permute-done.1), channel_id=1, source_target_pairs={{0,1},{1,2},{2,3},{3,4},{4,5},{5,6},{6,7},{7,0},{8,9},{9,10},{10,1... | collective-permute-start | bytes 786440 | tf_op jit(solution)/shard_map/ppermute | solution.py:192
  29.9 9.7 %collective-permute-start.4 = (bf16[2,8,8192]{2,1,0:T(8,128)(2,1)S(1)}, bf16[2,8,8192]{2,1,0:T(8,128)(2,1)S(1)}, u32[]{:S(2)}, u32[]{:S(2)}) collective-permute-start(bf16[2,8,8192]{2,1,0:T(8,128)(2,1)S(1)} %collective-permute-done.2), channel_id=1, source_target_pairs={{0,7},{1,0},{2,1},{3,2},{4,3},{5,4},{6,5},{7,6},{8,15},{9,8},{10,9... | collective-permute-start | bytes 786440 | tf_op jit(solution)/shard_map/ppermute | solution.py:192
  37.6 9.5 %collective-permute-start.5 = (bf16[2,8,8192]{2,1,0:T(8,128)(2,1)S(1)}, bf16[2,8,8192]{2,1,0:T(8,128)(2,1)S(1)}, u32[]{:S(2)}, u32[]{:S(2)}) collective-permute-start(bf16[2,8,8192]{2,1,0:T(8,128)(2,1)S(1)} %collective-permute-done.3), channel_id=1, source_target_pairs={{0,1},{1,2},{2,3},{3,4},{4,5},{5,6},{6,7},{7,0},{8,9},{9,10},{10,1... | collective-permute-start | bytes 786440 | tf_op jit(solution)/shard_map/ppermute | solution.py:192
  39.6 9.5 %collective-permute-start.6 = (bf16[2,8,8192]{2,1,0:T(8,128)(2,1)S(1)}, bf16[2,8,8192]{2,1,0:T(8,128)(2,1)S(1)}, u32[]{:S(2)}, u32[]{:S(2)}) collective-permute-start(bf16[2,8,8192]{2,1,0:T(8,128)(2,1)S(1)} %collective-permute-done.4), channel_id=1, source_target_pairs={{0,7},{1,0},{2,1},{3,2},{4,3},{5,4},{6,5},{7,6},{8,15},{9,8},{10,9... | collective-permute-start | bytes 786440 | tf_op jit(solution)/shard_map/ppermute | solution.py:192
  56.6 42.3 %collective-permute-start.8 = (bf16[128,8192]{1,0:T(8,128)(2,1)S(1)}, bf16[128,8192]{1,0:T(8,128)(2,1)}, u32[]{:S(2)}, u32[]{:S(2)}) collective-permute-start(bf16[128,8192]{1,0:T(8,128)(2,1)S(1)} %bitcast.99), channel_id=1, source_target_pairs={{0,16},{16,0},{32,48},{48,32},{64,80},{80,64},{96,112},{112,96},{1... | collective-permute-start | bytes 6291464 | tf_op jit(solution)/shard_map/ppermute | solution.py:189
  58.6 10.2 %collective-permute-start.9 = (bf16[4,128,128]{2,1,0:T(8,128)(2,1)S(1)}, bf16[4,128,128]{2,1,0:T(8,128)(2,1)S(1)}, u32[]{:S(2)}, u32[]{:S(2)}) collective-permute-start(bf16[4,128,128]{2,1,0:T(8,128)(2,1)S(1)} %copy-done.7), channel_id=1, source_target_pairs={{0,32},{16,48},{32,0},{48,16},{64,96},{80,112},{96,64},{112,80},{1... | collective-permute-start | bytes 393224 | tf_op jit(solution)/shard_map/ppermute | solution.py:189
  65.9 33.0 %collective-permute-start.18 = (bf16[768,128]{1,0:T(8,128)(2,1)}, bf16[768,128]{1,0:T(8,128)(2,1)S(1)}, u32[]{:S(2)}, u32[]{:S(2)}) collective-permute-start(bf16[768,128]{1,0:T(8,128)(2,1)} %get-tuple-element.20.refs_3_), channel_id=1, source_target_pairs={{0,16},{16,0},{32,48},{48,32},{64,80},{80,64},{96,112},{112,96},{1... | collective-permute-start | bytes 589832 | tf_op jit(solution)/shard_map/ppermute | solution.py:189
  68.8 10.7 %collective-permute-start.10 = (bf16[2,4,128,128]{3,2,1,0:T(8,128)(2,1)S(1)}, bf16[2,4,128,128]{3,2,1,0:T(8,128)(2,1)S(1)}, u32[]{:S(2)}, u32[]{:S(2)}) collective-permute-start(bf16[2,4,128,128]{3,2,1,0:T(8,128)(2,1)S(1)} %pad_maximum_fusion.1), channel_id=1, source_target_pairs={{0,64},{16,80},{32,96},{48,112},{64,128},{80,144},{96,160},{112,17... | collective-permute-start | bytes 786440 | tf_op jit(solution)/shard_map/ppermute | solution.py:189
  73.5 11.6 %collective-permute-start.11 = (bf16[2,4,128,128]{3,2,1,0:T(8,128)(2,1)S(1)}, bf16[2,4,128,128]{3,2,1,0:T(8,128)(2,1)S(1)}, u32[]{:S(2)}, u32[]{:S(2)}) collective-permute-start(bf16[2,4,128,128]{3,2,1,0:T(8,128)(2,1)S(1)} %pad_maximum_fusion.1), channel_id=1, source_target_pairs={{0,448},{16,464},{32,480},{48,496},{64,0},{80,16},{96,32},{112,48}... | collective-permute-start | bytes 786440 | tf_op jit(solution)/shard_map/ppermute | solution.py:189
  79.5 10.7 %collective-permute-start.12 = (bf16[2,4,128,128]{3,2,1,0:T(8,128)(2,1)S(1)}, bf16[2,4,128,128]{3,2,1,0:T(8,128)(2,1)}, u32[]{:S(2)}, u32[]{:S(2)}) collective-permute-start(bf16[2,4,128,128]{3,2,1,0:T(8,128)(2,1)S(1)} %collective-permute-done.10), channel_id=1, source_target_pairs={{0,64},{16,80},{32,96},{48,112},{64,128},{80,144},{96,160},{112,17... | collective-permute-start | bytes 786440 | tf_op jit(solution)/shard_map/ppermute | solution.py:189
  85.1 10.8 %collective-permute-start.13 = (bf16[2,4,128,128]{3,2,1,0:T(8,128)(2,1)S(1)}, bf16[2,4,128,128]{3,2,1,0:T(8,128)(2,1)S(1)}, u32[]{:S(2)}, u32[]{:S(2)}) collective-permute-start(bf16[2,4,128,128]{3,2,1,0:T(8,128)(2,1)S(1)} %collective-permute-done.11), channel_id=1, source_target_pairs={{0,448},{16,464},{32,480},{48,496},{64,0},{80,16},{96,32},{112,48}... | collective-permute-start | bytes 786440 | tf_op jit(solution)/shard_map/ppermute | solution.py:189
  90.2 18.8 %collective-permute-start.14 = (bf16[2,4,128,128]{3,2,1,0:T(8,128)(2,1)}, bf16[2,4,128,128]{3,2,1,0:T(8,128)(2,1)S(1)}, u32[]{:S(2)}, u32[]{:S(2)}) collective-permute-start(bf16[2,4,128,128]{3,2,1,0:T(8,128)(2,1)} %collective-permute-done.12), channel_id=1, source_target_pairs={{0,64},{16,80},{32,96},{48,112},{64,128},{80,144},{96,160},{112,17... | collective-permute-start | bytes 786440 | tf_op jit(solution)/shard_map/ppermute | solution.py:189
  95.9 28.0 %collective-permute-start.15 = (bf16[2,4,128,128]{3,2,1,0:T(8,128)(2,1)S(1)}, bf16[2,4,128,128]{3,2,1,0:T(8,128)(2,1)S(1)}, u32[]{:S(2)}, u32[]{:S(2)}) collective-permute-start(bf16[2,4,128,128]{3,2,1,0:T(8,128)(2,1)S(1)} %collective-permute-done.13), channel_id=1, source_target_pairs={{0,448},{16,464},{32,480},{48,496},{64,0},{80,16},{96,32},{112,48}... | collective-permute-start | bytes 786440 | tf_op jit(solution)/shard_map/ppermute | solution.py:189
  103.1 15.9 %collective-permute-start.19 = (bf16[2,4,128,128]{3,2,1,0:T(8,128)(2,1)}, bf16[2,4,128,128]{3,2,1,0:T(8,128)(2,1)S(1)}, u32[]{:S(2)}, u32[]{:S(2)}) collective-permute-start(bf16[2,4,128,128]{3,2,1,0:T(8,128)(2,1)} %bitcast.107), channel_id=1, source_target_pairs={{0,64},{16,80},{32,96},{48,112},{64,128},{80,144},{96,160},{112,17... | collective-permute-start | bytes 786440 | tf_op jit(solution)/shard_map/ppermute | solution.py:189
  109.0 27.6 %collective-permute-start.16 = (bf16[2,4,128,128]{3,2,1,0:T(8,128)(2,1)S(1)}, bf16[2,4,128,128]{3,2,1,0:T(8,128)(2,1)S(1)}, u32[]{:S(2)}, u32[]{:S(2)}) collective-permute-start(bf16[2,4,128,128]{3,2,1,0:T(8,128)(2,1)S(1)} %collective-permute-done.14), channel_id=1, source_target_pairs={{0,64},{16,80},{32,96},{48,112},{64,128},{80,144},{96,160},{112,17... | collective-permute-start | bytes 786440 | tf_op jit(solution)/shard_map/ppermute | solution.py:189
  115.1 12.8 %collective-permute-start.23 = (bf16[2,4,128,128]{3,2,1,0:T(8,128)(2,1)S(1)}, bf16[2,4,128,128]{3,2,1,0:T(8,128)(2,1)S(1)}, u32[]{:S(2)}, u32[]{:S(2)}) collective-permute-start(bf16[2,4,128,128]{3,2,1,0:T(8,128)(2,1)S(1)} %slice_bitcast_fusion), channel_id=1, source_target_pairs={{0,448},{16,464},{32,480},{48,496},{64,0},{80,16},{96,32},{112,48}... | collective-permute-start | bytes 786440 | tf_op jit(solution)/shard_map/ppermute | solution.py:189
  129.5 17.1 %collective-permute-start.24 = (bf16[2,4,128,128]{3,2,1,0:T(8,128)(2,1)S(1)}, bf16[2,4,128,128]{3,2,1,0:T(8,128)(2,1)S(1)}, u32[]{:S(2)}, u32[]{:S(2)}) collective-permute-start(bf16[2,4,128,128]{3,2,1,0:T(8,128)(2,1)S(1)} %get-tuple-element.25), channel_id=1, source_target_pairs={{0,448},{16,464},{32,480},{48,496},{64,0},{80,16},{96,32},{112,48}... | collective-permute-start | bytes 786440 | tf_op jit(solution)/shard_map/ppermute | solution.py:189
  131.8 14.9 %collective-permute-start.21 = (bf16[2,4,128,128]{3,2,1,0:T(8,128)(2,1)S(1)}, bf16[2,4,128,128]{3,2,1,0:T(8,128)(2,1)S(1)}, u32[]{:S(2)}, u32[]{:S(2)}) collective-permute-start(bf16[2,4,128,128]{3,2,1,0:T(8,128)(2,1)S(1)} %get-tuple-element.26), channel_id=1, source_target_pairs={{0,64},{16,80},{32,96},{48,112},{64,128},{80,144},{96,160},{112,17... | collective-permute-start | bytes 786440 | tf_op jit(solution)/shard_map/ppermute | solution.py:189
  146.8 11.9 %collective-permute-start.25 = (bf16[2,4,128,128]{3,2,1,0:T(8,128)(2,1)S(1)}, bf16[2,4,128,128]{3,2,1,0:T(8,128)(2,1)S(1)}, u32[]{:S(2)}, u32[]{:S(2)}) collective-permute-start(bf16[2,4,128,128]{3,2,1,0:T(8,128)(2,1)S(1)} %get-tuple-element.23), channel_id=1, source_target_pairs={{0,448},{16,464},{32,480},{48,496},{64,0},{80,16},{96,32},{112,48}... | collective-permute-start | bytes 786440 | tf_op jit(solution)/shard_map/ppermute | solution.py:189
  148.7 10.0 %collective-permute-start.22 = (bf16[2,4,128,128]{3,2,1,0:T(8,128)(2,1)S(1)}, bf16[2,4,128,128]{3,2,1,0:T(8,128)(2,1)S(1)}, u32[]{:S(2)}, u32[]{:S(2)}) collective-permute-start(bf16[2,4,128,128]{3,2,1,0:T(8,128)(2,1)S(1)} %get-tuple-element.24), channel_id=1, source_target_pairs={{0,64},{16,80},{32,96},{48,112},{64,128},{80,144},{96,160},{112,17... | collective-permute-start | bytes 786440 | tf_op jit(solution)/shard_map/ppermute | solution.py:189
  153.9 10.4 %collective-permute-start.17 = (f32[128,768]{1,0:T(8,128)}, f32[128,768]{1,0:T(8,128)S(1)}, u32[]{:S(2)}, u32[]{:S(2)}) collective-permute-start(f32[128,768]{1,0:T(8,128)} %get-tuple-element.17), channel_id=1, source_target_pairs={{0,16},{16,0},{32,48},{48,32},{64,80},{80,64},{96,112},{112,96},{1... | collective-permute-start | bytes 1179656 | tf_op jit(solution)/shard_map/ppermute | solution.py:189
  161.5 9.5 %collective-permute-start.26 = (bf16[4,128,128]{2,1,0:T(8,128)(2,1)}, bf16[4,128,128]{2,1,0:T(8,128)(2,1)S(1)}, u32[]{:S(2)}, u32[]{:S(2)}) collective-permute-start(bf16[4,128,128]{2,1,0:T(8,128)(2,1)} %get-tuple-element.22), channel_id=1, source_target_pairs={{0,32},{16,48},{32,0},{48,16},{64,96},{80,112},{96,64},{112,80},{1... | collective-permute-start | bytes 393224 | tf_op jit(solution)/shard_map/ppermute | solution.py:189
  (12 other events, 91.3 us)
where the time goes:
time: 175 us; the launch traced here: 174 us
  starting transfers between devices  95.8 us (55%)
  Pallas kernels  31.9 us (18%)
  waiting for transfers between devices  29.3 us (17%)
  local copies, waits for them, and re-layouts  9.36 us (5%)
  other arithmetic  5.27 us (3%)
  between operations  1.86 us (1%)
    ppermute x19, starting transfers between devices, over_f(): return lax.ppermute(x, 'fsdp', [(i, move(i)) for i in range(fsdp_count)])  63.6 us
    ppermute x8, starting transfers between devices, over_t(): lax.ppermute(x, 'tensor', [(i, move(i)) for i in range(tensor_count)])  32.3 us
    ppermute x8, waiting for transfers between devices, over_t(): lax.ppermute(x, 'tensor', [(i, move(i)) for i in range(tensor_count)])  19.6 us
    pallas_call x5, Pallas kernels, partials(): pl.pallas_call(body, out_shape=shape((count, 2, CAP, BLK, BLK)), grid_spe...  15.5 us
    ppermute x19, waiting for transfers between devices, over_f(): return lax.ppermute(x, 'fsdp', [(i, move(i)) for i in range(fsdp_count)])  9.73 us
    pallas_call x1, Pallas kernels, per_device(): pl.pallas_call(hidden_grad_kernel, out_shape=(shape((rows, units), jnp.fl...  6.09 us
    dynamic_update_slice x14, local copies, waits for them, and re-layouts, put(): return lax.dynamic_update_slice(full, piece[:, None], start)  4.15 us
    unnamed x18, local copies, waits for them, and re-layouts  3.55 us
  transfers between devices with their start and end apart: 27, of which 9 were waited for; matrix products, arithmetic and copies ran while one was open for 6% of the time, Pallas kernels for 16%

commit v1 on v0

--- a/solution.py
+++ b/solution.py
@@ -60,8 +60,8 @@
     hidden_ref[...] = hidden.T.astype(jnp.bfloat16)
 
 
-def partial_kernel(scale, dest_ref, table_ref, core_ref, own_h, other_h, own_p, other_p, out_ref):
-    dest = dest_ref[pl.program_id(0)]
+def partial_kernel(scale, table_ref, core_ref, own_h, other_h, own_p, other_p, out_ref):
+    dest = pl.program_id(0)
     wide = 2 * BLK
     for xh in range(2):
         s = 2 * dest + xh
@@ -124,18 +124,6 @@
             other_ref[:, pl.ds(r, BLK)] += part[rows:]
 
 
-def combine_kernel(xh_ref, part_ref, up_ref, down_ref, own_ref, send_ref):
-    def total(i):
-        return (
-            part_ref[0, i].astype(jnp.float32)
-            + up_ref[i].astype(jnp.float32)
-            + down_ref[i].astype(jnp.float32)
-        )
-
-    own_ref[...] = total(xh_ref[0])
-    send_ref[...] = total(1 - xh_ref[0]).astype(jnp.bfloat16)
-
-
 def gates_kernel(own_ref, other_ref, gate_ref, up_ref, d_gate_ref, d_up_ref):
     d_hidden = own_ref[...] + other_ref[...]
     gate = gate_ref[...].astype(jnp.float32)
@@ -147,6 +135,7 @@
 
 def place_kernel(f_ref, mask_ref, own_ref, other_ref, out_ref):
     row_blocks = mask_ref.shape[0]
+    xh = (f_ref[0] >> 1) & 1
     out_ref[...] = jnp.zeros_like(out_ref)
     count = jnp.int32(0)
     for r in range(row_blocks):
@@ -155,7 +144,9 @@
 
             @pl.when(kept == 1)
             def _(r=r, c=c, count=count):
-                total = own_ref[count] + other_ref[count].astype(jnp.float32)
+                total = own_ref[xh, count].astype(jnp.float32) + other_ref[count].astype(
+                    jnp.float32
+                )
                 out_ref[r * BLK : (r + 1) * BLK, c * BLK : (c + 1) * BLK] = total.astype(
                     jnp.bfloat16
                 )
@@ -178,7 +169,7 @@
     t = lax.axis_index("tensor")
     ring_y = fsdp_count // 4
     ring_z = tensor_count // 2
-    y, xh = f >> 2, (f >> 1) & 1
+    xh = (f >> 1) & 1
     xl, z = t >> (ring_z.bit_length() - 1), t & (ring_z - 1)
     tok, width = out_grad.shape
     rows, units = gate_pre.shape
@@ -190,9 +181,6 @@
 
     def over_t(x, move):
         return lax.ppermute(x, "tensor", [(i, move(i)) for i in range(tensor_count)])
-
-    def y_step(x, d):
-        return over_f(x, lambda i: (i + 4 * d) % fsdp_count)
 
     def z_step(x, d):
         return over_t(x, lambda i: (i // ring_z) * ring_z + (i + d) % ring_z)
@@ -251,62 +239,37 @@
         return full
 
     panel = gather(pair(masked, masked_other, xl), z_step, z, ring_z).reshape(rows, width)
-    weights = gather(pair(packed, packed_other, xh), y_step, y, ring_y)
-    weights = weights.transpose(1, 0, 2, 3, 4).reshape(shard_count, CAP, BLK, BLK)
+    columns = [[k + 4 * i for i in range(ring_y)] for k in range(4)]
+    weights = lax.all_gather(
+        pair(packed, packed_other, xh), "fsdp", axis_index_groups=columns, tiled=True
+    )
     panel_other = swap_core(panel)
     core_arr = (f & 1).reshape(1).astype(jnp.int32)
 
-    def partials(*offsets):
-        count = len(offsets)
-        dests = jnp.stack([(y + d + ring_y) & (ring_y - 1) for d in offsets]).astype(jnp.int32)
-        panel_spec = pl.BlockSpec((rows, width // ring_y), lambda i, ds, tab, cr: (0, ds[i]))
-        whole = pl.BlockSpec((units, rows), lambda i, ds, tab, cr: (0, 0))
-
-        def body(*refs):
-            partial_kernel(scale, *refs)
-
-        return pl.pallas_call(
-            body,
-            out_shape=shape((count, 2, CAP, BLK, BLK)),
-            grid_spec=pltpu.PrefetchScalarGridSpec(
-                num_scalar_prefetch=3,
-                grid=(count,),
-                in_specs=[whole, whole, panel_spec, panel_spec],
-                out_specs=pl.BlockSpec(
-                    (1, 2, CAP, BLK, BLK), lambda i, ds, tab, cr: (i, 0, 0, 0, 0)
-                ),
+    panel_spec = pl.BlockSpec((rows, width // ring_y), lambda i, tab, cr: (0, i))
+    whole = pl.BlockSpec((units, rows), lambda i, tab, cr: (0, 0))
+
+    def body(*refs):
+        partial_kernel(scale, *refs)
+
+    tiles = pl.pallas_call(
+        body,
+        out_shape=shape((ring_y, 2, CAP, BLK, BLK)),
+        grid_spec=pltpu.PrefetchScalarGridSpec(
+            num_scalar_prefetch=2,
+            grid=(ring_y,),
+            in_specs=[whole, whole, panel_spec, panel_spec],
+            out_specs=pl.BlockSpec(
+                (1, 2, CAP, BLK, BLK), lambda i, tab, cr: (i, 0, 0, 0, 0)
             ),
-            name="partial",
-            cost_estimate=cost(count * 8 * 2 * BLK * BLK * 2 * rows, count << 18),
-        )(dests, table, core_arr, hidden_t, hidden_other, panel, panel_other)
-
-    def added(part, running):
-        return (part.astype(jnp.float32) + running.astype(jnp.float32)).astype(jnp.bfloat16)
-
-    half = ring_y // 2
-    send_up = partials(half)[0]
-    down = None
-    for d in range(half, 0, -1):
-        up = y_step(send_up, 1)
-        if d == half:
-            part = partials(d - 1, 1 - d)
-            send_down = part[1]
-            send_up = added(part[0], up)
-            continue
-        down = y_step(send_down, -1)
-        if d > 1:
-            part = partials(d - 1, 1 - d)
-            send_up = added(part[0], up)
-            send_down = added(part[1], down)
-    here = partials(0)
-    own_sum, send_sum = pl.pallas_call(
-        combine_kernel,
-        out_shape=(shape((CAP, BLK, BLK), jnp.float32), shape((CAP, BLK, BLK))),
-        in_specs=[SMEM, VMEM, VMEM, VMEM],
-        out_specs=(VMEM, VMEM),
-        name="combine",
-        cost_estimate=cost(1000, 1 << 20),
-    )(xh.reshape(1).astype(jnp.int32), here, up, down)
+        ),
+        name="partial",
+        cost_estimate=cost(ring_y * 16 * BLK * BLK * 2 * rows, ring_y << 19),
+    )(table, core_arr, hidden_t, hidden_other, panel, panel_other)
+    sums = lax.psum_scatter(
+        tiles, "fsdp", scatter_dimension=0, axis_index_groups=columns, tiled=True
+    )[0]
+    send_sum = lax.dynamic_index_in_dim(sums, 1 - xh, 0, keepdims=False)
     other_sum = swap_xh(send_sum)
 
     groups = 4
@@ -345,7 +308,7 @@
         out_specs=VMEM,
         name="place",
         cost_estimate=cost(1000, 1 << 20),
-    )(f_arr, tile_mask, own_sum, other_sum)
+    )(f_arr, tile_mask, sums, other_sum)
     return (d_gate, d_up, d_weight)
 
 

time: 175 us -> 143 us (0.82)
  the two profiles are of different devices: /device:TPU:24 before, /device:TPU:2 now
where the time goes in v1:
time: 143 us; the launch traced here: 142 us
  waiting for transfers between devices  54 us (38%)
  starting transfers between devices  44.8 us (31%)
  Pallas kernels  22.4 us (16%)
  between operations  15 us (10%)
  local copies, waits for them, and re-layouts  3.34 us (2%)
  other arithmetic  2.63 us (2%)
    reduce_scatter x1, waiting for transfers between devices, per_device(): lax.psum_scatter(tiles, 'fsdp', scatter_dimension=0, axis_index_groups=co...  35.3 us
    ppermute x8, starting transfers between devices, over_t(): lax.ppermute(x, 'tensor', [(i, move(i)) for i in range(tensor_count)])  32.3 us
    ppermute x8, waiting for transfers between devices, over_t(): lax.ppermute(x, 'tensor', [(i, move(i)) for i in range(tensor_count)])  15.9 us
    ppermute x5, starting transfers between devices, over_f(): return lax.ppermute(x, 'fsdp', [(i, move(i)) for i in range(fsdp_count)])  12.4 us
    pallas_call x1, Pallas kernels, per_device(): pl.pallas_call(body, out_shape=shape((ring_y, 2, CAP, BLK, BLK)), grid_sp...  7.94 us
    pallas_call x1, Pallas kernels, per_device(): pl.pallas_call(hidden_grad_kernel, out_shape=(shape((rows, units), jnp.fl...  6.02 us
  transfers between devices with their start and end apart: 15, of which 8 were waited for; matrix products, arithmetic and copies ran while one was open for 3% of the time, Pallas kernels for 13%

profile of v1, /device:TPU:2, one launch (start us, length us, event | category | flops | bytes accessed | tf_op | source)
XLA Modules:
  0.0 142.2 jit_solution(4758650254438797848)
XLA Ops:
  7.9 2.0 %prep.1 = (bf16[8,8192]{1,0:T(8,128)(2,1)}, bf16[4,128,128]{2,1,0:T(8,128)(2,1)}) custom-call(s32[1]{0:T(128)} %bitcast.f_ref, s32[1]{0:T(128)S(6)} %copy.33.live_ref, s32[6,64]{1,0:T(8,128)} %mask_ref.5, bf16[8,8192]{1,0:T(8,128)(2,1)} %grad_ref.1, bf16[768,256]{1,0:T(8,128)(2,1)} %weight_ref.1), custom_call_target="tpu_custom_call" | custom-call | flops 1000 | bytes 1048576 | tf_op jit(solution)/shard_map/prep/pallas_call | solution.py:197
  9.8 7.8 %collective-permute-start = (bf16[8,8192]{1,0:T(8,128)(2,1)}, bf16[8,8192]{1,0:T(8,128)(2,1)S(1)}, u32[]{:S(2)}, u32[]{:S(2)}) collective-permute-start(bf16[8,8192]{1,0:T(8,128)(2,1)} %get-tuple-element.12), channel_id=1, source_target_pairs={{0,8},{1,9},{2,10},{3,11},{4,12},{5,13},{6,14},{7,15},{8,0},{9,1},... | collective-permute-start | bytes 393224 | tf_op jit(solution)/shard_map/ppermute | solution.py:183
  17.6 1.9 %collective-permute-start.9 = (bf16[4,128,128]{2,1,0:T(8,128)(2,1)}, bf16[4,128,128]{2,1,0:T(8,128)(2,1)S(1)}, u32[]{:S(2)}, u32[]{:S(2)}) collective-permute-start(bf16[4,128,128]{2,1,0:T(8,128)(2,1)} %get-tuple-element.13), channel_id=1, source_target_pairs={{0,32},{16,48},{32,0},{48,16},{64,96},{80,112},{96,64},{112,80},{1... | collective-permute-start | bytes 393224 | tf_op jit(solution)/shard_map/ppermute | solution.py:180
  19.6 2.0 %collective-permute-done = bf16[8,8192]{1,0:T(8,128)(2,1)S(1)} collective-permute-done((bf16[8,8192]{1,0:T(8,128)(2,1)}, bf16[8,8192]{1,0:T(8,128)(2,1)S(1)}, u32[]{:S(2)}, u32[]{:S(2)}) %collective-permute-start) | collective-permute-done | bytes 131104 | tf_op jit(solution)/shard_map/ppermute | solution.py:183
  22.5 1.9 %collective-permute-start.1 = (bf16[2,8,8192]{2,1,0:T(8,128)(2,1)S(1)}, bf16[2,8,8192]{2,1,0:T(8,128)(2,1)S(1)}, u32[]{:S(2)}, u32[]{:S(2)}) collective-permute-start(bf16[2,8,8192]{2,1,0:T(8,128)(2,1)S(1)} %pad_maximum_fusion), channel_id=1, source_target_pairs={{0,1},{1,2},{2,3},{3,4},{4,5},{5,6},{6,7},{7,0},{8,9},{9,10},{10,1... | collective-permute-start | bytes 786440 | tf_op jit(solution)/shard_map/ppermute | solution.py:183
  24.4 6.6 %collective-permute-start.2 = (bf16[2,8,8192]{2,1,0:T(8,128)(2,1)S(1)}, bf16[2,8,8192]{2,1,0:T(8,128)(2,1)S(1)}, u32[]{:S(2)}, u32[]{:S(2)}) collective-permute-start(bf16[2,8,8192]{2,1,0:T(8,128)(2,1)S(1)} %pad_maximum_fusion), channel_id=1, source_target_pairs={{0,7},{1,0},{2,1},{3,2},{4,3},{5,4},{6,5},{7,6},{8,15},{9,8},{10,9... | collective-permute-start | bytes 786440 | tf_op jit(solution)/shard_map/ppermute | solution.py:183
  34.5 1.9 %collective-permute-start.3 = (bf16[2,8,8192]{2,1,0:T(8,128)(2,1)S(1)}, bf16[2,8,8192]{2,1,0:T(8,128)(2,1)S(1)}, u32[]{:S(2)}, u32[]{:S(2)}) collective-permute-start(bf16[2,8,8192]{2,1,0:T(8,128)(2,1)S(1)} %collective-permute-done.1), channel_id=1, source_target_pairs={{0,1},{1,2},{2,3},{3,4},{4,5},{5,6},{6,7},{7,0},{8,9},{9,10},{10,1... | collective-permute-start | bytes 786440 | tf_op jit(solution)/shard_map/ppermute | solution.py:183
  36.4 5.1 %collective-permute-start.4 = (bf16[2,8,8192]{2,1,0:T(8,128)(2,1)S(1)}, bf16[2,8,8192]{2,1,0:T(8,128)(2,1)S(1)}, u32[]{:S(2)}, u32[]{:S(2)}) collective-permute-start(bf16[2,8,8192]{2,1,0:T(8,128)(2,1)S(1)} %collective-permute-done.2), channel_id=1, source_target_pairs={{0,7},{1,0},{2,1},{3,2},{4,3},{5,4},{6,5},{7,6},{8,15},{9,8},{10,9... | collective-permute-start | bytes 786440 | tf_op jit(solution)/shard_map/ppermute | solution.py:183
  41.7 2.6 %collective-permute-done.3 = bf16[2,8,8192]{2,1,0:T(8,128)(2,1)S(1)} collective-permute-done((bf16[2,8,8192]{2,1,0:T(8,128)(2,1)S(1)}, bf16[2,8,8192]{2,1,0:T(8,128)(2,1)S(1)}, u32[]{:S(2)}, u32[]{:S(2)}) %collective-permute-start.3) | collective-permute-done | bytes 262176 | tf_op jit(solution)/shard_map/ppermute | solution.py:183
  44.2 1.9 %collective-permute-start.5 = (bf16[2,8,8192]{2,1,0:T(8,128)(2,1)S(1)}, bf16[2,8,8192]{2,1,0:T(8,128)(2,1)S(1)}, u32[]{:S(2)}, u32[]{:S(2)}) collective-permute-start(bf16[2,8,8192]{2,1,0:T(8,128)(2,1)S(1)} %collective-permute-done.3), channel_id=1, source_target_pairs={{0,1},{1,2},{2,3},{3,4},{4,5},{5,6},{6,7},{7,0},{8,9},{9,10},{10,1... | collective-permute-start | bytes 786440 | tf_op jit(solution)/shard_map/ppermute | solution.py:183
  46.2 5.1 %collective-permute-start.6 = (bf16[2,8,8192]{2,1,0:T(8,128)(2,1)S(1)}, bf16[2,8,8192]{2,1,0:T(8,128)(2,1)S(1)}, u32[]{:S(2)}, u32[]{:S(2)}) collective-permute-start(bf16[2,8,8192]{2,1,0:T(8,128)(2,1)S(1)} %collective-permute-done.4), channel_id=1, source_target_pairs={{0,7},{1,0},{2,1},{3,2},{4,3},{5,4},{6,5},{7,6},{8,15},{9,8},{10,9... | collective-permute-start | bytes 786440 | tf_op jit(solution)/shard_map/ppermute | solution.py:183
  51.4 2.3 %collective-permute-done.5 = bf16[2,8,8192]{2,1,0:T(8,128)(2,1)S(1)} collective-permute-done((bf16[2,8,8192]{2,1,0:T(8,128)(2,1)S(1)}, bf16[2,8,8192]{2,1,0:T(8,128)(2,1)S(1)}, u32[]{:S(2)}, u32[]{:S(2)}) %collective-permute-start.5) | collective-permute-done | bytes 262176 | tf_op jit(solution)/shard_map/ppermute | solution.py:183
  53.7 1.9 %collective-permute-start.7 = (bf16[2,8,8192]{2,1,0:T(8,128)(2,1)S(1)}, bf16[2,8,8192]{2,1,0:T(8,128)(2,1)S(1)}, u32[]{:S(2)}, u32[]{:S(2)}) collective-permute-start(bf16[2,8,8192]{2,1,0:T(8,128)(2,1)S(1)} %collective-permute-done.5), channel_id=1, source_target_pairs={{0,1},{1,2},{2,3},{3,4},{4,5},{5,6},{6,7},{7,0},{8,9},{9,10},{10,1... | collective-permute-start | bytes 786440 | tf_op jit(solution)/shard_map/ppermute | solution.py:183
  55.7 7.5 %collective-permute-done.7 = bf16[2,8,8192]{2,1,0:T(8,128)(2,1)S(1)} collective-permute-done((bf16[2,8,8192]{2,1,0:T(8,128)(2,1)S(1)}, bf16[2,8,8192]{2,1,0:T(8,128)(2,1)S(1)}, u32[]{:S(2)}, u32[]{:S(2)}) %collective-permute-start.7) | collective-permute-done | bytes 262176 | tf_op jit(solution)/shard_map/ppermute | solution.py:183
  63.2 1.9 %collective-permute-start.8 = (bf16[128,8192]{1,0:T(8,128)(2,1)S(1)}, bf16[128,8192]{1,0:T(8,128)(2,1)}, u32[]{:S(2)}, u32[]{:S(2)}) collective-permute-start(bf16[128,8192]{1,0:T(8,128)(2,1)S(1)} %bitcast.46), channel_id=1, source_target_pairs={{0,16},{16,0},{32,48},{48,32},{64,80},{80,64},{96,112},{112,96},{1... | collective-permute-start | bytes 6291464 | tf_op jit(solution)/shard_map/ppermute | solution.py:180
  65.1 2.4 %hidden.1 = (s32[128]{0:T(128)}, bf16[768,128]{1,0:T(8,128)(2,1)}) custom-call(s32[1]{0:T(128)} %bitcast.f_ref, s32[6,64]{1,0:T(8,128)} %mask_ref.5, bf16[128,768]{1,0:T(8,128)(2,1)} %gate_ref.3, bf16[128,768]{1,0:T(8,128)(2,1)} %up_ref.3), custom_call_target="tpu_custom_call" | custom-call | flops 1000 | bytes 1048576 | tf_op jit(solution)/shard_map/hidden/pallas_call | solution.py:209
  67.6 2.4 %collective-permute-start.11 = (bf16[768,128]{1,0:T(8,128)(2,1)}, bf16[768,128]{1,0:T(8,128)(2,1)S(1)}, u32[]{:S(2)}, u32[]{:S(2)}) collective-permute-start(bf16[768,128]{1,0:T(8,128)(2,1)} %get-tuple-element.18.refs_2_), channel_id=1, source_target_pairs={{0,16},{16,0},{32,48},{48,32},{64,80},{80,64},{96,112},{112,96},{1... | collective-permute-start | bytes 589832 | tf_op jit(solution)/shard_map/ppermute | solution.py:180
  71.9 7.9 %partial.1 = bf16[8,2,4,128,128]{4,3,2,1,0:T(8,128)(2,1)} custom-call(s32[128]{0:T(128)} %get-tuple-element.11.table_ref.refs_0_, s32[1]{0:T(128)} %bitcast.1.core_ref.refs_1_, bf16[768,128]{1,0:T(8,128)(2,1)} %get-tuple-element.18.refs_2_, bf16[768,128]{1,0:T(8,128)(2,1)} %copy-done.2, bf16[128,8192]{1,0:T(8,128)(2,1)} %bitcast.47, ...), custom_call_target="tpu_custom_call" | custom-call | flops 536870912 | bytes 4194304 | tf_op jit(solution)/shard_map/partial/pallas_call | solution.py:255
  79.9 6.0 %hidden_grad.1 = (f32[128,768]{1,0:T(8,128)}, f32[128,768]{1,0:T(8,128)}) custom-call(s32[128]{0:T(128)} %get-tuple-element.11.table_ref.refs_0_, s32[1]{0:T(128)} %bitcast.1.core_ref.refs_1_, bf16[128,8192]{1,0:T(8,128)(2,1)} %bitcast.48, bf16[128,8192]{1,0:T(8,128)(2,1)} %collective-permute-done.8.other_p.refs_5_, ...), custom_call_target="tpu_custom_call" | custom-call | flops 536870912 | bytes 6291456 | tf_op jit(solution)/shard_map/hidden_grad/pallas_call | solution.py:279
  85.9 2.3 %collective-permute-start.10 = (f32[128,768]{1,0:T(8,128)}, f32[128,768]{1,0:T(8,128)S(1)}, u32[]{:S(2)}, u32[]{:S(2)}) collective-permute-start(f32[128,768]{1,0:T(8,128)} %get-tuple-element.15), channel_id=1, source_target_pairs={{0,16},{16,0},{32,48},{48,32},{64,80},{80,64},{96,112},{112,96},{1... | collective-permute-start | bytes 1179656 | tf_op jit(solution)/shard_map/ppermute | solution.py:180
  88.2 35.3 %reduce-scatter.2.cloned.1.call-done = bf16[1,2,4,128,128]{4,3,2,1,0:T(8,128)(2,1)} async-done(((bf16[8,2,4,128,128]{4,3,2,1,0:T(8,128)(2,1)}), bf16[1,2,4,128,128]{4,3,2,1,0:T(8,128)(2,1)}) %reduce-scatter.2.cloned.1.call-update) | async-done | bytes 262160 | tf_op jit(solution)/shard_map/reduce_scatter | solution.py:269
  124.4 3.9 %collective-permute-start.12 = (bf16[4,128,128]{2,1,0:T(8,128)(2,1)S(1)}, bf16[4,128,128]{2,1,0:T(8,128)(2,1)S(1)}, u32[]{:S(2)}, u32[]{:S(2)}) collective-permute-start(bf16[4,128,128]{2,1,0:T(8,128)(2,1)S(1)} %dynamic-slice_bitcast_fusion), channel_id=1, source_target_pairs={{0,32},{16,48},{32,0},{48,16},{64,96},{80,112},{96,64},{112,80},{1... | collective-permute-start | bytes 393224 | tf_op jit(solution)/shard_map/ppermute | solution.py:180
  129.1 2.1 %gates.1 = (bf16[128,768]{1,0:T(8,128)(2,1)}, bf16[128,768]{1,0:T(8,128)(2,1)}) custom-call(f32[128,768]{1,0:T(8,128)} %get-tuple-element.14.own_ref, f32[128,768]{1,0:T(8,128)} %copy-done.1, bf16[128,768]{1,0:T(8,128)(2,1)} %gate_ref.3, bf16[128,768]{1,0:T(8,128)(2,1)} %up_ref.3), custom_call_target="tpu_custom_call" | custom-call | flops 1000 | bytes 1572864 | tf_op jit(solution)/shard_map/gates/pallas_call | solution.py:296
  133.4 1.9 %place.1 = bf16[768,256]{1,0:T(8,128)(2,1)} custom-call(s32[1]{0:T(128)} %bitcast.f_ref, s32[6,64]{1,0:T(8,128)} %mask_ref.5, bf16[2,4,128,128]{3,2,1,0:T(8,128)(2,1)} %bitcast.49, bf16[4,128,128]{2,1,0:T(8,128)(2,1)} %copy-done.3), custom_call_target="tpu_custom_call" | custom-call | flops 1000 | bytes 1048576 | tf_op jit(solution)/shard_map/place/pallas_call | solution.py:304
  (36 shorter events, 10.5 us)
Async XLA Ops:
  7.2 72.7 %all-gather.2.cloned.1.call-start = ((), (), s32[]{:S(2)}) async-start(), calls=%async_computation.1 | async-start | bytes 2359296 | tf_op jit(solution)/shard_map/all_gather | solution.py:243
  9.8 11.7 %collective-permute-start = (bf16[8,8192]{1,0:T(8,128)(2,1)}, bf16[8,8192]{1,0:T(8,128)(2,1)S(1)}, u32[]{:S(2)}, u32[]{:S(2)}) collective-permute-start(bf16[8,8192]{1,0:T(8,128)(2,1)} %get-tuple-element.12), channel_id=1, source_target_pairs={{0,8},{1,9},{2,10},{3,11},{4,12},{5,13},{6,14},{7,15},{8,0},{9,1},... | collective-permute-start | bytes 393224 | tf_op jit(solution)/shard_map/ppermute | solution.py:183
  17.6 13.4 %collective-permute-start.9 = (bf16[4,128,128]{2,1,0:T(8,128)(2,1)}, bf16[4,128,128]{2,1,0:T(8,128)(2,1)S(1)}, u32[]{:S(2)}, u32[]{:S(2)}) collective-permute-start(bf16[4,128,128]{2,1,0:T(8,128)(2,1)} %get-tuple-element.13), channel_id=1, source_target_pairs={{0,32},{16,48},{32,0},{48,16},{64,96},{80,112},{96,64},{112,80},{1... | collective-permute-start | bytes 393224 | tf_op jit(solution)/shard_map/ppermute | solution.py:180
  22.5 12.0 %collective-permute-start.1 = (bf16[2,8,8192]{2,1,0:T(8,128)(2,1)S(1)}, bf16[2,8,8192]{2,1,0:T(8,128)(2,1)S(1)}, u32[]{:S(2)}, u32[]{:S(2)}) collective-permute-start(bf16[2,8,8192]{2,1,0:T(8,128)(2,1)S(1)} %pad_maximum_fusion), channel_id=1, source_target_pairs={{0,1},{1,2},{2,3},{3,4},{4,5},{5,6},{6,7},{7,0},{8,9},{9,10},{10,1... | collective-permute-start | bytes 786440 | tf_op jit(solution)/shard_map/ppermute | solution.py:183
  24.4 12.0 %collective-permute-start.2 = (bf16[2,8,8192]{2,1,0:T(8,128)(2,1)S(1)}, bf16[2,8,8192]{2,1,0:T(8,128)(2,1)S(1)}, u32[]{:S(2)}, u32[]{:S(2)}) collective-permute-start(bf16[2,8,8192]{2,1,0:T(8,128)(2,1)S(1)} %pad_maximum_fusion), channel_id=1, source_target_pairs={{0,7},{1,0},{2,1},{3,2},{4,3},{5,4},{6,5},{7,6},{8,15},{9,8},{10,9... | collective-permute-start | bytes 786440 | tf_op jit(solution)/shard_map/ppermute | solution.py:183
  32.7 90.8 %reduce-scatter.2.cloned.1.call-start = ((), (), s32[]{:S(2)}) async-start(), calls=%async_computation.2 | async-start | bytes 2359296 | tf_op jit(solution)/shard_map/reduce_scatter | solution.py:269
  34.5 9.7 %collective-permute-start.3 = (bf16[2,8,8192]{2,1,0:T(8,128)(2,1)S(1)}, bf16[2,8,8192]{2,1,0:T(8,128)(2,1)S(1)}, u32[]{:S(2)}, u32[]{:S(2)}) collective-permute-start(bf16[2,8,8192]{2,1,0:T(8,128)(2,1)S(1)} %collective-permute-done.1), channel_id=1, source_target_pairs={{0,1},{1,2},{2,3},{3,4},{4,5},{5,6},{6,7},{7,0},{8,9},{9,10},{10,1... | collective-permute-start | bytes 786440 | tf_op jit(solution)/shard_map/ppermute | solution.py:183
  36.4 9.7 %collective-permute-start.4 = (bf16[2,8,8192]{2,1,0:T(8,128)(2,1)S(1)}, bf16[2,8,8192]{2,1,0:T(8,128)(2,1)S(1)}, u32[]{:S(2)}, u32[]{:S(2)}) collective-permute-start(bf16[2,8,8192]{2,1,0:T(8,128)(2,1)S(1)} %collective-permute-done.2), channel_id=1, source_target_pairs={{0,7},{1,0},{2,1},{3,2},{4,3},{5,4},{6,5},{7,6},{8,15},{9,8},{10,9... | collective-permute-start | bytes 786440 | tf_op jit(solution)/shard_map/ppermute | solution.py:183
  44.2 9.5 %collective-permute-start.5 = (bf16[2,8,8192]{2,1,0:T(8,128)(2,1)S(1)}, bf16[2,8,8192]{2,1,0:T(8,128)(2,1)S(1)}, u32[]{:S(2)}, u32[]{:S(2)}) collective-permute-start(bf16[2,8,8192]{2,1,0:T(8,128)(2,1)S(1)} %collective-permute-done.3), channel_id=1, source_target_pairs={{0,1},{1,2},{2,3},{3,4},{4,5},{5,6},{6,7},{7,0},{8,9},{9,10},{10,1... | collective-permute-start | bytes 786440 | tf_op jit(solution)/shard_map/ppermute | solution.py:183
  46.2 9.5 %collective-permute-start.6 = (bf16[2,8,8192]{2,1,0:T(8,128)(2,1)S(1)}, bf16[2,8,8192]{2,1,0:T(8,128)(2,1)S(1)}, u32[]{:S(2)}, u32[]{:S(2)}) collective-permute-start(bf16[2,8,8192]{2,1,0:T(8,128)(2,1)S(1)} %collective-permute-done.4), channel_id=1, source_target_pairs={{0,7},{1,0},{2,1},{3,2},{4,3},{5,4},{6,5},{7,6},{8,15},{9,8},{10,9... | collective-permute-start | bytes 786440 | tf_op jit(solution)/shard_map/ppermute | solution.py:183
  53.7 9.5 %collective-permute-start.7 = (bf16[2,8,8192]{2,1,0:T(8,128)(2,1)S(1)}, bf16[2,8,8192]{2,1,0:T(8,128)(2,1)S(1)}, u32[]{:S(2)}, u32[]{:S(2)}) collective-permute-start(bf16[2,8,8192]{2,1,0:T(8,128)(2,1)S(1)} %collective-permute-done.5), channel_id=1, source_target_pairs={{0,1},{1,2},{2,3},{3,4},{4,5},{5,6},{6,7},{7,0},{8,9},{9,10},{10,1... | collective-permute-start | bytes 786440 | tf_op jit(solution)/shard_map/ppermute | solution.py:183
  63.2 8.0 %copy-start = (bf16[2,8,8,8192]{3,2,1,0:T(8,128)(2,1)}, bf16[2,8,8,8192]{3,2,1,0:T(8,128)(2,1)S(1)}, u32[]{:S(2)}) copy-start(bf16[2,8,8,8192]{3,2,1,0:T(8,128)(2,1)S(1)} %bitcast_dynamic-update-slice_fusion) | copy-start | bytes 6291460
  63.2 8.0 %collective-permute-start.8 = (bf16[128,8192]{1,0:T(8,128)(2,1)S(1)}, bf16[128,8192]{1,0:T(8,128)(2,1)}, u32[]{:S(2)}, u32[]{:S(2)}) collective-permute-start(bf16[128,8192]{1,0:T(8,128)(2,1)S(1)} %bitcast.46), channel_id=1, source_target_pairs={{0,16},{16,0},{32,48},{48,32},{64,80},{80,64},{96,112},{112,96},{1... | collective-permute-start | bytes 6291464 | tf_op jit(solution)/shard_map/ppermute | solution.py:180
  67.6 3.7 %collective-permute-start.11 = (bf16[768,128]{1,0:T(8,128)(2,1)}, bf16[768,128]{1,0:T(8,128)(2,1)S(1)}, u32[]{:S(2)}, u32[]{:S(2)}) collective-permute-start(bf16[768,128]{1,0:T(8,128)(2,1)} %get-tuple-element.18.refs_2_), channel_id=1, source_target_pairs={{0,16},{16,0},{32,48},{48,32},{64,80},{80,64},{96,112},{112,96},{1... | collective-permute-start | bytes 589832 | tf_op jit(solution)/shard_map/ppermute | solution.py:180
  71.2 0.7 copy-start.2
  85.9 42.4 %collective-permute-start.10 = (f32[128,768]{1,0:T(8,128)}, f32[128,768]{1,0:T(8,128)S(1)}, u32[]{:S(2)}, u32[]{:S(2)}) collective-permute-start(f32[128,768]{1,0:T(8,128)} %get-tuple-element.15), channel_id=1, source_target_pairs={{0,16},{16,0},{32,48},{48,32},{64,80},{80,64},{96,112},{112,96},{1... | collective-permute-start | bytes 1179656 | tf_op jit(solution)/shard_map/ppermute | solution.py:180
  124.4 8.4 %collective-permute-start.12 = (bf16[4,128,128]{2,1,0:T(8,128)(2,1)S(1)}, bf16[4,128,128]{2,1,0:T(8,128)(2,1)S(1)}, u32[]{:S(2)}, u32[]{:S(2)}) collective-permute-start(bf16[4,128,128]{2,1,0:T(8,128)(2,1)S(1)} %dynamic-slice_bitcast_fusion), channel_id=1, source_target_pairs={{0,32},{16,48},{32,0},{48,16},{64,96},{80,112},{96,64},{112,80},{1... | collective-permute-start | bytes 393224 | tf_op jit(solution)/shard_map/ppermute | solution.py:180
  128.3 0.7 copy-start.1
  132.8 0.7 copy-start.3
Sparse Core Ops, SparseCore 0:
  32.8 42.2 all-gather.1
  80.0 43.4 reduce-scatter.1

commit v2 on v1

--- a/solution.py
+++ b/solution.py
@@ -1,3 +1,4 @@
+import functools
 import math
 
 import jax
@@ -11,10 +12,21 @@
 BLK = 128
 CAP = 4
 TAB = 8
+TOK = 8
 
 
 VMEM = pl.BlockSpec(memory_space=pltpu.VMEM)
 SMEM = pl.BlockSpec(memory_space=pltpu.SMEM)
+
+
+def by_ring(x):
+    rows, width = x.shape
+    return jnp.swapaxes(x.reshape(2, rows // (2 * TOK), TOK, width), 0, 1).reshape(rows, width)
+
+
+def by_token(x):
+    rows, width = x.shape
+    return jnp.swapaxes(x.reshape(rows // (2 * TOK), 2, TOK, width), 0, 1).reshape(rows, width)
 
 
 def prep_kernel(f_ref, live_ref, mask_ref, grad_ref, weight_ref, masked_ref, packed_ref):
@@ -57,26 +69,26 @@
     gate = gate_ref[...].astype(jnp.float32)
     up = up_ref[...].astype(jnp.float32)
     hidden = gate * jax.nn.sigmoid(gate) * up
-    hidden_ref[...] = hidden.T.astype(jnp.bfloat16)
-
-
-def partial_kernel(scale, table_ref, core_ref, own_h, other_h, own_p, other_p, out_ref):
+    hidden_ref[...] = by_ring(hidden).T.astype(jnp.bfloat16)
+
+
+def partial_kernel(table_ref, core_ref, hidden_ref, panel_ref, out_ref):
     dest = pl.program_id(0)
     wide = 2 * BLK
     for xh in range(2):
         s = 2 * dest + xh
         at = pl.multiple_of((2 * xh + core_ref[0]) * wide, wide)
-        right = jnp.concatenate([own_p[:, pl.ds(at, wide)], other_p[:, pl.ds(at, wide)]], axis=0)
+        right = panel_ref[:, pl.ds(at, wide)]
         places = [table_ref[s * TAB + k] for k in range(CAP)]
         rows = [pl.multiple_of((b >> 1) * BLK, BLK) for b in places]
         left = jnp.concatenate(
             [
-                jnp.concatenate([own_h[pl.ds(r, BLK), :], other_h[pl.ds(r, BLK), :]], axis=1)
+                jnp.concatenate([hidden_ref[c, pl.ds(r, BLK), :] for c in range(2)], axis=1)
                 for r in rows
             ],
             axis=0,
         )
-        term = jnp.dot(left, right, preferred_element_type=jnp.float32) * scale
+        term = jnp.dot(left, right, preferred_element_type=jnp.float32)
         for k, b in enumerate(places):
             tile = term[k * BLK : (k + 1) * BLK]
             kept = jnp.where((b & 1) == 0, tile[:, :BLK], tile[:, BLK:])
@@ -84,22 +96,21 @@
 
 
 def hidden_grad_kernel(
-    table_ref, core_ref, own_p, other_p, weight_ref, own_ref, other_ref
+    table_ref, core_ref, panel_ref, weight_ref, own_ref, other_ref, sum_ref
 ):
     group = pl.program_id(0)
     shards = weight_ref.shape[0]
     wide = 2 * BLK
-    rows = own_p.shape[0]
+    rows = own_ref.shape[0]
 
     @pl.when(group == 0)
     def _():
-        own_ref[...] = jnp.zeros_like(own_ref)
-        other_ref[...] = jnp.zeros_like(other_ref)
+        sum_ref[...] = jnp.zeros_like(sum_ref)
 
     for i in range(shards):
         s = group * shards + i
         at = pl.multiple_of((2 * i + core_ref[0]) * wide, wide)
-        left = jnp.concatenate([own_p[:, pl.ds(at, wide)], other_p[:, pl.ds(at, wide)]], axis=0)
+        left = panel_ref[:, pl.ds(at, wide)]
         places = [table_ref[s * TAB + k] for k in range(CAP)]
         halves = []
         for k, b in enumerate(places):
@@ -120,12 +131,17 @@
         for k, b in enumerate(places):
             r = pl.multiple_of((b >> 1) * BLK, BLK)
             part = term[:, k * BLK : (k + 1) * BLK]
-            own_ref[:, pl.ds(r, BLK)] += part[:rows]
-            other_ref[:, pl.ds(r, BLK)] += part[rows:]
+            sum_ref[0, :, pl.ds(r, BLK)] += part[:rows]
+            sum_ref[1, :, pl.ds(r, BLK)] += part[rows:]
+
+    @pl.when(group == pl.num_programs(0) - 1)
+    def _():
+        own_ref[...] = sum_ref[core_ref[0]]
+        other_ref[...] = sum_ref[1 - core_ref[0]]
 
 
 def gates_kernel(own_ref, other_ref, gate_ref, up_ref, d_gate_ref, d_up_ref):
-    d_hidden = own_ref[...] + other_ref[...]
+    d_hidden = by_token(own_ref[...] + other_ref[...])
     gate = gate_ref[...].astype(jnp.float32)
     up = up_ref[...].astype(jnp.float32)
     s = jax.nn.sigmoid(gate)
@@ -133,7 +149,7 @@
     d_gate_ref[...] = (d_hidden * up * s * (1.0 + gate * (1.0 - s))).astype(jnp.bfloat16)
 
 
-def place_kernel(f_ref, mask_ref, own_ref, other_ref, out_ref):
+def place_kernel(scale, f_ref, mask_ref, own_ref, other_ref, out_ref):
     row_blocks = mask_ref.shape[0]
     xh = (f_ref[0] >> 1) & 1
     out_ref[...] = jnp.zeros_like(out_ref)
@@ -147,9 +163,9 @@
                 total = own_ref[xh, count].astype(jnp.float32) + other_ref[count].astype(
                     jnp.float32
                 )
-                out_ref[r * BLK : (r + 1) * BLK, c * BLK : (c + 1) * BLK] = total.astype(
-                    jnp.bfloat16
-                )
+                out_ref[r * BLK : (r + 1) * BLK, c * BLK : (c + 1) * BLK] = (
+                    total * scale
+                ).astype(jnp.bfloat16)
 
             count = count + kept
 
@@ -169,8 +185,8 @@
     t = lax.axis_index("tensor")
     ring_y = fsdp_count // 4
     ring_z = tensor_count // 2
-    xh = (f >> 1) & 1
-    xl, z = t >> (ring_z.bit_length() - 1), t & (ring_z - 1)
+    y, xh = f >> 2, (f >> 1) & 1
+    xl = t >> (ring_z.bit_length() - 1)
     tok, width = out_grad.shape
     rows, units = gate_pre.shape
     scale = 1.0 / math.sqrt(rows * fsdp_count)
@@ -182,8 +198,8 @@
     def over_t(x, move):
         return lax.ppermute(x, "tensor", [(i, move(i)) for i in range(tensor_count)])
 
-    def z_step(x, d):
-        return over_t(x, lambda i: (i // ring_z) * ring_z + (i + d) % ring_z)
+    def y_step(x, d):
+        return over_f(x, lambda i: (i + 4 * d) % fsdp_count)
 
     def swap_core(x):
         return over_f(x, lambda i: i ^ 1)
@@ -221,51 +237,52 @@
         second = jnp.where(index == 0, other, own)
         return jnp.stack([first, second])
 
-    def gather(block, step, index, count):
-        full = jnp.zeros((2, count) + block.shape[1:], block.dtype)
-
-        def put(full, piece, at):
-            start = (0, at & (count - 1)) + (0,) * (block.ndim - 1)
-            return lax.dynamic_update_slice(full, piece[:, None], start)
-
-        full = put(full, block, index)
-        up = down = block
-        for d in range(1, count // 2 + 1):
-            up = step(up, 1)
-            full = put(full, up, index - d + count)
-            if d < count // 2:
-                down = step(down, -1)
-                full = put(full, down, index + d)
-        return full
-
-    panel = gather(pair(masked, masked_other, xl), z_step, z, ring_z).reshape(rows, width)
     columns = [[k + 4 * i for i in range(ring_y)] for k in range(4)]
-    weights = lax.all_gather(
-        pair(packed, packed_other, xh), "fsdp", axis_index_groups=columns, tiled=True
-    )
-    panel_other = swap_core(panel)
+    chips = [
+        [(2 * i + c) * tensor_count + half * ring_z + j for c in range(2) for j in range(ring_z)]
+        for i in range(fsdp_count // 2)
+        for half in range(2)
+    ]
+    panel = lax.all_gather(
+        pair(masked, masked_other, xl),
+        ("fsdp", "tensor"),
+        axis_index_groups=chips,
+        tiled=True,
+    ).reshape(2 * rows, width)
+    hidden_pair = pair(hidden_t, hidden_other, f & 1)
+
+    weights = jnp.zeros((ring_y, 2, CAP, BLK, BLK), jnp.bfloat16)
+
+    def put(full, piece, at):
+        return lax.dynamic_update_slice(full, piece[None], (at & (ring_y - 1), 0, 0, 0, 0))
+
+    up = down = pair(packed, packed_other, xh)
+    weights = put(weights, up, y)
+    for d in range(1, ring_y // 2 + 1):
+        up = y_step(up, 1)
+        weights = put(weights, up, y - d + ring_y)
+        if d < ring_y // 2:
+            down = y_step(down, -1)
+            weights = put(weights, down, y + d)
+    weights = weights.reshape(shard_count, CAP, BLK, BLK)
     core_arr = (f & 1).reshape(1).astype(jnp.int32)
 
-    panel_spec = pl.BlockSpec((rows, width // ring_y), lambda i, tab, cr: (0, i))
-    whole = pl.BlockSpec((units, rows), lambda i, tab, cr: (0, 0))
-
-    def body(*refs):
-        partial_kernel(scale, *refs)
-
+    panel_spec = pl.BlockSpec((2 * rows, width // ring_y), lambda i, tab, cr: (0, i))
+    whole = pl.BlockSpec((2, units, rows), lambda i, tab, cr: (0, 0, 0))
     tiles = pl.pallas_call(
-        body,
+        partial_kernel,
         out_shape=shape((ring_y, 2, CAP, BLK, BLK)),
         grid_spec=pltpu.PrefetchScalarGridSpec(
             num_scalar_prefetch=2,
             grid=(ring_y,),
-            in_specs=[whole, whole, panel_spec, panel_spec],
+            in_specs=[whole, panel_spec],
             out_specs=pl.BlockSpec(
                 (1, 2, CAP, BLK, BLK), lambda i, tab, cr: (i, 0, 0, 0, 0)
             ),
         ),
         name="partial",
         cost_estimate=cost(ring_y * 16 * BLK * BLK * 2 * rows, ring_y << 19),
-    )(table, core_arr, hidden_t, hidden_other, panel, panel_other)
+    )(table, core_arr, hidden_pair, panel)
     sums = lax.psum_scatter(
         tiles, "fsdp", scatter_dimension=0, axis_index_groups=columns, tiled=True
     )[0]
@@ -275,7 +292,7 @@
     groups = 4
     per_group = shard_count // groups
     acc_spec = pl.BlockSpec((rows, units), lambda i, tab, cr: (0, 0))
-    panel_spec = pl.BlockSpec((rows, width // groups), lambda i, tab, cr: (0, i))
+    panel_spec = pl.BlockSpec((2 * rows, width // groups), lambda i, tab, cr: (0, i))
     own_part, sent_part = pl.pallas_call(
         hidden_grad_kernel,
         out_shape=(shape((rows, units), jnp.float32), shape((rows, units), jnp.float32)),
@@ -284,14 +301,14 @@
             grid=(groups,),
             in_specs=[
                 panel_spec,
-                panel_spec,
                 pl.BlockSpec((per_group, CAP, BLK, BLK), lambda i, tab, cr: (i, 0, 0, 0)),
             ],
             out_specs=(acc_spec, acc_spec),
+            scratch_shapes=[pltpu.VMEM((2, rows, units), jnp.float32)],
         ),
         name="hidden_grad",
         cost_estimate=cost(shard_count * CAP * 4 * rows * BLK * BLK, 6 << 20),
-    )(table, core_arr, panel, panel_other, weights)
+    )(table, core_arr, panel, weights)
     other_part = swap_core(sent_part)
     d_gate, d_up = pl.pallas_call(
         gates_kernel,
@@ -302,7 +319,7 @@
         cost_estimate=cost(1000, 3 << 19),
     )(own_part, other_part, gate_pre, up_pre)
     d_weight = pl.pallas_call(
-        place_kernel,
+        functools.partial(place_kernel, scale),
         out_shape=shape(down_weight.shape),
         in_specs=[SMEM, SMEM, VMEM, VMEM],
         out_specs=VMEM,

time: 143 us -> 170 us (1.19)
  the two profiles are of different devices: /device:TPU:2 before, /device:TPU:1 now
where the time goes in v2:
time: 170 us; the launch traced here: 169 us
  waiting for transfers between devices  70.8 us (42%)
  starting transfers between devices  51.5 us (30%)
  Pallas kernels  22.7 us (13%)
  between operations  15 us (9%)
  local copies, waits for them, and re-layouts  5.36 us (3%)
  other arithmetic  3.49 us (2%)
    ppermute x11, starting transfers between devices, over_f(): return lax.ppermute(x, 'fsdp', [(i, move(i)) for i in range(fsdp_count)])  47.5 us
    all_gather x1, waiting for transfers between devices, per_device(): lax.all_gather(pair(masked, masked_other, xl), ('fsdp', 'tensor'), axis_i...  37.1 us
    ppermute x11, waiting for transfers between devices, over_f(): return lax.ppermute(x, 'fsdp', [(i, move(i)) for i in range(fsdp_count)])  31.2 us
    pallas_call x1, Pallas kernels, per_device(): pl.pallas_call(partial_kernel, out_shape=shape((ring_y, 2, CAP, BLK, BLK)...  7.95 us
    pallas_call x1, Pallas kernels, per_device(): pl.pallas_call(hidden_grad_kernel, out_shape=(shape((rows, units), jnp.fl...  6.26 us
    ppermute x1, starting transfers between devices, over_t(): lax.ppermute(x, 'tensor', [(i, move(i)) for i in range(tensor_count)])  3.93 us
    unnamed x8, local copies, waits for them, and re-layouts  3.66 us
    another operation x6, other arithmetic, pair(): return jnp.stack([first, second])  3.45 us
  transfers between devices with their start and end apart: 14, of which 9 were waited for; matrix products, arithmetic and copies ran while one was open for 2% of the time, Pallas kernels for 6%

profile of v2, /device:TPU:1, one launch (start us, length us, event | category | flops | bytes accessed | tf_op | source)
XLA Modules:
  0.0 168.9 jit_solution(8980477621104252976)
XLA Ops:
  7.9 2.0 %prep.1 = (bf16[8,8192]{1,0:T(8,128)(2,1)}, bf16[4,128,128]{2,1,0:T(8,128)(2,1)}) custom-call(s32[1]{0:T(128)} %bitcast.f_ref, s32[1]{0:T(128)S(6)} %copy.17.live_ref, s32[6,64]{1,0:T(8,128)} %mask_ref.5, bf16[8,8192]{1,0:T(8,128)(2,1)} %grad_ref.1, bf16[768,256]{1,0:T(8,128)(2,1)} %weight_ref.1), custom_call_target="tpu_custom_call" | custom-call | flops 1000 | bytes 1048576 | tf_op jit(solution)/shard_map/prep/pallas_call | solution.py:213
  9.8 3.9 %collective-permute-start = (bf16[8,8192]{1,0:T(8,128)(2,1)}, bf16[8,8192]{1,0:T(8,128)(2,1)S(1)}, u32[]{:S(2)}, u32[]{:S(2)}) collective-permute-start(bf16[8,8192]{1,0:T(8,128)(2,1)} %get-tuple-element.12), channel_id=1, source_target_pairs={{0,8},{1,9},{2,10},{3,11},{4,12},{5,13},{6,14},{7,15},{8,0},{9,1},... | collective-permute-start | bytes 393224 | tf_op jit(solution)/shard_map/ppermute | solution.py:199
  13.8 2.5 %collective-permute-done = bf16[8,8192]{1,0:T(8,128)(2,1)S(1)} collective-permute-done((bf16[8,8192]{1,0:T(8,128)(2,1)}, bf16[8,8192]{1,0:T(8,128)(2,1)S(1)}, u32[]{:S(2)}, u32[]{:S(2)}) %collective-permute-start) | collective-permute-done | bytes 131104 | tf_op jit(solution)/shard_map/ppermute | solution.py:199
  18.1 2.4 %hidden.1 = (s32[128]{0:T(128)}, bf16[768,128]{1,0:T(8,128)(2,1)}) custom-call(s32[1]{0:T(128)} %bitcast.f_ref, s32[6,64]{1,0:T(8,128)} %mask_ref.5, bf16[128,768]{1,0:T(8,128)(2,1)} %gate_ref.3, bf16[128,768]{1,0:T(8,128)(2,1)} %up_ref.3), custom_call_target="tpu_custom_call" | custom-call | flops 1000 | bytes 1048576 | tf_op jit(solution)/shard_map/hidden/pallas_call | solution.py:225
  20.5 9.3 %collective-permute-start.10 = (bf16[768,128]{1,0:T(8,128)(2,1)}, bf16[768,128]{1,0:T(8,128)(2,1)S(1)}, u32[]{:S(2)}, u32[]{:S(2)}) collective-permute-start(bf16[768,128]{1,0:T(8,128)(2,1)} %get-tuple-element.18), channel_id=1, source_target_pairs={{0,16},{16,0},{32,48},{48,32},{64,80},{80,64},{96,112},{112,96},{1... | collective-permute-start | bytes 589832 | tf_op jit(solution)/shard_map/ppermute | solution.py:196
  32.8 37.1 %all-gather.2.cloned.1.call-done = bf16[32,8,8192]{2,1,0:T(8,128)(2,1)} async-done(((bf16[2,8,8192]{2,1,0:T(8,128)(2,1)}), bf16[32,8,8192]{2,1,0:T(8,128)(2,1)}) %all-gather.2.cloned.1.call-update) | async-done | bytes 4194320 | tf_op jit(solution)/shard_map/all_gather | solution.py:246
  69.9 7.9 %partial.1 = bf16[8,2,4,128,128]{4,3,2,1,0:T(8,128)(2,1)} custom-call(s32[128]{0:T(128)} %get-tuple-element.11.table_ref, s32[1]{0:T(128)} %bitcast.1.core_ref, bf16[2,768,128]{2,1,0:T(8,128)(2,1)} %pad_maximum_fusion.hidden_ref, bf16[256,8192]{1,0:T(8,128)(2,1)} %bitcast.35), custom_call_target="tpu_custom_call" | custom-call | flops 536870912 | bytes 4194304 | tf_op jit(solution)/shard_map/partial/pallas_call | solution.py:272
  78.7 4.6 %collective-permute-start.1 = (bf16[4,128,128]{2,1,0:T(8,128)(2,1)S(1)}, bf16[4,128,128]{2,1,0:T(8,128)(2,1)S(1)}, u32[]{:S(2)}, u32[]{:S(2)}) collective-permute-start(bf16[4,128,128]{2,1,0:T(8,128)(2,1)S(1)} %copy-done.2), channel_id=1, source_target_pairs={{0,32},{16,48},{32,0},{48,16},{64,96},{80,112},{96,64},{112,80},{1... | collective-permute-start | bytes 393224 | tf_op jit(solution)/shard_map/ppermute | solution.py:196
  83.3 3.6 %collective-permute-done.1 = bf16[4,128,128]{2,1,0:T(8,128)(2,1)S(1)} collective-permute-done((bf16[4,128,128]{2,1,0:T(8,128)(2,1)S(1)}, bf16[4,128,128]{2,1,0:T(8,128)(2,1)S(1)}, u32[]{:S(2)}, u32[]{:S(2)}) %collective-permute-start.1) | collective-permute-done | bytes 131104 | tf_op jit(solution)/shard_map/ppermute | solution.py:196
  87.0 3.1 %collective-permute-start.2 = (bf16[2,4,128,128]{3,2,1,0:T(8,128)(2,1)S(1)}, bf16[2,4,128,128]{3,2,1,0:T(8,128)(2,1)S(1)}, u32[]{:S(2)}, u32[]{:S(2)}) collective-permute-start(bf16[2,4,128,128]{3,2,1,0:T(8,128)(2,1)S(1)} %pad_maximum_fusion.2), channel_id=1, source_target_pairs={{0,64},{16,80},{32,96},{48,112},{64,128},{80,144},{96,160},{112,17... | collective-permute-start | bytes 786440 | tf_op jit(solution)/shard_map/ppermute | solution.py:196
  90.1 3.4 %collective-permute-start.3 = (bf16[2,4,128,128]{3,2,1,0:T(8,128)(2,1)S(1)}, bf16[2,4,128,128]{3,2,1,0:T(8,128)(2,1)S(1)}, u32[]{:S(2)}, u32[]{:S(2)}) collective-permute-start(bf16[2,4,128,128]{3,2,1,0:T(8,128)(2,1)S(1)} %pad_maximum_fusion.2), channel_id=1, source_target_pairs={{0,448},{16,464},{32,480},{48,496},{64,0},{80,16},{96,32},{112,48}... | collective-permute-start | bytes 786440 | tf_op jit(solution)/shard_map/ppermute | solution.py:196
  94.1 8.0 %collective-permute-done.2 = bf16[2,4,128,128]{3,2,1,0:T(8,128)(2,1)S(1)} collective-permute-done((bf16[2,4,128,128]{3,2,1,0:T(8,128)(2,1)S(1)}, bf16[2,4,128,128]{3,2,1,0:T(8,128)(2,1)S(1)}, u32[]{:S(2)}, u32[]{:S(2)}) %collective-permute-start.2) | collective-permute-done | bytes 262176 | tf_op jit(solution)/shard_map/ppermute | solution.py:196
  102.1 2.0 %collective-permute-start.4 = (bf16[2,4,128,128]{3,2,1,0:T(8,128)(2,1)S(1)}, bf16[2,4,128,128]{3,2,1,0:T(8,128)(2,1)S(1)}, u32[]{:S(2)}, u32[]{:S(2)}) collective-permute-start(bf16[2,4,128,128]{3,2,1,0:T(8,128)(2,1)S(1)} %collective-permute-done.2), channel_id=1, source_target_pairs={{0,64},{16,80},{32,96},{48,112},{64,128},{80,144},{96,160},{112,17... | collective-permute-start | bytes 786440 | tf_op jit(solution)/shard_map/ppermute | solution.py:196
  104.1 4.5 %collective-permute-start.5 = (bf16[2,4,128,128]{3,2,1,0:T(8,128)(2,1)S(1)}, bf16[2,4,128,128]{3,2,1,0:T(8,128)(2,1)S(1)}, u32[]{:S(2)}, u32[]{:S(2)}) collective-permute-start(bf16[2,4,128,128]{3,2,1,0:T(8,128)(2,1)S(1)} %collective-permute-done.3), channel_id=1, source_target_pairs={{0,448},{16,464},{32,480},{48,496},{64,0},{80,16},{96,32},{112,48}... | collective-permute-start | bytes 786440 | tf_op jit(solution)/shard_map/ppermute | solution.py:196
  108.7 8.7 %collective-permute-done.4 = bf16[2,4,128,128]{3,2,1,0:T(8,128)(2,1)S(1)} collective-permute-done((bf16[2,4,128,128]{3,2,1,0:T(8,128)(2,1)S(1)}, bf16[2,4,128,128]{3,2,1,0:T(8,128)(2,1)S(1)}, u32[]{:S(2)}, u32[]{:S(2)}) %collective-permute-start.4) | collective-permute-done | bytes 262176 | tf_op jit(solution)/shard_map/ppermute | solution.py:196
  119.3 4.6 %collective-permute-start.7 = (bf16[2,4,128,128]{3,2,1,0:T(8,128)(2,1)S(1)}, bf16[2,4,128,128]{3,2,1,0:T(8,128)(2,1)S(1)}, u32[]{:S(2)}, u32[]{:S(2)}) collective-permute-start(bf16[2,4,128,128]{3,2,1,0:T(8,128)(2,1)S(1)} %collective-permute-done.5), channel_id=1, source_target_pairs={{0,448},{16,464},{32,480},{48,496},{64,0},{80,16},{96,32},{112,48}... | collective-permute-start | bytes 786440 | tf_op jit(solution)/shard_map/ppermute | solution.py:196
  124.0 3.4 %collective-permute-done.6 = bf16[2,4,128,128]{3,2,1,0:T(8,128)(2,1)S(1)} collective-permute-done((bf16[2,4,128,128]{3,2,1,0:T(8,128)(2,1)S(1)}, bf16[2,4,128,128]{3,2,1,0:T(8,128)(2,1)S(1)}, u32[]{:S(2)}, u32[]{:S(2)}) %collective-permute-start.6) | collective-permute-done | bytes 262176 | tf_op jit(solution)/shard_map/ppermute | solution.py:196
  127.4 2.9 %collective-permute-start.8 = (bf16[2,4,128,128]{3,2,1,0:T(8,128)(2,1)S(1)}, bf16[2,4,128,128]{3,2,1,0:T(8,128)(2,1)S(1)}, u32[]{:S(2)}, u32[]{:S(2)}) collective-permute-start(bf16[2,4,128,128]{3,2,1,0:T(8,128)(2,1)S(1)} %collective-permute-done.6), channel_id=1, source_target_pairs={{0,64},{16,80},{32,96},{48,112},{64,128},{80,144},{96,160},{112,17... | collective-permute-start | bytes 786440 | tf_op jit(solution)/shard_map/ppermute | solution.py:196
  130.5 5.3 %collective-permute-done.8 = bf16[2,4,128,128]{3,2,1,0:T(8,128)(2,1)S(1)} collective-permute-done((bf16[2,4,128,128]{3,2,1,0:T(8,128)(2,1)S(1)}, bf16[2,4,128,128]{3,2,1,0:T(8,128)(2,1)S(1)}, u32[]{:S(2)}, u32[]{:S(2)}) %collective-permute-start.8) | collective-permute-done | bytes 262176 | tf_op jit(solution)/shard_map/ppermute | solution.py:196
  137.2 6.3 %hidden_grad.1 = (f32[128,768]{1,0:T(8,128)}, f32[128,768]{1,0:T(8,128)}) custom-call(s32[128]{0:T(128)} %get-tuple-element.11.table_ref, s32[1]{0:T(128)} %bitcast.1.core_ref, bf16[256,8192]{1,0:T(8,128)(2,1)} %bitcast.36, bf16[16,4,128,128]{3,2,1,0:T(8,128)(2,1)} %bitcast.37), custom_call_target="tpu_custom_call" | custom-call | flops 536870912 | bytes 6291456 | tf_op jit(solution)/shard_map/hidden_grad/pallas_call | solution.py:296
  143.4 6.6 %collective-permute-start.9 = (f32[128,768]{1,0:T(8,128)}, f32[128,768]{1,0:T(8,128)S(1)}, u32[]{:S(2)}, u32[]{:S(2)}) collective-permute-start(f32[128,768]{1,0:T(8,128)} %get-tuple-element.15), channel_id=1, source_target_pairs={{0,16},{16,0},{32,48},{48,32},{64,80},{80,64},{96,112},{112,96},{1... | collective-permute-start | bytes 1179656 | tf_op jit(solution)/shard_map/ppermute | solution.py:196
  151.0 4.6 %collective-permute-start.11 = (bf16[4,128,128]{2,1,0:T(8,128)(2,1)S(1)}, bf16[4,128,128]{2,1,0:T(8,128)(2,1)S(1)}, u32[]{:S(2)}, u32[]{:S(2)}) collective-permute-start(bf16[4,128,128]{2,1,0:T(8,128)(2,1)S(1)} %dynamic-slice_bitcast_fusion), channel_id=1, source_target_pairs={{0,32},{16,48},{32,0},{48,16},{64,96},{80,112},{96,64},{112,80},{1... | collective-permute-start | bytes 393224 | tf_op jit(solution)/shard_map/ppermute | solution.py:196
  156.4 2.1 %gates.1 = (bf16[128,768]{1,0:T(8,128)(2,1)}, bf16[128,768]{1,0:T(8,128)(2,1)}) custom-call(f32[128,768]{1,0:T(8,128)} %get-tuple-element.14.own_ref, f32[128,768]{1,0:T(8,128)} %copy-done.1, bf16[128,768]{1,0:T(8,128)(2,1)} %gate_ref.3, bf16[128,768]{1,0:T(8,128)(2,1)} %up_ref.3), custom_call_target="tpu_custom_call" | custom-call | flops 1000 | bytes 1572864 | tf_op jit(solution)/shard_map/gates/pallas_call | solution.py:313
  160.1 2.0 %place.1 = bf16[768,256]{1,0:T(8,128)(2,1)} custom-call(s32[1]{0:T(128)} %bitcast.f_ref, s32[6,64]{1,0:T(8,128)} %mask_ref.5, bf16[2,4,128,128]{3,2,1,0:T(8,128)(2,1)} %bitcast.38, bf16[4,128,128]{2,1,0:T(8,128)(2,1)} %copy-done.3), custom_call_target="tpu_custom_call" | custom-call | flops 1000 | bytes 1048576 | tf_op jit(solution)/shard_map/place/pallas_call | solution.py:321
  (36 shorter events, 13.1 us)
Async XLA Ops:
  7.2 62.7 %all-gather.2.cloned.1.call-start = ((), (), s32[]{:S(2)}) async-start(), calls=%async_computation.1 | async-start | bytes 4456448 | tf_op jit(solution)/shard_map/all_gather | solution.py:246
  9.8 6.5 %collective-permute-start = (bf16[8,8192]{1,0:T(8,128)(2,1)}, bf16[8,8192]{1,0:T(8,128)(2,1)S(1)}, u32[]{:S(2)}, u32[]{:S(2)}) collective-permute-start(bf16[8,8192]{1,0:T(8,128)(2,1)} %get-tuple-element.12), channel_id=1, source_target_pairs={{0,8},{1,9},{2,10},{3,11},{4,12},{5,13},{6,14},{7,15},{8,0},{9,1},... | collective-permute-start | bytes 393224 | tf_op jit(solution)/shard_map/ppermute | solution.py:199
  18.0 132.0 %reduce-scatter.2.cloned.1.call-start = ((), (), s32[]{:S(2)}) async-start(), calls=%async_computation.2 | async-start | bytes 2359296 | tf_op jit(solution)/shard_map/reduce_scatter | solution.py:286
  20.5 10.6 %collective-permute-start.10 = (bf16[768,128]{1,0:T(8,128)(2,1)}, bf16[768,128]{1,0:T(8,128)(2,1)S(1)}, u32[]{:S(2)}, u32[]{:S(2)}) collective-permute-start(bf16[768,128]{1,0:T(8,128)(2,1)} %get-tuple-element.18), channel_id=1, source_target_pairs={{0,16},{16,0},{32,48},{48,32},{64,80},{80,64},{96,112},{112,96},{1... | collective-permute-start | bytes 589832 | tf_op jit(solution)/shard_map/ppermute | solution.py:196
  77.8 0.9 copy-start.2
  78.7 8.2 %collective-permute-start.1 = (bf16[4,128,128]{2,1,0:T(8,128)(2,1)S(1)}, bf16[4,128,128]{2,1,0:T(8,128)(2,1)S(1)}, u32[]{:S(2)}, u32[]{:S(2)}) collective-permute-start(bf16[4,128,128]{2,1,0:T(8,128)(2,1)S(1)} %copy-done.2), channel_id=1, source_target_pairs={{0,32},{16,48},{32,0},{48,16},{64,96},{80,112},{96,64},{112,80},{1... | collective-permute-start | bytes 393224 | tf_op jit(solution)/shard_map/ppermute | solution.py:196
  87.0 15.1 %collective-permute-start.2 = (bf16[2,4,128,128]{3,2,1,0:T(8,128)(2,1)S(1)}, bf16[2,4,128,128]{3,2,1,0:T(8,128)(2,1)S(1)}, u32[]{:S(2)}, u32[]{:S(2)}) collective-permute-start(bf16[2,4,128,128]{3,2,1,0:T(8,128)(2,1)S(1)} %pad_maximum_fusion.2), channel_id=1, source_target_pairs={{0,64},{16,80},{32,96},{48,112},{64,128},{80,144},{96,160},{112,17... | collective-permute-start | bytes 786440 | tf_op jit(solution)/shard_map/ppermute | solution.py:196
  90.1 14.0 %collective-permute-start.3 = (bf16[2,4,128,128]{3,2,1,0:T(8,128)(2,1)S(1)}, bf16[2,4,128,128]{3,2,1,0:T(8,128)(2,1)S(1)}, u32[]{:S(2)}, u32[]{:S(2)}) collective-permute-start(bf16[2,4,128,128]{3,2,1,0:T(8,128)(2,1)S(1)} %pad_maximum_fusion.2), channel_id=1, source_target_pairs={{0,448},{16,464},{32,480},{48,496},{64,0},{80,16},{96,32},{112,48}... | collective-permute-start | bytes 786440 | tf_op jit(solution)/shard_map/ppermute | solution.py:196
  102.1 15.3 %collective-permute-start.4 = (bf16[2,4,128,128]{3,2,1,0:T(8,128)(2,1)S(1)}, bf16[2,4,128,128]{3,2,1,0:T(8,128)(2,1)S(1)}, u32[]{:S(2)}, u32[]{:S(2)}) collective-permute-start(bf16[2,4,128,128]{3,2,1,0:T(8,128)(2,1)S(1)} %collective-permute-done.2), channel_id=1, source_target_pairs={{0,64},{16,80},{32,96},{48,112},{64,128},{80,144},{96,160},{112,17... | collective-permute-start | bytes 786440 | tf_op jit(solution)/shard_map/ppermute | solution.py:196
  104.1 15.2 %collective-permute-start.5 = (bf16[2,4,128,128]{3,2,1,0:T(8,128)(2,1)S(1)}, bf16[2,4,128,128]{3,2,1,0:T(8,128)(2,1)S(1)}, u32[]{:S(2)}, u32[]{:S(2)}) collective-permute-start(bf16[2,4,128,128]{3,2,1,0:T(8,128)(2,1)S(1)} %collective-permute-done.3), channel_id=1, source_target_pairs={{0,448},{16,464},{32,480},{48,496},{64,0},{80,16},{96,32},{112,48}... | collective-permute-start | bytes 786440 | tf_op jit(solution)/shard_map/ppermute | solution.py:196
  117.4 10.0 %collective-permute-start.6 = (bf16[2,4,128,128]{3,2,1,0:T(8,128)(2,1)S(1)}, bf16[2,4,128,128]{3,2,1,0:T(8,128)(2,1)S(1)}, u32[]{:S(2)}, u32[]{:S(2)}) collective-permute-start(bf16[2,4,128,128]{3,2,1,0:T(8,128)(2,1)S(1)} %collective-permute-done.4), channel_id=1, source_target_pairs={{0,64},{16,80},{32,96},{48,112},{64,128},{80,144},{96,160},{112,17... | collective-permute-start | bytes 786440 | tf_op jit(solution)/shard_map/ppermute | solution.py:196
  119.3 11.1 %collective-permute-start.7 = (bf16[2,4,128,128]{3,2,1,0:T(8,128)(2,1)S(1)}, bf16[2,4,128,128]{3,2,1,0:T(8,128)(2,1)S(1)}, u32[]{:S(2)}, u32[]{:S(2)}) collective-permute-start(bf16[2,4,128,128]{3,2,1,0:T(8,128)(2,1)S(1)} %collective-permute-done.5), channel_id=1, source_target_pairs={{0,448},{16,464},{32,480},{48,496},{64,0},{80,16},{96,32},{112,48}... | collective-permute-start | bytes 786440 | tf_op jit(solution)/shard_map/ppermute | solution.py:196
  127.4 8.3 %collective-permute-start.8 = (bf16[2,4,128,128]{3,2,1,0:T(8,128)(2,1)S(1)}, bf16[2,4,128,128]{3,2,1,0:T(8,128)(2,1)S(1)}, u32[]{:S(2)}, u32[]{:S(2)}) collective-permute-start(bf16[2,4,128,128]{3,2,1,0:T(8,128)(2,1)S(1)} %collective-permute-done.6), channel_id=1, source_target_pairs={{0,64},{16,80},{32,96},{48,112},{64,128},{80,144},{96,160},{112,17... | collective-permute-start | bytes 786440 | tf_op jit(solution)/shard_map/ppermute | solution.py:196
  135.8 1.4 copy-start
  143.4 12.2 %collective-permute-start.9 = (f32[128,768]{1,0:T(8,128)}, f32[128,768]{1,0:T(8,128)S(1)}, u32[]{:S(2)}, u32[]{:S(2)}) collective-permute-start(f32[128,768]{1,0:T(8,128)} %get-tuple-element.15), channel_id=1, source_target_pairs={{0,16},{16,0},{32,48},{48,32},{64,80},{80,64},{96,112},{112,96},{1... | collective-permute-start | bytes 1179656 | tf_op jit(solution)/shard_map/ppermute | solution.py:196
  151.0 8.4 %collective-permute-start.11 = (bf16[4,128,128]{2,1,0:T(8,128)(2,1)S(1)}, bf16[4,128,128]{2,1,0:T(8,128)(2,1)S(1)}, u32[]{:S(2)}, u32[]{:S(2)}) collective-permute-start(bf16[4,128,128]{2,1,0:T(8,128)(2,1)S(1)} %dynamic-slice_bitcast_fusion), channel_id=1, source_target_pairs={{0,32},{16,48},{32,0},{48,16},{64,96},{80,112},{96,64},{112,80},{1... | collective-permute-start | bytes 393224 | tf_op jit(solution)/shard_map/ppermute | solution.py:196
  155.6 0.7 copy-start.1
  159.4 0.7 copy-start.3
Sparse Core Ops, SparseCore 0:
  18.1 51.6 all-gather.1
  78.0 47.7 reduce-scatter.1

commit v3 on v2

--- a/solution.py
+++ b/solution.py
@@ -29,11 +29,8 @@
     return jnp.swapaxes(x.reshape(rows // (2 * TOK), 2, TOK, width), 0, 1).reshape(rows, width)
 
 
-def prep_kernel(f_ref, live_ref, mask_ref, grad_ref, weight_ref, masked_ref, packed_ref):
+def pack_kernel(f_ref, mask_ref, weight_ref, packed_ref):
     row_blocks = mask_ref.shape[0]
-    rows = lax.broadcasted_iota(jnp.int32, grad_ref.shape, 0)
-    value = grad_ref[...].astype(jnp.float32)
-    masked_ref[...] = jnp.where(rows < live_ref[0], value, 0.0).astype(jnp.bfloat16)
     packed_ref[...] = jnp.zeros_like(packed_ref)
     count = jnp.int32(0)
     for r in range(row_blocks):
@@ -73,26 +70,29 @@
 
 
 def partial_kernel(table_ref, core_ref, hidden_ref, panel_ref, out_ref):
-    dest = pl.program_id(0)
+    count = out_ref.shape[0]
     wide = 2 * BLK
-    for xh in range(2):
-        s = 2 * dest + xh
-        at = pl.multiple_of((2 * xh + core_ref[0]) * wide, wide)
-        right = panel_ref[:, pl.ds(at, wide)]
-        places = [table_ref[s * TAB + k] for k in range(CAP)]
-        rows = [pl.multiple_of((b >> 1) * BLK, BLK) for b in places]
-        left = jnp.concatenate(
-            [
-                jnp.concatenate([hidden_ref[c, pl.ds(r, BLK), :] for c in range(2)], axis=1)
-                for r in rows
-            ],
-            axis=0,
-        )
-        term = jnp.dot(left, right, preferred_element_type=jnp.float32)
-        for k, b in enumerate(places):
-            tile = term[k * BLK : (k + 1) * BLK]
-            kept = jnp.where((b & 1) == 0, tile[:, :BLK], tile[:, BLK:])
-            out_ref[0, xh, k] = kept.astype(jnp.bfloat16)
+    for i in range(count):
+        dest = pl.program_id(0) * count + i
+        for flip in range(2):
+            xh = flip ^ core_ref[1]
+            s = 2 * dest + xh
+            at = pl.multiple_of(i * 4 * wide + (2 * xh + core_ref[0]) * wide, wide)
+            right = panel_ref[:, pl.ds(at, wide)]
+            places = [table_ref[s * TAB + k] for k in range(CAP)]
+            rows = [pl.multiple_of((b >> 1) * BLK, BLK) for b in places]
+            left = jnp.concatenate(
+                [
+                    jnp.concatenate([hidden_ref[c, pl.ds(r, BLK), :] for c in range(2)], axis=1)
+                    for r in rows
+                ],
+                axis=0,
+            )
+            term = jnp.dot(left, right, preferred_element_type=jnp.float32)
+            for k, b in enumerate(places):
+                tile = term[k * BLK : (k + 1) * BLK]
+                kept = jnp.where((b & 1) == 0, tile[:, :BLK], tile[:, BLK:])
+                out_ref[i, flip, k] = kept.astype(jnp.bfloat16)
 
 
 def hidden_grad_kernel(
@@ -151,7 +151,6 @@
 
 def place_kernel(scale, f_ref, mask_ref, own_ref, other_ref, out_ref):
     row_blocks = mask_ref.shape[0]
-    xh = (f_ref[0] >> 1) & 1
     out_ref[...] = jnp.zeros_like(out_ref)
     count = jnp.int32(0)
     for r in range(row_blocks):
@@ -160,7 +159,7 @@
 
             @pl.when(kept == 1)
             def _(r=r, c=c, count=count):
-                total = own_ref[xh, count].astype(jnp.float32) + other_ref[count].astype(
+                total = own_ref[0, count].astype(jnp.float32) + other_ref[count].astype(
                     jnp.float32
                 )
                 out_ref[r * BLK : (r + 1) * BLK, c * BLK : (c + 1) * BLK] = (
@@ -210,15 +209,16 @@
     def swap_xl(x):
         return over_t(x, lambda i: (i + ring_z) % tensor_count)
 
-    masked, packed = pl.pallas_call(
-        prep_kernel,
-        out_shape=(shape((tok, width)), shape((CAP, BLK, BLK))),
-        in_specs=[SMEM, SMEM, SMEM, VMEM, VMEM],
-        out_specs=(VMEM, VMEM),
-        name="prep",
+    grad_other = swap_xl(out_grad)
+    live_other = swap_xl(live_rows)
+    packed = pl.pallas_call(
+        pack_kernel,
+        out_shape=shape((CAP, BLK, BLK)),
+        in_specs=[SMEM, SMEM, VMEM],
+        out_specs=VMEM,
+        name="pack",
         cost_estimate=cost(1000, 1 << 20),
-    )(f_arr, live_rows, tile_mask, out_grad, down_weight)
-    masked_other = swap_xl(masked)
+    )(f_arr, tile_mask, down_weight)
     packed_other = swap_xh(packed)
 
     shard_count = fsdp_count // 2
@@ -233,9 +233,15 @@
     hidden_other = swap_core(hidden_t)
 
     def pair(own, other, index):
-        first = jnp.where(index == 0, own, other)
-        second = jnp.where(index == 0, other, own)
-        return jnp.stack([first, second])
+        first = (jnp.arange(2) == index).reshape((2,) + (1,) * own.ndim)
+        return jnp.where(first, own[None], other[None])
+
+    live = pair(live_rows, live_other, xl).reshape(2, 1, 1)
+    masked = jnp.where(
+        jnp.arange(tok)[None, :, None] < live,
+        pair(out_grad, grad_other, xl),
+        jnp.zeros((), jnp.bfloat16),
+    )
 
     columns = [[k + 4 * i for i in range(ring_y)] for k in range(4)]
     chips = [
@@ -244,7 +250,7 @@
         for half in range(2)
     ]
     panel = lax.all_gather(
-        pair(masked, masked_other, xl),
+        masked,
         ("fsdp", "tensor"),
         axis_index_groups=chips,
         tiled=True,
@@ -265,19 +271,20 @@
             down = y_step(down, -1)
             weights = put(weights, down, y + d)
     weights = weights.reshape(shard_count, CAP, BLK, BLK)
-    core_arr = (f & 1).reshape(1).astype(jnp.int32)
-
-    panel_spec = pl.BlockSpec((2 * rows, width // ring_y), lambda i, tab, cr: (0, i))
+    core_arr = jnp.stack([f & 1, xh]).astype(jnp.int32)
+    per_step = ring_y // 2
+
+    panel_spec = pl.BlockSpec((2 * rows, width // ring_y * per_step), lambda i, tab, cr: (0, i))
     whole = pl.BlockSpec((2, units, rows), lambda i, tab, cr: (0, 0, 0))
     tiles = pl.pallas_call(
         partial_kernel,
         out_shape=shape((ring_y, 2, CAP, BLK, BLK)),
         grid_spec=pltpu.PrefetchScalarGridSpec(
             num_scalar_prefetch=2,
-            grid=(ring_y,),
+            grid=(ring_y // per_step,),
             in_specs=[whole, panel_spec],
             out_specs=pl.BlockSpec(
-                (1, 2, CAP, BLK, BLK), lambda i, tab, cr: (i, 0, 0, 0, 0)
+                (per_step, 2, CAP, BLK, BLK), lambda i, tab, cr: (i, 0, 0, 0, 0)
             ),
         ),
         name="partial",
@@ -286,7 +293,7 @@
     sums = lax.psum_scatter(
         tiles, "fsdp", scatter_dimension=0, axis_index_groups=columns, tiled=True
     )[0]
-    send_sum = lax.dynamic_index_in_dim(sums, 1 - xh, 0, keepdims=False)
+    send_sum = sums[1]
     other_sum = swap_xh(send_sum)
 
     groups = 4
@@ -316,6 +323,7 @@
         in_specs=[VMEM] * 4,
         out_specs=(VMEM, VMEM),
         name="gates",
+        compiler_params=pltpu.CompilerParams(vmem_limit_bytes=16 << 20),
         cost_estimate=cost(1000, 3 << 19),
     )(own_part, other_part, gate_pre, up_pre)
     d_weight = pl.pallas_call(
@@ -324,6 +332,7 @@
         in_specs=[SMEM, SMEM, VMEM, VMEM],
         out_specs=VMEM,
         name="place",
+        compiler_params=pltpu.CompilerParams(vmem_limit_bytes=16 << 20),
         cost_estimate=cost(1000, 1 << 20),
     )(f_arr, tile_mask, sums, other_sum)
     return (d_gate, d_up, d_weight)

time: 170 us -> 170 us (level)
  Pallas kernels: 22.7 us -> 17.9 us
  waiting for transfers between devices: 70.8 us -> 73.4 us
  other arithmetic: 3.49 us -> 5.96 us
    select_n x0 -> x4, other arithmetic: none -> 5.05 us  [the longest x3 3.34 us: pair(): return jnp.where(first, own[None], other[None])]
    pallas_call x1, Pallas kernels: 7.95 us -> 4.79 us  [per_device(): pl.pallas_call(partial_kernel, out_shape=shape((ring_y, 2, CAP, BLK, BLK)...]
    another operation x6 -> x1, other arithmetic: 3.45 us -> 0.64 us  [per_device(): core_arr = jnp.stack([f & 1, xh]).astype(jnp.int32)]
    ppermute x11, starting transfers between devices: 47.5 us -> 45.6 us  [over_f(): return lax.ppermute(x, 'fsdp', [(i, move(i)) for i in range(fsdp_count)])]
    ppermute x1 -> x2, starting transfers between devices: 3.93 us -> 5.86 us  [over_t(): lax.ppermute(x, 'tensor', [(i, move(i)) for i in range(tensor_count)])]
    unnamed x8 -> x14, local copies, waits for them, and re-layouts: 3.66 us -> 3.35 us
  transfers between devices with their start and end apart: 14 -> 15, of which waited for: 9 -> 9; matrix products, arithmetic and copies ran while one was open for 2% -> 4% of each run, Pallas kernels for 6% -> 7%
where the time goes in v3:
time: 170 us; the launch traced here: 169 us
  waiting for transfers between devices  73.4 us (43%)
  starting transfers between devices  51.5 us (30%)
  Pallas kernels  17.9 us (11%)
  between operations  15 us (9%)
  other arithmetic  5.96 us (4%)
  local copies, waits for them, and re-layouts  5.04 us (3%)
    ppermute x11, starting transfers between devices, over_f(): return lax.ppermute(x, 'fsdp', [(i, move(i)) for i in range(fsdp_count)])  45.6 us
    all_gather x1, waiting for transfers between devices, per_device(): lax.all_gather(masked, ('fsdp', 'tensor'), axis_index_groups=chips, tiled...  37.9 us
    ppermute x11, waiting for transfers between devices, over_f(): return lax.ppermute(x, 'fsdp', [(i, move(i)) for i in range(fsdp_count)])  32.8 us
    pallas_call x1, Pallas kernels, per_device(): pl.pallas_call(hidden_grad_kernel, out_shape=(shape((rows, units), jnp.fl...  6.4 us
    ppermute x2, starting transfers between devices, over_t(): lax.ppermute(x, 'tensor', [(i, move(i)) for i in range(tensor_count)])  5.86 us
    pallas_call x1, Pallas kernels, per_device(): pl.pallas_call(partial_kernel, out_shape=shape((ring_y, 2, CAP, BLK, BLK)...  4.79 us
  transfers between devices with their start and end apart: 15, of which 9 were waited for; matrix products, arithmetic and copies ran while one was open for 4% of the time, Pallas kernels for 7%

profile of v3, /device:TPU:1, one launch (start us, length us, event | category | flops | bytes accessed | tf_op | source)
XLA Modules:
  0.0 168.9 jit_solution(16218299391184215329)
XLA Ops:
  7.2 3.9 %collective-permute-start = (s32[1]{0:T(128)}, s32[1]{0:T(128)}, u32[]{:S(2)}, u32[]{:S(2)}) collective-permute-start(s32[1]{0:T(128)} %param.7), channel_id=1, source_target_pairs={{0,8},{1,9},{2,10},{3,11},{4,12},{5,13},{6,14},{7,15},{8,0},{9,1},... | collective-permute-start | bytes 20 | tf_op jit(solution)/shard_map/ppermute | solution.py:198
  11.2 1.9 %collective-permute-start.1 = (bf16[8,8192]{1,0:T(8,128)(2,1)}, bf16[8,8192]{1,0:T(8,128)(2,1)S(1)}, u32[]{:S(2)}, u32[]{:S(2)}) collective-permute-start(bf16[8,8192]{1,0:T(8,128)(2,1)} %param.6), channel_id=1, source_target_pairs={{0,8},{1,9},{2,10},{3,11},{4,12},{5,13},{6,14},{7,15},{8,0},{9,1},... | collective-permute-start | bytes 393224 | tf_op jit(solution)/shard_map/ppermute | solution.py:198
  14.4 2.7 %collective-permute-done.1 = bf16[8,8192]{1,0:T(8,128)(2,1)S(1)} collective-permute-done((bf16[8,8192]{1,0:T(8,128)(2,1)}, bf16[8,8192]{1,0:T(8,128)(2,1)S(1)}, u32[]{:S(2)}, u32[]{:S(2)}) %collective-permute-start.1) | collective-permute-done | bytes 131104 | tf_op jit(solution)/shard_map/ppermute | solution.py:198
  18.9 2.4 %hidden.1 = (s32[128]{0:T(128)}, bf16[768,128]{1,0:T(8,128)(2,1)}) custom-call(s32[1]{0:T(128)} %bitcast.f_ref, s32[6,64]{1,0:T(8,128)} %mask_ref.5, bf16[128,768]{1,0:T(8,128)(2,1)} %gate_ref.3, bf16[128,768]{1,0:T(8,128)(2,1)} %up_ref.3), custom_call_target="tpu_custom_call" | custom-call | flops 1000 | bytes 1048576 | tf_op jit(solution)/shard_map/hidden/pallas_call | solution.py:225
  21.3 7.9 %collective-permute-start.11 = (bf16[768,128]{1,0:T(8,128)(2,1)}, bf16[768,128]{1,0:T(8,128)(2,1)S(1)}, u32[]{:S(2)}, u32[]{:S(2)}) collective-permute-start(bf16[768,128]{1,0:T(8,128)(2,1)} %get-tuple-element.14), channel_id=1, source_target_pairs={{0,16},{16,0},{32,48},{48,32},{64,80},{80,64},{96,112},{112,96},{1... | collective-permute-start | bytes 589832 | tf_op jit(solution)/shard_map/ppermute | solution.py:195
  32.2 37.9 %all-gather.2.cloned.1.call-done = bf16[32,8,8192]{2,1,0:T(8,128)(2,1)} async-done(((bf16[2,8,8192]{2,1,0:T(8,128)(2,1)}), bf16[32,8,8192]{2,1,0:T(8,128)(2,1)}) %all-gather.2.cloned.1.call-update) | async-done | bytes 4194320 | tf_op jit(solution)/shard_map/all_gather | solution.py:252
  70.2 4.8 %partial.1 = bf16[8,2,4,128,128]{4,3,2,1,0:T(8,128)(2,1)} custom-call(s32[128]{0:T(128)} %get-tuple-element.9.table_ref, s32[2]{0:T(128)} %pad_add_fusion.core_ref, bf16[2,768,128]{2,1,0:T(8,128)(2,1)} %broadcast_select_fusion.hidden_ref, bf16[256,8192]{1,0:T(8,128)(2,1)} %bitcast.26), custom_call_target="tpu_custom_call" | custom-call | flops 536870912 | bytes 4194304 | tf_op jit(solution)/shard_map/partial/pallas_call | solution.py:279
  75.0 1.8 %pack.1 = bf16[4,128,128]{2,1,0:T(8,128)(2,1)} custom-call(s32[1]{0:T(128)} %bitcast.f_ref, s32[6,64]{1,0:T(8,128)} %mask_ref.5, bf16[768,256]{1,0:T(8,128)(2,1)} %weight_ref.1), custom_call_target="tpu_custom_call" | custom-call | flops 1000 | bytes 1048576 | tf_op jit(solution)/shard_map/pack/pallas_call | solution.py:214
  76.8 4.7 %collective-permute-start.2 = (bf16[4,128,128]{2,1,0:T(8,128)(2,1)}, bf16[4,128,128]{2,1,0:T(8,128)(2,1)S(1)}, u32[]{:S(2)}, u32[]{:S(2)}) collective-permute-start(bf16[4,128,128]{2,1,0:T(8,128)(2,1)} %pack.1), channel_id=1, source_target_pairs={{0,32},{16,48},{32,0},{48,16},{64,96},{80,112},{96,64},{112,80},{1... | collective-permute-start | bytes 393224 | tf_op jit(solution)/shard_map/ppermute | solution.py:195
  81.6 3.7 %collective-permute-done.2 = bf16[4,128,128]{2,1,0:T(8,128)(2,1)S(1)} collective-permute-done((bf16[4,128,128]{2,1,0:T(8,128)(2,1)}, bf16[4,128,128]{2,1,0:T(8,128)(2,1)S(1)}, u32[]{:S(2)}, u32[]{:S(2)}) %collective-permute-start.2) | collective-permute-done | bytes 131104 | tf_op jit(solution)/shard_map/ppermute | solution.py:195
  86.3 3.1 %collective-permute-start.3 = (bf16[2,4,128,128]{3,2,1,0:T(8,128)(2,1)S(1)}, bf16[2,4,128,128]{3,2,1,0:T(8,128)(2,1)S(1)}, u32[]{:S(2)}, u32[]{:S(2)}) collective-permute-start(bf16[2,4,128,128]{3,2,1,0:T(8,128)(2,1)S(1)} %broadcast_select_fusion.1), channel_id=1, source_target_pairs={{0,64},{16,80},{32,96},{48,112},{64,128},{80,144},{96,160},{112,17... | collective-permute-start | bytes 786440 | tf_op jit(solution)/shard_map/ppermute | solution.py:195
  89.4 3.4 %collective-permute-start.4 = (bf16[2,4,128,128]{3,2,1,0:T(8,128)(2,1)S(1)}, bf16[2,4,128,128]{3,2,1,0:T(8,128)(2,1)S(1)}, u32[]{:S(2)}, u32[]{:S(2)}) collective-permute-start(bf16[2,4,128,128]{3,2,1,0:T(8,128)(2,1)S(1)} %broadcast_select_fusion.1), channel_id=1, source_target_pairs={{0,448},{16,464},{32,480},{48,496},{64,0},{80,16},{96,32},{112,48}... | collective-permute-start | bytes 786440 | tf_op jit(solution)/shard_map/ppermute | solution.py:195
  93.6 9.3 %collective-permute-done.3 = bf16[2,4,128,128]{3,2,1,0:T(8,128)(2,1)S(1)} collective-permute-done((bf16[2,4,128,128]{3,2,1,0:T(8,128)(2,1)S(1)}, bf16[2,4,128,128]{3,2,1,0:T(8,128)(2,1)S(1)}, u32[]{:S(2)}, u32[]{:S(2)}) %collective-permute-start.3) | collective-permute-done | bytes 262176 | tf_op jit(solution)/shard_map/ppermute | solution.py:195
  102.9 1.9 %collective-permute-start.5 = (bf16[2,4,128,128]{3,2,1,0:T(8,128)(2,1)S(1)}, bf16[2,4,128,128]{3,2,1,0:T(8,128)(2,1)S(1)}, u32[]{:S(2)}, u32[]{:S(2)}) collective-permute-start(bf16[2,4,128,128]{3,2,1,0:T(8,128)(2,1)S(1)} %collective-permute-done.3), channel_id=1, source_target_pairs={{0,64},{16,80},{32,96},{48,112},{64,128},{80,144},{96,160},{112,17... | collective-permute-start | bytes 786440 | tf_op jit(solution)/shard_map/ppermute | solution.py:195
  104.8 4.6 %collective-permute-start.6 = (bf16[2,4,128,128]{3,2,1,0:T(8,128)(2,1)S(1)}, bf16[2,4,128,128]{3,2,1,0:T(8,128)(2,1)S(1)}, u32[]{:S(2)}, u32[]{:S(2)}) collective-permute-start(bf16[2,4,128,128]{3,2,1,0:T(8,128)(2,1)S(1)} %collective-permute-done.4), channel_id=1, source_target_pairs={{0,448},{16,464},{32,480},{48,496},{64,0},{80,16},{96,32},{112,48}... | collective-permute-start | bytes 786440 | tf_op jit(solution)/shard_map/ppermute | solution.py:195
  109.5 9.1 %collective-permute-done.5 = bf16[2,4,128,128]{3,2,1,0:T(8,128)(2,1)S(1)} collective-permute-done((bf16[2,4,128,128]{3,2,1,0:T(8,128)(2,1)S(1)}, bf16[2,4,128,128]{3,2,1,0:T(8,128)(2,1)S(1)}, u32[]{:S(2)}, u32[]{:S(2)}) %collective-permute-start.5) | collective-permute-done | bytes 262176 | tf_op jit(solution)/shard_map/ppermute | solution.py:195
  118.6 1.9 %collective-permute-start.7 = (bf16[2,4,128,128]{3,2,1,0:T(8,128)(2,1)S(1)}, bf16[2,4,128,128]{3,2,1,0:T(8,128)(2,1)S(1)}, u32[]{:S(2)}, u32[]{:S(2)}) collective-permute-start(bf16[2,4,128,128]{3,2,1,0:T(8,128)(2,1)S(1)} %collective-permute-done.5), channel_id=1, source_target_pairs={{0,64},{16,80},{32,96},{48,112},{64,128},{80,144},{96,160},{112,17... | collective-permute-start | bytes 786440 | tf_op jit(solution)/shard_map/ppermute | solution.py:195
  120.5 4.6 %collective-permute-start.8 = (bf16[2,4,128,128]{3,2,1,0:T(8,128)(2,1)S(1)}, bf16[2,4,128,128]{3,2,1,0:T(8,128)(2,1)S(1)}, u32[]{:S(2)}, u32[]{:S(2)}) collective-permute-start(bf16[2,4,128,128]{3,2,1,0:T(8,128)(2,1)S(1)} %collective-permute-done.6), channel_id=1, source_target_pairs={{0,448},{16,464},{32,480},{48,496},{64,0},{80,16},{96,32},{112,48}... | collective-permute-start | bytes 786440 | tf_op jit(solution)/shard_map/ppermute | solution.py:195
  126.9 1.9 %collective-permute-start.9 = (bf16[2,4,128,128]{3,2,1,0:T(8,128)(2,1)S(1)}, bf16[2,4,128,128]{3,2,1,0:T(8,128)(2,1)S(1)}, u32[]{:S(2)}, u32[]{:S(2)}) collective-permute-start(bf16[2,4,128,128]{3,2,1,0:T(8,128)(2,1)S(1)} %collective-permute-done.7), channel_id=1, source_target_pairs={{0,64},{16,80},{32,96},{48,112},{64,128},{80,144},{96,160},{112,17... | collective-permute-start | bytes 786440 | tf_op jit(solution)/shard_map/ppermute | solution.py:195
  128.9 6.3 %collective-permute-done.9 = bf16[2,4,128,128]{3,2,1,0:T(8,128)(2,1)S(1)} collective-permute-done((bf16[2,4,128,128]{3,2,1,0:T(8,128)(2,1)S(1)}, bf16[2,4,128,128]{3,2,1,0:T(8,128)(2,1)S(1)}, u32[]{:S(2)}, u32[]{:S(2)}) %collective-permute-start.9) | collective-permute-done | bytes 262176 | tf_op jit(solution)/shard_map/ppermute | solution.py:195
  136.7 6.4 %hidden_grad.1 = (f32[128,768]{1,0:T(8,128)}, f32[128,768]{1,0:T(8,128)}) custom-call(s32[128]{0:T(128)} %get-tuple-element.9.table_ref, s32[2]{0:T(128)} %pad_add_fusion.core_ref, bf16[256,8192]{1,0:T(8,128)(2,1)} %bitcast.27, bf16[16,4,128,128]{3,2,1,0:T(8,128)(2,1)} %bitcast.28), custom_call_target="tpu_custom_call" | custom-call | flops 536870912 | bytes 6291456 | tf_op jit(solution)/shard_map/hidden_grad/pallas_call | solution.py:303
  143.1 7.1 %collective-permute-start.10 = (f32[128,768]{1,0:T(8,128)}, f32[128,768]{1,0:T(8,128)S(1)}, u32[]{:S(2)}, u32[]{:S(2)}) collective-permute-start(f32[128,768]{1,0:T(8,128)} %get-tuple-element.11), channel_id=1, source_target_pairs={{0,16},{16,0},{32,48},{48,32},{64,80},{80,64},{96,112},{112,96},{1... | collective-permute-start | bytes 1179656 | tf_op jit(solution)/shard_map/ppermute | solution.py:195
  151.1 4.5 %collective-permute-start.12 = (bf16[4,128,128]{2,1,0:T(8,128)(2,1)S(1)}, bf16[4,128,128]{2,1,0:T(8,128)(2,1)S(1)}, u32[]{:S(2)}, u32[]{:S(2)}) collective-permute-start(bf16[4,128,128]{2,1,0:T(8,128)(2,1)S(1)} %slice_bitcast_fusion), channel_id=1, source_target_pairs={{0,32},{16,48},{32,0},{48,16},{64,96},{80,112},{96,64},{112,80},{1... | collective-permute-start | bytes 393224 | tf_op jit(solution)/shard_map/ppermute | solution.py:195
  157.5 2.0 %collective-permute-done.12.other_ref = bf16[4,128,128]{2,1,0:T(8,128)(2,1)S(1)} collective-permute-done((bf16[4,128,128]{2,1,0:T(8,128)(2,1)S(1)}, bf16[4,128,128]{2,1,0:T(8,128)(2,1)S(1)}, u32[]{:S(2)}, u32[]{:S(2)}) %collective-permute-start.12) | collective-permute-done | bytes 131104 | tf_op jit(solution)/shard_map/ppermute | solution.py:195
  (47 shorter events, 15.9 us)
Async XLA Ops:
  7.2 63.0 %all-gather.2.cloned.1.call-start = ((), (), s32[]{:S(2)}) async-start(), calls=%async_computation.1 | async-start | bytes 4456448 | tf_op jit(solution)/shard_map/all_gather | solution.py:252
  7.2 6.5 %collective-permute-start = (s32[1]{0:T(128)}, s32[1]{0:T(128)}, u32[]{:S(2)}, u32[]{:S(2)}) collective-permute-start(s32[1]{0:T(128)} %param.7), channel_id=1, source_target_pairs={{0,8},{1,9},{2,10},{3,11},{4,12},{5,13},{6,14},{7,15},{8,0},{9,1},... | collective-permute-start | bytes 20 | tf_op jit(solution)/shard_map/ppermute | solution.py:198
  11.2 5.9 %collective-permute-start.1 = (bf16[8,8192]{1,0:T(8,128)(2,1)}, bf16[8,8192]{1,0:T(8,128)(2,1)S(1)}, u32[]{:S(2)}, u32[]{:S(2)}) collective-permute-start(bf16[8,8192]{1,0:T(8,128)(2,1)} %param.6), channel_id=1, source_target_pairs={{0,8},{1,9},{2,10},{3,11},{4,12},{5,13},{6,14},{7,15},{8,0},{9,1},... | collective-permute-start | bytes 393224 | tf_op jit(solution)/shard_map/ppermute | solution.py:198
  18.8 131.3 %reduce-scatter.2.cloned.1.call-start = ((), (), s32[]{:S(2)}) async-start(), calls=%async_computation.2 | async-start | bytes 2359296 | tf_op jit(solution)/shard_map/reduce_scatter | solution.py:293
  21.3 9.1 %collective-permute-start.11 = (bf16[768,128]{1,0:T(8,128)(2,1)}, bf16[768,128]{1,0:T(8,128)(2,1)S(1)}, u32[]{:S(2)}, u32[]{:S(2)}) collective-permute-start(bf16[768,128]{1,0:T(8,128)(2,1)} %get-tuple-element.14), channel_id=1, source_target_pairs={{0,16},{16,0},{32,48},{48,32},{64,80},{80,64},{96,112},{112,96},{1... | collective-permute-start | bytes 589832 | tf_op jit(solution)/shard_map/ppermute | solution.py:195
  76.8 16.6 %copy-start.6 = (bf16[4,128,128]{2,1,0:T(8,128)(2,1)S(1)}, bf16[4,128,128]{2,1,0:T(8,128)(2,1)}, u32[]{:S(2)}) copy-start(bf16[4,128,128]{2,1,0:T(8,128)(2,1)} %pack.1) | copy-start | bytes 393220
  76.8 8.5 %collective-permute-start.2 = (bf16[4,128,128]{2,1,0:T(8,128)(2,1)}, bf16[4,128,128]{2,1,0:T(8,128)(2,1)S(1)}, u32[]{:S(2)}, u32[]{:S(2)}) collective-permute-start(bf16[4,128,128]{2,1,0:T(8,128)(2,1)} %pack.1), channel_id=1, source_target_pairs={{0,32},{16,48},{32,0},{48,16},{64,96},{80,112},{96,64},{112,80},{1... | collective-permute-start | bytes 393224 | tf_op jit(solution)/shard_map/ppermute | solution.py:195
  86.3 16.6 %collective-permute-start.3 = (bf16[2,4,128,128]{3,2,1,0:T(8,128)(2,1)S(1)}, bf16[2,4,128,128]{3,2,1,0:T(8,128)(2,1)S(1)}, u32[]{:S(2)}, u32[]{:S(2)}) collective-permute-start(bf16[2,4,128,128]{3,2,1,0:T(8,128)(2,1)S(1)} %broadcast_select_fusion.1), channel_id=1, source_target_pairs={{0,64},{16,80},{32,96},{48,112},{64,128},{80,144},{96,160},{112,17... | collective-permute-start | bytes 786440 | tf_op jit(solution)/shard_map/ppermute | solution.py:195
  89.4 15.4 %collective-permute-start.4 = (bf16[2,4,128,128]{3,2,1,0:T(8,128)(2,1)S(1)}, bf16[2,4,128,128]{3,2,1,0:T(8,128)(2,1)S(1)}, u32[]{:S(2)}, u32[]{:S(2)}) collective-permute-start(bf16[2,4,128,128]{3,2,1,0:T(8,128)(2,1)S(1)} %broadcast_select_fusion.1), channel_id=1, source_target_pairs={{0,448},{16,464},{32,480},{48,496},{64,0},{80,16},{96,32},{112,48}... | collective-permute-start | bytes 786440 | tf_op jit(solution)/shard_map/ppermute | solution.py:195
  102.9 15.7 %collective-permute-start.5 = (bf16[2,4,128,128]{3,2,1,0:T(8,128)(2,1)S(1)}, bf16[2,4,128,128]{3,2,1,0:T(8,128)(2,1)S(1)}, u32[]{:S(2)}, u32[]{:S(2)}) collective-permute-start(bf16[2,4,128,128]{3,2,1,0:T(8,128)(2,1)S(1)} %collective-permute-done.3), channel_id=1, source_target_pairs={{0,64},{16,80},{32,96},{48,112},{64,128},{80,144},{96,160},{112,17... | collective-permute-start | bytes 786440 | tf_op jit(solution)/shard_map/ppermute | solution.py:195
  104.8 15.7 %collective-permute-start.6 = (bf16[2,4,128,128]{3,2,1,0:T(8,128)(2,1)S(1)}, bf16[2,4,128,128]{3,2,1,0:T(8,128)(2,1)S(1)}, u32[]{:S(2)}, u32[]{:S(2)}) collective-permute-start(bf16[2,4,128,128]{3,2,1,0:T(8,128)(2,1)S(1)} %collective-permute-done.4), channel_id=1, source_target_pairs={{0,448},{16,464},{32,480},{48,496},{64,0},{80,16},{96,32},{112,48}... | collective-permute-start | bytes 786440 | tf_op jit(solution)/shard_map/ppermute | solution.py:195
  118.6 8.3 %collective-permute-start.7 = (bf16[2,4,128,128]{3,2,1,0:T(8,128)(2,1)S(1)}, bf16[2,4,128,128]{3,2,1,0:T(8,128)(2,1)S(1)}, u32[]{:S(2)}, u32[]{:S(2)}) collective-permute-start(bf16[2,4,128,128]{3,2,1,0:T(8,128)(2,1)S(1)} %collective-permute-done.5), channel_id=1, source_target_pairs={{0,64},{16,80},{32,96},{48,112},{64,128},{80,144},{96,160},{112,17... | collective-permute-start | bytes 786440 | tf_op jit(solution)/shard_map/ppermute | solution.py:195
  120.5 8.4 %collective-permute-start.8 = (bf16[2,4,128,128]{3,2,1,0:T(8,128)(2,1)S(1)}, bf16[2,4,128,128]{3,2,1,0:T(8,128)(2,1)S(1)}, u32[]{:S(2)}, u32[]{:S(2)}) collective-permute-start(bf16[2,4,128,128]{3,2,1,0:T(8,128)(2,1)S(1)} %collective-permute-done.6), channel_id=1, source_target_pairs={{0,448},{16,464},{32,480},{48,496},{64,0},{80,16},{96,32},{112,48}... | collective-permute-start | bytes 786440 | tf_op jit(solution)/shard_map/ppermute | solution.py:195
  126.9 8.3 %collective-permute-start.9 = (bf16[2,4,128,128]{3,2,1,0:T(8,128)(2,1)S(1)}, bf16[2,4,128,128]{3,2,1,0:T(8,128)(2,1)S(1)}, u32[]{:S(2)}, u32[]{:S(2)}) collective-permute-start(bf16[2,4,128,128]{3,2,1,0:T(8,128)(2,1)S(1)} %collective-permute-done.7), channel_id=1, source_target_pairs={{0,64},{16,80},{32,96},{48,112},{64,128},{80,144},{96,160},{112,17... | collective-permute-start | bytes 786440 | tf_op jit(solution)/shard_map/ppermute | solution.py:195
  135.2 1.4 copy-start.5
  136.6 18.9 %copy-start = (bf16[128,768]{1,0:T(8,128)(2,1)S(1)}, bf16[128,768]{1,0:T(8,128)(2,1)}, u32[]{:S(2)}) copy-start(bf16[128,768]{1,0:T(8,128)(2,1)} %gate_ref.3) | copy-start | bytes 589828
  136.6 19.0 %copy-start.1 = (bf16[128,768]{1,0:T(8,128)(2,1)S(1)}, bf16[128,768]{1,0:T(8,128)(2,1)}, u32[]{:S(2)}) copy-start(bf16[128,768]{1,0:T(8,128)(2,1)} %up_ref.3) | copy-start | bytes 589828
  136.7 22.9 %copy-start.4 = (s32[6,64]{1,0:T(8,128)S(1)}, s32[6,64]{1,0:T(8,128)}, u32[]{:S(2)}) copy-start(s32[6,64]{1,0:T(8,128)} %mask_ref.5) | copy-start | bytes 4612
  143.1 12.5 %collective-permute-start.10 = (f32[128,768]{1,0:T(8,128)}, f32[128,768]{1,0:T(8,128)S(1)}, u32[]{:S(2)}, u32[]{:S(2)}) collective-permute-start(f32[128,768]{1,0:T(8,128)} %get-tuple-element.11), channel_id=1, source_target_pairs={{0,16},{16,0},{32,48},{48,32},{64,80},{80,64},{96,112},{112,96},{1... | collective-permute-start | bytes 1179656 | tf_op jit(solution)/shard_map/ppermute | solution.py:195
  151.1 8.4 %collective-permute-start.12 = (bf16[4,128,128]{2,1,0:T(8,128)(2,1)S(1)}, bf16[4,128,128]{2,1,0:T(8,128)(2,1)S(1)}, u32[]{:S(2)}, u32[]{:S(2)}) collective-permute-start(bf16[4,128,128]{2,1,0:T(8,128)(2,1)S(1)} %slice_bitcast_fusion), channel_id=1, source_target_pairs={{0,32},{16,48},{32,0},{48,16},{64,96},{80,112},{96,64},{112,80},{1... | collective-permute-start | bytes 393224 | tf_op jit(solution)/shard_map/ppermute | solution.py:195
  155.6 1.0 copy-start.3
  159.5 1.0 copy-start.2
Sparse Core Ops, SparseCore 0:
  18.9 51.1 all-gather.1
  75.1 47.4 reduce-scatter.1

commit v4 on v3

--- a/solution.py
+++ b/solution.py
@@ -66,7 +66,18 @@
     gate = gate_ref[...].astype(jnp.float32)
     up = up_ref[...].astype(jnp.float32)
     hidden = gate * jax.nn.sigmoid(gate) * up
-    hidden_ref[...] = by_ring(hidden).T.astype(jnp.bfloat16)
+    hidden_ref[...] = by_ring(hidden).astype(jnp.bfloat16)
+
+
+def join_kernel(core_ref, own_ref, other_ref, out_ref):
+    rows, _ = own_ref.shape
+    first = core_ref[0] == 0
+    pieces = []
+    for at in range(0, rows, 2 * TOK):
+        own = own_ref[at : at + 2 * TOK, :].astype(jnp.float32)
+        other = other_ref[at : at + 2 * TOK, :].astype(jnp.float32)
+        pieces += [jnp.where(first, own, other), jnp.where(first, other, own)]
+    out_ref[...] = jnp.concatenate(pieces, axis=0).T.astype(jnp.bfloat16)
 
 
 def partial_kernel(table_ref, core_ref, hidden_ref, panel_ref, out_ref):
@@ -81,13 +92,7 @@
             right = panel_ref[:, pl.ds(at, wide)]
             places = [table_ref[s * TAB + k] for k in range(CAP)]
             rows = [pl.multiple_of((b >> 1) * BLK, BLK) for b in places]
-            left = jnp.concatenate(
-                [
-                    jnp.concatenate([hidden_ref[c, pl.ds(r, BLK), :] for c in range(2)], axis=1)
-                    for r in rows
-                ],
-                axis=0,
-            )
+            left = jnp.concatenate([hidden_ref[pl.ds(r, BLK), :] for r in rows], axis=0)
             term = jnp.dot(left, right, preferred_element_type=jnp.float32)
             for k, b in enumerate(places):
                 tile = term[k * BLK : (k + 1) * BLK]
@@ -131,13 +136,16 @@
         for k, b in enumerate(places):
             r = pl.multiple_of((b >> 1) * BLK, BLK)
             part = term[:, k * BLK : (k + 1) * BLK]
-            sum_ref[0, :, pl.ds(r, BLK)] += part[:rows]
-            sum_ref[1, :, pl.ds(r, BLK)] += part[rows:]
+            sum_ref[:, pl.ds(r, BLK)] += part
 
     @pl.when(group == pl.num_programs(0) - 1)
     def _():
-        own_ref[...] = sum_ref[core_ref[0]]
-        other_ref[...] = sum_ref[1 - core_ref[0]]
+        first = core_ref[0] == 0
+        for at in range(0, rows, 2 * TOK):
+            a = sum_ref[2 * at : 2 * at + 2 * TOK, :]
+            b = sum_ref[2 * at + 2 * TOK : 2 * at + 4 * TOK, :]
+            own_ref[at : at + 2 * TOK, :] = jnp.where(first, a, b)
+            other_ref[at : at + 2 * TOK, :] = jnp.where(first, b, a)
 
 
 def gates_kernel(own_ref, other_ref, gate_ref, up_ref, d_gate_ref, d_up_ref):
@@ -159,7 +167,7 @@
 
             @pl.when(kept == 1)
             def _(r=r, c=c, count=count):
-                total = own_ref[0, count].astype(jnp.float32) + other_ref[count].astype(
+                total = own_ref[count] + other_ref[count].astype(
                     jnp.float32
                 )
                 out_ref[r * BLK : (r + 1) * BLK, c * BLK : (c + 1) * BLK] = (
@@ -222,30 +230,32 @@
     packed_other = swap_xh(packed)
 
     shard_count = fsdp_count // 2
-    table, hidden_t = pl.pallas_call(
+    table, hidden = pl.pallas_call(
         table_kernel,
-        out_shape=(shape((shard_count * TAB,), jnp.int32), shape((units, rows))),
+        out_shape=(shape((shard_count * TAB,), jnp.int32), shape((rows, units))),
         in_specs=[SMEM, SMEM, VMEM, VMEM],
         out_specs=(SMEM, VMEM),
         name="hidden",
         cost_estimate=cost(1000, 1 << 20),
     )(f_arr, tile_mask, gate_pre, up_pre)
-    hidden_other = swap_core(hidden_t)
+    hidden_other = swap_core(hidden)
 
     def pair(own, other, index):
         first = (jnp.arange(2) == index).reshape((2,) + (1,) * own.ndim)
         return jnp.where(first, own[None], other[None])
 
-    live = pair(live_rows, live_other, xl).reshape(2, 1, 1)
+    block = (2, tok, width)
+    mine = lax.broadcasted_iota(jnp.int32, block, 0) == xl
+    limit = jnp.where(mine, live_rows[0], live_other[0])
     masked = jnp.where(
-        jnp.arange(tok)[None, :, None] < live,
-        pair(out_grad, grad_other, xl),
+        lax.broadcasted_iota(jnp.int32, block, 1) < limit,
+        jnp.where(mine, out_grad[None], grad_other[None]),
         jnp.zeros((), jnp.bfloat16),
     )
 
     columns = [[k + 4 * i for i in range(ring_y)] for k in range(4)]
     chips = [
-        [(2 * i + c) * tensor_count + half * ring_z + j for c in range(2) for j in range(ring_z)]
+        [(2 * i + c) * tensor_count + half * ring_z + j for j in range(ring_z) for c in range(2)]
         for i in range(fsdp_count // 2)
         for half in range(2)
     ]
@@ -255,7 +265,15 @@
         axis_index_groups=chips,
         tiled=True,
     ).reshape(2 * rows, width)
-    hidden_pair = pair(hidden_t, hidden_other, f & 1)
+    core_arr = jnp.stack([f & 1, xh]).astype(jnp.int32)
+    hidden_pair = pl.pallas_call(
+        join_kernel,
+        out_shape=shape((units, 2 * rows)),
+        in_specs=[SMEM, VMEM, VMEM],
+        out_specs=VMEM,
+        name="join",
+        cost_estimate=cost(1000, 1 << 20),
+    )(core_arr, hidden, hidden_other)
 
     weights = jnp.zeros((ring_y, 2, CAP, BLK, BLK), jnp.bfloat16)
 
@@ -271,11 +289,10 @@
             down = y_step(down, -1)
             weights = put(weights, down, y + d)
     weights = weights.reshape(shard_count, CAP, BLK, BLK)
-    core_arr = jnp.stack([f & 1, xh]).astype(jnp.int32)
     per_step = ring_y // 2
 
     panel_spec = pl.BlockSpec((2 * rows, width // ring_y * per_step), lambda i, tab, cr: (0, i))
-    whole = pl.BlockSpec((2, units, rows), lambda i, tab, cr: (0, 0, 0))
+    whole = pl.BlockSpec((units, 2 * rows), lambda i, tab, cr: (0, 0))
     tiles = pl.pallas_call(
         partial_kernel,
         out_shape=shape((ring_y, 2, CAP, BLK, BLK)),
@@ -293,7 +310,7 @@
     sums = lax.psum_scatter(
         tiles, "fsdp", scatter_dimension=0, axis_index_groups=columns, tiled=True
     )[0]
-    send_sum = sums[1]
+    own_sum, send_sum = sums[0].astype(jnp.float32), sums[1]
     other_sum = swap_xh(send_sum)
 
     groups = 4
@@ -311,7 +328,7 @@
                 pl.BlockSpec((per_group, CAP, BLK, BLK), lambda i, tab, cr: (i, 0, 0, 0)),
             ],
             out_specs=(acc_spec, acc_spec),
-            scratch_shapes=[pltpu.VMEM((2, rows, units), jnp.float32)],
+            scratch_shapes=[pltpu.VMEM((2 * rows, units), jnp.float32)],
         ),
         name="hidden_grad",
         cost_estimate=cost(shard_count * CAP * 4 * rows * BLK * BLK, 6 << 20),
@@ -334,7 +351,7 @@
         name="place",
         compiler_params=pltpu.CompilerParams(vmem_limit_bytes=16 << 20),
         cost_estimate=cost(1000, 1 << 20),
-    )(f_arr, tile_mask, sums, other_sum)
+    )(f_arr, tile_mask, own_sum, other_sum)
     return (d_gate, d_up, d_weight)
 
 

time: 170 us -> 169 us (level)
  Pallas kernels: 17.9 us -> 19.8 us
    select_n x3 -> x1, other arithmetic: 3.34 us -> 0.99 us  [pair(): return jnp.where(first, own[None], other[None])]
    pallas_call x0 -> x1, Pallas kernels: none -> 1.95 us  [per_device(): pl.pallas_call(join_kernel, out_shape=shape((units, 2 * rows)), in_specs=...]
  transfers between devices with their start and end apart: 15 -> 15, of which waited for: 9 -> 9; matrix products, arithmetic and copies ran while one was open for 4% -> 3% of each run, Pallas kernels for 7% -> 8%
where the time goes in v4:
time: 169 us; the launch traced here: 168 us
  waiting for transfers between devices  72.7 us (43%)
  starting transfers between devices  51.5 us (30%)
  Pallas kernels  19.8 us (12%)
  between operations  15 us (9%)
  other arithmetic  5.2 us (3%)
  local copies, waits for them, and re-layouts  3.84 us (2%)
    ppermute x11, starting transfers between devices, over_f(): return lax.ppermute(x, 'fsdp', [(i, move(i)) for i in range(fsdp_count)])  45.6 us
    all_gather x1, waiting for transfers between devices, per_device(): lax.all_gather(masked, ('fsdp', 'tensor'), axis_index_groups=chips, tiled...  37.1 us
    ppermute x11, waiting for transfers between devices, over_f(): return lax.ppermute(x, 'fsdp', [(i, move(i)) for i in range(fsdp_count)])  32.8 us
    pallas_call x1, Pallas kernels, per_device(): pl.pallas_call(hidden_grad_kernel, out_shape=(shape((rows, units), jnp.fl...  6.4 us
    ppermute x2, starting transfers between devices, over_t(): lax.ppermute(x, 'tensor', [(i, move(i)) for i in range(tensor_count)])  5.86 us
    pallas_call x1, Pallas kernels, per_device(): pl.pallas_call(partial_kernel, out_shape=shape((ring_y, 2, CAP, BLK, BLK)...  4.78 us
  transfers between devices with their start and end apart: 15, of which 9 were waited for; matrix products, arithmetic and copies ran while one was open for 3% of the time, Pallas kernels for 8%

profile of v4, /device:TPU:1, one launch (start us, length us, event | category | flops | bytes accessed | tf_op | source)
XLA Modules:
  0.0 168.0 jit_solution(7859954218934082729)
XLA Ops:
  7.2 3.9 %collective-permute-start = (s32[1]{0:T(128)}, s32[1]{0:T(128)}, u32[]{:S(2)}, u32[]{:S(2)}) collective-permute-start(s32[1]{0:T(128)} %param.7), channel_id=1, source_target_pairs={{0,8},{1,9},{2,10},{3,11},{4,12},{5,13},{6,14},{7,15},{8,0},{9,1},... | collective-permute-start | bytes 20 | tf_op jit(solution)/shard_map/ppermute | solution.py:206
  11.2 1.9 %collective-permute-start.1 = (bf16[8,8192]{1,0:T(8,128)(2,1)}, bf16[8,8192]{1,0:T(8,128)(2,1)S(1)}, u32[]{:S(2)}, u32[]{:S(2)}) collective-permute-start(bf16[8,8192]{1,0:T(8,128)(2,1)} %param.6), channel_id=1, source_target_pairs={{0,8},{1,9},{2,10},{3,11},{4,12},{5,13},{6,14},{7,15},{8,0},{9,1},... | collective-permute-start | bytes 393224 | tf_op jit(solution)/shard_map/ppermute | solution.py:206
  14.4 2.6 %collective-permute-done.1 = bf16[8,8192]{1,0:T(8,128)(2,1)S(1)} collective-permute-done((bf16[8,8192]{1,0:T(8,128)(2,1)}, bf16[8,8192]{1,0:T(8,128)(2,1)S(1)}, u32[]{:S(2)}, u32[]{:S(2)}) %collective-permute-start.1) | collective-permute-done | bytes 131104 | tf_op jit(solution)/shard_map/ppermute | solution.py:206
  18.9 2.3 %hidden.1 = (s32[128]{0:T(128)}, bf16[128,768]{1,0:T(8,128)(2,1)}) custom-call(s32[1]{0:T(128)} %bitcast.f_ref, s32[6,64]{1,0:T(8,128)} %mask_ref.5, bf16[128,768]{1,0:T(8,128)(2,1)} %gate_ref.3, bf16[128,768]{1,0:T(8,128)(2,1)} %up_ref.3), custom_call_target="tpu_custom_call" | custom-call | flops 1000 | bytes 1048576 | tf_op jit(solution)/shard_map/hidden/pallas_call | solution.py:233
  21.3 7.9 %collective-permute-start.11 = (bf16[128,768]{1,0:T(8,128)(2,1)}, bf16[128,768]{1,0:T(8,128)(2,1)S(1)}, u32[]{:S(2)}, u32[]{:S(2)}) collective-permute-start(bf16[128,768]{1,0:T(8,128)(2,1)} %get-tuple-element.14.own_ref), channel_id=1, source_target_pairs={{0,16},{16,0},{32,48},{48,32},{64,80},{80,64},{96,112},{112,96},{1... | collective-permute-start | bytes 589832 | tf_op jit(solution)/shard_map/ppermute | solution.py:203
  31.1 2.0 %join.1.hidden_ref = bf16[768,256]{1,0:T(8,128)(2,1)} custom-call(s32[2]{0:T(128)} %pad_add_fusion.core_ref, bf16[128,768]{1,0:T(8,128)(2,1)} %get-tuple-element.14.own_ref, bf16[128,768]{1,0:T(8,128)(2,1)} %copy-done.6), custom_call_target="tpu_custom_call" | custom-call | flops 1000 | bytes 1048576 | tf_op jit(solution)/shard_map/join/pallas_call | solution.py:269
  33.1 37.1 %all-gather.2.cloned.1.call-done = bf16[32,8,8192]{2,1,0:T(8,128)(2,1)} async-done(((bf16[2,8,8192]{2,1,0:T(8,128)(2,1)}), bf16[32,8,8192]{2,1,0:T(8,128)(2,1)}) %all-gather.2.cloned.1.call-update) | async-done | bytes 4194320 | tf_op jit(solution)/shard_map/all_gather | solution.py:262
  70.2 4.8 %partial.1 = bf16[8,2,4,128,128]{4,3,2,1,0:T(8,128)(2,1)} custom-call(s32[128]{0:T(128)} %get-tuple-element.9.table_ref, s32[2]{0:T(128)} %pad_add_fusion.core_ref, bf16[768,256]{1,0:T(8,128)(2,1)} %join.1.hidden_ref, bf16[256,8192]{1,0:T(8,128)(2,1)} %bitcast.29), custom_call_target="tpu_custom_call" | custom-call | flops 536870912 | bytes 4194304 | tf_op jit(solution)/shard_map/partial/pallas_call | solution.py:296
  76.9 4.7 %collective-permute-start.2 = (bf16[4,128,128]{2,1,0:T(8,128)(2,1)}, bf16[4,128,128]{2,1,0:T(8,128)(2,1)S(1)}, u32[]{:S(2)}, u32[]{:S(2)}) collective-permute-start(bf16[4,128,128]{2,1,0:T(8,128)(2,1)} %pack.1), channel_id=1, source_target_pairs={{0,32},{16,48},{32,0},{48,16},{64,96},{80,112},{96,64},{112,80},{1... | collective-permute-start | bytes 393224 | tf_op jit(solution)/shard_map/ppermute | solution.py:203
  81.6 3.7 %collective-permute-done.2 = bf16[4,128,128]{2,1,0:T(8,128)(2,1)S(1)} collective-permute-done((bf16[4,128,128]{2,1,0:T(8,128)(2,1)}, bf16[4,128,128]{2,1,0:T(8,128)(2,1)S(1)}, u32[]{:S(2)}, u32[]{:S(2)}) %collective-permute-start.2) | collective-permute-done | bytes 131104 | tf_op jit(solution)/shard_map/ppermute | solution.py:203
  86.4 3.1 %collective-permute-start.3 = (bf16[2,4,128,128]{3,2,1,0:T(8,128)(2,1)S(1)}, bf16[2,4,128,128]{3,2,1,0:T(8,128)(2,1)S(1)}, u32[]{:S(2)}, u32[]{:S(2)}) collective-permute-start(bf16[2,4,128,128]{3,2,1,0:T(8,128)(2,1)S(1)} %broadcast_select_fusion), channel_id=1, source_target_pairs={{0,64},{16,80},{32,96},{48,112},{64,128},{80,144},{96,160},{112,17... | collective-permute-start | bytes 786440 | tf_op jit(solution)/shard_map/ppermute | solution.py:203
  89.5 3.4 %collective-permute-start.4 = (bf16[2,4,128,128]{3,2,1,0:T(8,128)(2,1)S(1)}, bf16[2,4,128,128]{3,2,1,0:T(8,128)(2,1)S(1)}, u32[]{:S(2)}, u32[]{:S(2)}) collective-permute-start(bf16[2,4,128,128]{3,2,1,0:T(8,128)(2,1)S(1)} %broadcast_select_fusion), channel_id=1, source_target_pairs={{0,448},{16,464},{32,480},{48,496},{64,0},{80,16},{96,32},{112,48}... | collective-permute-start | bytes 786440 | tf_op jit(solution)/shard_map/ppermute | solution.py:203
  93.6 9.4 %collective-permute-done.3 = bf16[2,4,128,128]{3,2,1,0:T(8,128)(2,1)S(1)} collective-permute-done((bf16[2,4,128,128]{3,2,1,0:T(8,128)(2,1)S(1)}, bf16[2,4,128,128]{3,2,1,0:T(8,128)(2,1)S(1)}, u32[]{:S(2)}, u32[]{:S(2)}) %collective-permute-start.3) | collective-permute-done | bytes 262176 | tf_op jit(solution)/shard_map/ppermute | solution.py:203
  102.9 1.9 %collective-permute-start.5 = (bf16[2,4,128,128]{3,2,1,0:T(8,128)(2,1)S(1)}, bf16[2,4,128,128]{3,2,1,0:T(8,128)(2,1)S(1)}, u32[]{:S(2)}, u32[]{:S(2)}) collective-permute-start(bf16[2,4,128,128]{3,2,1,0:T(8,128)(2,1)S(1)} %collective-permute-done.3), channel_id=1, source_target_pairs={{0,64},{16,80},{32,96},{48,112},{64,128},{80,144},{96,160},{112,17... | collective-permute-start | bytes 786440 | tf_op jit(solution)/shard_map/ppermute | solution.py:203
  104.9 4.6 %collective-permute-start.6 = (bf16[2,4,128,128]{3,2,1,0:T(8,128)(2,1)S(1)}, bf16[2,4,128,128]{3,2,1,0:T(8,128)(2,1)S(1)}, u32[]{:S(2)}, u32[]{:S(2)}) collective-permute-start(bf16[2,4,128,128]{3,2,1,0:T(8,128)(2,1)S(1)} %collective-permute-done.4), channel_id=1, source_target_pairs={{0,448},{16,464},{32,480},{48,496},{64,0},{80,16},{96,32},{112,48}... | collective-permute-start | bytes 786440 | tf_op jit(solution)/shard_map/ppermute | solution.py:203
  109.6 9.1 %collective-permute-done.5 = bf16[2,4,128,128]{3,2,1,0:T(8,128)(2,1)S(1)} collective-permute-done((bf16[2,4,128,128]{3,2,1,0:T(8,128)(2,1)S(1)}, bf16[2,4,128,128]{3,2,1,0:T(8,128)(2,1)S(1)}, u32[]{:S(2)}, u32[]{:S(2)}) %collective-permute-start.5) | collective-permute-done | bytes 262176 | tf_op jit(solution)/shard_map/ppermute | solution.py:203
  118.6 1.9 %collective-permute-start.7 = (bf16[2,4,128,128]{3,2,1,0:T(8,128)(2,1)S(1)}, bf16[2,4,128,128]{3,2,1,0:T(8,128)(2,1)S(1)}, u32[]{:S(2)}, u32[]{:S(2)}) collective-permute-start(bf16[2,4,128,128]{3,2,1,0:T(8,128)(2,1)S(1)} %collective-permute-done.5), channel_id=1, source_target_pairs={{0,64},{16,80},{32,96},{48,112},{64,128},{80,144},{96,160},{112,17... | collective-permute-start | bytes 786440 | tf_op jit(solution)/shard_map/ppermute | solution.py:203
  120.5 4.6 %collective-permute-start.8 = (bf16[2,4,128,128]{3,2,1,0:T(8,128)(2,1)S(1)}, bf16[2,4,128,128]{3,2,1,0:T(8,128)(2,1)S(1)}, u32[]{:S(2)}, u32[]{:S(2)}) collective-permute-start(bf16[2,4,128,128]{3,2,1,0:T(8,128)(2,1)S(1)} %collective-permute-done.6), channel_id=1, source_target_pairs={{0,448},{16,464},{32,480},{48,496},{64,0},{80,16},{96,32},{112,48}... | collective-permute-start | bytes 786440 | tf_op jit(solution)/shard_map/ppermute | solution.py:203
  126.9 1.9 %collective-permute-start.9 = (bf16[2,4,128,128]{3,2,1,0:T(8,128)(2,1)S(1)}, bf16[2,4,128,128]{3,2,1,0:T(8,128)(2,1)S(1)}, u32[]{:S(2)}, u32[]{:S(2)}) collective-permute-start(bf16[2,4,128,128]{3,2,1,0:T(8,128)(2,1)S(1)} %collective-permute-done.7), channel_id=1, source_target_pairs={{0,64},{16,80},{32,96},{48,112},{64,128},{80,144},{96,160},{112,17... | collective-permute-start | bytes 786440 | tf_op jit(solution)/shard_map/ppermute | solution.py:203
  128.9 6.3 %collective-permute-done.9 = bf16[2,4,128,128]{3,2,1,0:T(8,128)(2,1)S(1)} collective-permute-done((bf16[2,4,128,128]{3,2,1,0:T(8,128)(2,1)S(1)}, bf16[2,4,128,128]{3,2,1,0:T(8,128)(2,1)S(1)}, u32[]{:S(2)}, u32[]{:S(2)}) %collective-permute-start.9) | collective-permute-done | bytes 262176 | tf_op jit(solution)/shard_map/ppermute | solution.py:203
  136.7 6.4 %hidden_grad.1 = (f32[128,768]{1,0:T(8,128)}, f32[128,768]{1,0:T(8,128)}) custom-call(s32[128]{0:T(128)} %get-tuple-element.9.table_ref, s32[2]{0:T(128)} %pad_add_fusion.core_ref, bf16[256,8192]{1,0:T(8,128)(2,1)} %bitcast.30, bf16[16,4,128,128]{3,2,1,0:T(8,128)(2,1)} %bitcast.31), custom_call_target="tpu_custom_call" | custom-call | flops 536870912 | bytes 6291456 | tf_op jit(solution)/shard_map/hidden_grad/pallas_call | solution.py:320
  143.1 7.1 %collective-permute-start.10 = (f32[128,768]{1,0:T(8,128)}, f32[128,768]{1,0:T(8,128)S(1)}, u32[]{:S(2)}, u32[]{:S(2)}) collective-permute-start(f32[128,768]{1,0:T(8,128)} %get-tuple-element.11), channel_id=1, source_target_pairs={{0,16},{16,0},{32,48},{48,32},{64,80},{80,64},{96,112},{112,96},{1... | collective-permute-start | bytes 1179656 | tf_op jit(solution)/shard_map/ppermute | solution.py:203
  151.2 4.5 %collective-permute-start.12 = (bf16[4,128,128]{2,1,0:T(8,128)(2,1)S(1)}, bf16[4,128,128]{2,1,0:T(8,128)(2,1)S(1)}, u32[]{:S(2)}, u32[]{:S(2)}) collective-permute-start(bf16[4,128,128]{2,1,0:T(8,128)(2,1)S(1)} %get-tuple-element.15), channel_id=1, source_target_pairs={{0,32},{16,48},{32,0},{48,16},{64,96},{80,112},{96,64},{112,80},{1... | collective-permute-start | bytes 393224 | tf_op jit(solution)/shard_map/ppermute | solution.py:203
  157.6 2.0 %collective-permute-done.12.other_ref = bf16[4,128,128]{2,1,0:T(8,128)(2,1)S(1)} collective-permute-done((bf16[4,128,128]{2,1,0:T(8,128)(2,1)S(1)}, bf16[4,128,128]{2,1,0:T(8,128)(2,1)S(1)}, u32[]{:S(2)}, u32[]{:S(2)}) %collective-permute-start.12) | collective-permute-done | bytes 131104 | tf_op jit(solution)/shard_map/ppermute | solution.py:203
  (45 shorter events, 15.9 us)
Async XLA Ops:
  7.2 63.0 %all-gather.2.cloned.1.call-start = ((), (), s32[]{:S(2)}) async-start(), calls=%async_computation.1 | async-start | bytes 4456448 | tf_op jit(solution)/shard_map/all_gather | solution.py:262
  7.2 6.5 %collective-permute-start = (s32[1]{0:T(128)}, s32[1]{0:T(128)}, u32[]{:S(2)}, u32[]{:S(2)}) collective-permute-start(s32[1]{0:T(128)} %param.7), channel_id=1, source_target_pairs={{0,8},{1,9},{2,10},{3,11},{4,12},{5,13},{6,14},{7,15},{8,0},{9,1},... | collective-permute-start | bytes 20 | tf_op jit(solution)/shard_map/ppermute | solution.py:206
  11.2 5.9 %collective-permute-start.1 = (bf16[8,8192]{1,0:T(8,128)(2,1)}, bf16[8,8192]{1,0:T(8,128)(2,1)S(1)}, u32[]{:S(2)}, u32[]{:S(2)}) collective-permute-start(bf16[8,8192]{1,0:T(8,128)(2,1)} %param.6), channel_id=1, source_target_pairs={{0,8},{1,9},{2,10},{3,11},{4,12},{5,13},{6,14},{7,15},{8,0},{9,1},... | collective-permute-start | bytes 393224 | tf_op jit(solution)/shard_map/ppermute | solution.py:206
  18.9 131.3 %reduce-scatter.2.cloned.1.call-start = ((), (), s32[]{:S(2)}) async-start(), calls=%async_computation.2 | async-start | bytes 2359296 | tf_op jit(solution)/shard_map/reduce_scatter | solution.py:310
  21.3 9.1 %collective-permute-start.11 = (bf16[128,768]{1,0:T(8,128)(2,1)}, bf16[128,768]{1,0:T(8,128)(2,1)S(1)}, u32[]{:S(2)}, u32[]{:S(2)}) collective-permute-start(bf16[128,768]{1,0:T(8,128)(2,1)} %get-tuple-element.14.own_ref), channel_id=1, source_target_pairs={{0,16},{16,0},{32,48},{48,32},{64,80},{80,64},{96,112},{112,96},{1... | collective-permute-start | bytes 589832 | tf_op jit(solution)/shard_map/ppermute | solution.py:203
  30.4 0.7 copy-start.6
  76.8 16.6 %copy-start.5 = (bf16[4,128,128]{2,1,0:T(8,128)(2,1)S(1)}, bf16[4,128,128]{2,1,0:T(8,128)(2,1)}, u32[]{:S(2)}) copy-start(bf16[4,128,128]{2,1,0:T(8,128)(2,1)} %pack.1) | copy-start | bytes 393220
  76.9 8.5 %collective-permute-start.2 = (bf16[4,128,128]{2,1,0:T(8,128)(2,1)}, bf16[4,128,128]{2,1,0:T(8,128)(2,1)S(1)}, u32[]{:S(2)}, u32[]{:S(2)}) collective-permute-start(bf16[4,128,128]{2,1,0:T(8,128)(2,1)} %pack.1), channel_id=1, source_target_pairs={{0,32},{16,48},{32,0},{48,16},{64,96},{80,112},{96,64},{112,80},{1... | collective-permute-start | bytes 393224 | tf_op jit(solution)/shard_map/ppermute | solution.py:203
  86.4 16.6 %collective-permute-start.3 = (bf16[2,4,128,128]{3,2,1,0:T(8,128)(2,1)S(1)}, bf16[2,4,128,128]{3,2,1,0:T(8,128)(2,1)S(1)}, u32[]{:S(2)}, u32[]{:S(2)}) collective-permute-start(bf16[2,4,128,128]{3,2,1,0:T(8,128)(2,1)S(1)} %broadcast_select_fusion), channel_id=1, source_target_pairs={{0,64},{16,80},{32,96},{48,112},{64,128},{80,144},{96,160},{112,17... | collective-permute-start | bytes 786440 | tf_op jit(solution)/shard_map/ppermute | solution.py:203
  89.5 15.4 %collective-permute-start.4 = (bf16[2,4,128,128]{3,2,1,0:T(8,128)(2,1)S(1)}, bf16[2,4,128,128]{3,2,1,0:T(8,128)(2,1)S(1)}, u32[]{:S(2)}, u32[]{:S(2)}) collective-permute-start(bf16[2,4,128,128]{3,2,1,0:T(8,128)(2,1)S(1)} %broadcast_select_fusion), channel_id=1, source_target_pairs={{0,448},{16,464},{32,480},{48,496},{64,0},{80,16},{96,32},{112,48}... | collective-permute-start | bytes 786440 | tf_op jit(solution)/shard_map/ppermute | solution.py:203
  102.9 15.7 %collective-permute-start.5 = (bf16[2,4,128,128]{3,2,1,0:T(8,128)(2,1)S(1)}, bf16[2,4,128,128]{3,2,1,0:T(8,128)(2,1)S(1)}, u32[]{:S(2)}, u32[]{:S(2)}) collective-permute-start(bf16[2,4,128,128]{3,2,1,0:T(8,128)(2,1)S(1)} %collective-permute-done.3), channel_id=1, source_target_pairs={{0,64},{16,80},{32,96},{48,112},{64,128},{80,144},{96,160},{112,17... | collective-permute-start | bytes 786440 | tf_op jit(solution)/shard_map/ppermute | solution.py:203
  104.9 15.6 %collective-permute-start.6 = (bf16[2,4,128,128]{3,2,1,0:T(8,128)(2,1)S(1)}, bf16[2,4,128,128]{3,2,1,0:T(8,128)(2,1)S(1)}, u32[]{:S(2)}, u32[]{:S(2)}) collective-permute-start(bf16[2,4,128,128]{3,2,1,0:T(8,128)(2,1)S(1)} %collective-permute-done.4), channel_id=1, source_target_pairs={{0,448},{16,464},{32,480},{48,496},{64,0},{80,16},{96,32},{112,48}... | collective-permute-start | bytes 786440 | tf_op jit(solution)/shard_map/ppermute | solution.py:203
  118.6 8.3 %collective-permute-start.7 = (bf16[2,4,128,128]{3,2,1,0:T(8,128)(2,1)S(1)}, bf16[2,4,128,128]{3,2,1,0:T(8,128)(2,1)S(1)}, u32[]{:S(2)}, u32[]{:S(2)}) collective-permute-start(bf16[2,4,128,128]{3,2,1,0:T(8,128)(2,1)S(1)} %collective-permute-done.5), channel_id=1, source_target_pairs={{0,64},{16,80},{32,96},{48,112},{64,128},{80,144},{96,160},{112,17... | collective-permute-start | bytes 786440 | tf_op jit(solution)/shard_map/ppermute | solution.py:203
  120.5 8.4 %collective-permute-start.8 = (bf16[2,4,128,128]{3,2,1,0:T(8,128)(2,1)S(1)}, bf16[2,4,128,128]{3,2,1,0:T(8,128)(2,1)S(1)}, u32[]{:S(2)}, u32[]{:S(2)}) collective-permute-start(bf16[2,4,128,128]{3,2,1,0:T(8,128)(2,1)S(1)} %collective-permute-done.6), channel_id=1, source_target_pairs={{0,448},{16,464},{32,480},{48,496},{64,0},{80,16},{96,32},{112,48}... | collective-permute-start | bytes 786440 | tf_op jit(solution)/shard_map/ppermute | solution.py:203
  126.9 8.3 %collective-permute-start.9 = (bf16[2,4,128,128]{3,2,1,0:T(8,128)(2,1)S(1)}, bf16[2,4,128,128]{3,2,1,0:T(8,128)(2,1)S(1)}, u32[]{:S(2)}, u32[]{:S(2)}) collective-permute-start(bf16[2,4,128,128]{3,2,1,0:T(8,128)(2,1)S(1)} %collective-permute-done.7), channel_id=1, source_target_pairs={{0,64},{16,80},{32,96},{48,112},{64,128},{80,144},{96,160},{112,17... | collective-permute-start | bytes 786440 | tf_op jit(solution)/shard_map/ppermute | solution.py:203
  135.3 1.4 copy-start.4
  136.7 19.0 %copy-start = (bf16[128,768]{1,0:T(8,128)(2,1)S(1)}, bf16[128,768]{1,0:T(8,128)(2,1)}, u32[]{:S(2)}) copy-start(bf16[128,768]{1,0:T(8,128)(2,1)} %gate_ref.3) | copy-start | bytes 589828
  136.7 19.0 %copy-start.1 = (bf16[128,768]{1,0:T(8,128)(2,1)S(1)}, bf16[128,768]{1,0:T(8,128)(2,1)}, u32[]{:S(2)}) copy-start(bf16[128,768]{1,0:T(8,128)(2,1)} %up_ref.3) | copy-start | bytes 589828
  136.7 22.9 %copy-start.3 = (s32[6,64]{1,0:T(8,128)S(1)}, s32[6,64]{1,0:T(8,128)}, u32[]{:S(2)}) copy-start(s32[6,64]{1,0:T(8,128)} %mask_ref.5) | copy-start | bytes 4612
  143.1 12.6 %collective-permute-start.10 = (f32[128,768]{1,0:T(8,128)}, f32[128,768]{1,0:T(8,128)S(1)}, u32[]{:S(2)}, u32[]{:S(2)}) collective-permute-start(f32[128,768]{1,0:T(8,128)} %get-tuple-element.11), channel_id=1, source_target_pairs={{0,16},{16,0},{32,48},{48,32},{64,80},{80,64},{96,112},{112,96},{1... | collective-permute-start | bytes 1179656 | tf_op jit(solution)/shard_map/ppermute | solution.py:203
  151.2 8.4 %collective-permute-start.12 = (bf16[4,128,128]{2,1,0:T(8,128)(2,1)S(1)}, bf16[4,128,128]{2,1,0:T(8,128)(2,1)S(1)}, u32[]{:S(2)}, u32[]{:S(2)}) collective-permute-start(bf16[4,128,128]{2,1,0:T(8,128)(2,1)S(1)} %get-tuple-element.15), channel_id=1, source_target_pairs={{0,32},{16,48},{32,0},{48,16},{64,96},{80,112},{96,64},{112,80},{1... | collective-permute-start | bytes 393224 | tf_op jit(solution)/shard_map/ppermute | solution.py:203
  155.7 1.0 copy-start.2
Sparse Core Ops, SparseCore 0:
  19.0 51.1 all-gather.1
  75.1 47.4 reduce-scatter.1

commit v5 on v4

--- a/solution.py
+++ b/solution.py
@@ -27,6 +27,16 @@
 def by_token(x):
     rows, width = x.shape
     return jnp.swapaxes(x.reshape(rows // (2 * TOK), 2, TOK, width), 0, 1).reshape(rows, width)
+
+
+def mask_kernel(xl_ref, live_ref, live_other_ref, own_ref, other_ref, out_ref):
+    rows = lax.broadcasted_iota(jnp.int32, own_ref.shape, 0)
+    for at, live, ref in (
+        (xl_ref[0], live_ref[0], own_ref),
+        (1 - xl_ref[0], live_other_ref[0], other_ref),
+    ):
+        value = ref[...].astype(jnp.float32)
+        out_ref[at] = jnp.where(rows < live, value, 0.0).astype(jnp.bfloat16)
 
 
 def pack_kernel(f_ref, mask_ref, weight_ref, packed_ref):
@@ -244,14 +254,15 @@
         first = (jnp.arange(2) == index).reshape((2,) + (1,) * own.ndim)
         return jnp.where(first, own[None], other[None])
 
-    block = (2, tok, width)
-    mine = lax.broadcasted_iota(jnp.int32, block, 0) == xl
-    limit = jnp.where(mine, live_rows[0], live_other[0])
-    masked = jnp.where(
-        lax.broadcasted_iota(jnp.int32, block, 1) < limit,
-        jnp.where(mine, out_grad[None], grad_other[None]),
-        jnp.zeros((), jnp.bfloat16),
-    )
+    masked = pl.pallas_call(
+        mask_kernel,
+        out_shape=shape((2, tok, width)),
+        in_specs=[SMEM, SMEM, SMEM, VMEM, VMEM],
+        out_specs=VMEM,
+        name="mask",
+        compiler_params=pltpu.CompilerParams(vmem_limit_bytes=16 << 20),
+        cost_estimate=cost(1000, 1 << 20),
+    )(xl.reshape(1).astype(jnp.int32), live_rows, live_other, out_grad, grad_other)
 
     columns = [[k + 4 * i for i in range(ring_y)] for k in range(4)]
     chips = [

time: 169 us -> 168 us (level)
  other arithmetic: 5.2 us -> 2.83 us
    select_n x2 -> x0, other arithmetic: 2.44 us -> none  [the longest x1 1.76 us: per_device(): jnp.where(lax.broadcasted_iota(jnp.int32, block, 1) < limit, jnp.where(mi...]
    unnamed x14 -> x16, local copies, waits for them, and re-layouts: 3.07 us -> 3.99 us
  transfers between devices with their start and end apart: 15 -> 15, of which waited for: 9 -> 9; matrix products, arithmetic and copies ran while one was open for 3% -> 2% of each run, Pallas kernels for 8% -> 8%
where the time goes in v5:
time: 168 us; the launch traced here: 167 us
  waiting for transfers between devices  71.9 us (43%)
  starting transfers between devices  51.3 us (31%)
  Pallas kernels  21.2 us (13%)
  between operations  15 us (9%)
  local copies, waits for them, and re-layouts  4.76 us (3%)
  other arithmetic  2.83 us (2%)
    ppermute x11, starting transfers between devices, over_f(): return lax.ppermute(x, 'fsdp', [(i, move(i)) for i in range(fsdp_count)])  45.4 us
    all_gather x1, waiting for transfers between devices, per_device(): lax.all_gather(masked, ('fsdp', 'tensor'), axis_index_groups=chips, tiled...  37.1 us
    ppermute x11, waiting for transfers between devices, over_f(): return lax.ppermute(x, 'fsdp', [(i, move(i)) for i in range(fsdp_count)])  32.7 us
    pallas_call x1, Pallas kernels, per_device(): pl.pallas_call(hidden_grad_kernel, out_shape=(shape((rows, units), jnp.fl...  6.42 us
    ppermute x2, starting transfers between devices, over_t(): lax.ppermute(x, 'tensor', [(i, move(i)) for i in range(tensor_count)])  5.86 us
    pallas_call x1, Pallas kernels, per_device(): pl.pallas_call(partial_kernel, out_shape=shape((ring_y, 2, CAP, BLK, BLK)...  4.78 us
    unnamed x16, local copies, waits for them, and re-layouts  3.99 us
  transfers between devices with their start and end apart: 15, of which 9 were waited for; matrix products, arithmetic and copies ran while one was open for 2% of the time, Pallas kernels for 8%

profile of v5, /device:TPU:1, one launch (start us, length us, event | category | flops | bytes accessed | tf_op | source)
XLA Modules:
  0.0 167.1 jit_solution(14826751013255178286)
XLA Ops:
  7.2 3.9 %collective-permute-start.1 = (bf16[8,8192]{1,0:T(8,128)(2,1)}, bf16[8,8192]{1,0:T(8,128)(2,1)S(1)}, u32[]{:S(2)}, u32[]{:S(2)}) collective-permute-start(bf16[8,8192]{1,0:T(8,128)(2,1)} %own_ref.1), channel_id=1, source_target_pairs={{0,8},{1,9},{2,10},{3,11},{4,12},{5,13},{6,14},{7,15},{8,0},{9,1},... | collective-permute-start | bytes 393224 | tf_op jit(solution)/shard_map/ppermute | solution.py:216
  11.2 1.9 %collective-permute-start = (s32[1]{0:T(128)}, s32[1]{0:T(128)}, u32[]{:S(2)}, u32[]{:S(2)}) collective-permute-start(s32[1]{0:T(128)} %param.7), channel_id=1, source_target_pairs={{0,8},{1,9},{2,10},{3,11},{4,12},{5,13},{6,14},{7,15},{8,0},{9,1},... | collective-permute-start | bytes 20 | tf_op jit(solution)/shard_map/ppermute | solution.py:216
  13.7 2.0 %collective-permute-done.live_other_ref = s32[1]{0:T(128)} collective-permute-done((s32[1]{0:T(128)}, s32[1]{0:T(128)}, u32[]{:S(2)}, u32[]{:S(2)}) %collective-permute-start) | collective-permute-done | bytes 36 | tf_op jit(solution)/shard_map/ppermute | solution.py:216
  18.1 2.3 %hidden.1 = (s32[128]{0:T(128)}, bf16[128,768]{1,0:T(8,128)(2,1)}) custom-call(s32[1]{0:T(128)} %bitcast.f_ref, s32[6,64]{1,0:T(8,128)} %mask_ref.5, bf16[128,768]{1,0:T(8,128)(2,1)} %gate_ref.3, bf16[128,768]{1,0:T(8,128)(2,1)} %up_ref.3), custom_call_target="tpu_custom_call" | custom-call | flops 1000 | bytes 1048576 | tf_op jit(solution)/shard_map/hidden/pallas_call | solution.py:243
  20.5 7.7 %collective-permute-start.11 = (bf16[128,768]{1,0:T(8,128)(2,1)}, bf16[128,768]{1,0:T(8,128)(2,1)S(1)}, u32[]{:S(2)}, u32[]{:S(2)}) collective-permute-start(bf16[128,768]{1,0:T(8,128)(2,1)} %get-tuple-element.14.own_ref), channel_id=1, source_target_pairs={{0,16},{16,0},{32,48},{48,32},{64,80},{80,64},{96,112},{112,96},{1... | collective-permute-start | bytes 589832 | tf_op jit(solution)/shard_map/ppermute | solution.py:213
  30.2 2.0 %join.1.hidden_ref = bf16[768,256]{1,0:T(8,128)(2,1)} custom-call(s32[2]{0:T(128)} %pad_add_fusion.core_ref, bf16[128,768]{1,0:T(8,128)(2,1)} %get-tuple-element.14.own_ref, bf16[128,768]{1,0:T(8,128)(2,1)} %copy-done.7), custom_call_target="tpu_custom_call" | custom-call | flops 1000 | bytes 1048576 | tf_op jit(solution)/shard_map/join/pallas_call | solution.py:280
  32.1 37.1 %all-gather.2.cloned.1.call-done = bf16[32,8,8192]{2,1,0:T(8,128)(2,1)} async-done(((bf16[2,8,8192]{2,1,0:T(8,128)(2,1)}), bf16[32,8,8192]{2,1,0:T(8,128)(2,1)}) %all-gather.2.cloned.1.call-update) | async-done | bytes 4194320 | tf_op jit(solution)/shard_map/all_gather | solution.py:273
  69.3 4.8 %partial.1 = bf16[8,2,4,128,128]{4,3,2,1,0:T(8,128)(2,1)} custom-call(s32[128]{0:T(128)} %get-tuple-element.9.table_ref, s32[2]{0:T(128)} %pad_add_fusion.core_ref, bf16[768,256]{1,0:T(8,128)(2,1)} %join.1.hidden_ref, bf16[256,8192]{1,0:T(8,128)(2,1)} %bitcast.27), custom_call_target="tpu_custom_call" | custom-call | flops 536870912 | bytes 4194304 | tf_op jit(solution)/shard_map/partial/pallas_call | solution.py:307
  75.9 4.7 %collective-permute-start.2 = (bf16[4,128,128]{2,1,0:T(8,128)(2,1)}, bf16[4,128,128]{2,1,0:T(8,128)(2,1)S(1)}, u32[]{:S(2)}, u32[]{:S(2)}) collective-permute-start(bf16[4,128,128]{2,1,0:T(8,128)(2,1)} %pack.1), channel_id=1, source_target_pairs={{0,32},{16,48},{32,0},{48,16},{64,96},{80,112},{96,64},{112,80},{1... | collective-permute-start | bytes 393224 | tf_op jit(solution)/shard_map/ppermute | solution.py:213
  80.7 3.7 %collective-permute-done.2 = bf16[4,128,128]{2,1,0:T(8,128)(2,1)S(1)} collective-permute-done((bf16[4,128,128]{2,1,0:T(8,128)(2,1)}, bf16[4,128,128]{2,1,0:T(8,128)(2,1)S(1)}, u32[]{:S(2)}, u32[]{:S(2)}) %collective-permute-start.2) | collective-permute-done | bytes 131104 | tf_op jit(solution)/shard_map/ppermute | solution.py:213
  85.4 3.1 %collective-permute-start.3 = (bf16[2,4,128,128]{3,2,1,0:T(8,128)(2,1)S(1)}, bf16[2,4,128,128]{3,2,1,0:T(8,128)(2,1)S(1)}, u32[]{:S(2)}, u32[]{:S(2)}) collective-permute-start(bf16[2,4,128,128]{3,2,1,0:T(8,128)(2,1)S(1)} %broadcast_select_fusion), channel_id=1, source_target_pairs={{0,64},{16,80},{32,96},{48,112},{64,128},{80,144},{96,160},{112,17... | collective-permute-start | bytes 786440 | tf_op jit(solution)/shard_map/ppermute | solution.py:213
  88.5 3.4 %collective-permute-start.4 = (bf16[2,4,128,128]{3,2,1,0:T(8,128)(2,1)S(1)}, bf16[2,4,128,128]{3,2,1,0:T(8,128)(2,1)S(1)}, u32[]{:S(2)}, u32[]{:S(2)}) collective-permute-start(bf16[2,4,128,128]{3,2,1,0:T(8,128)(2,1)S(1)} %broadcast_select_fusion), channel_id=1, source_target_pairs={{0,448},{16,464},{32,480},{48,496},{64,0},{80,16},{96,32},{112,48}... | collective-permute-start | bytes 786440 | tf_op jit(solution)/shard_map/ppermute | solution.py:213
  92.6 9.4 %collective-permute-done.3 = bf16[2,4,128,128]{3,2,1,0:T(8,128)(2,1)S(1)} collective-permute-done((bf16[2,4,128,128]{3,2,1,0:T(8,128)(2,1)S(1)}, bf16[2,4,128,128]{3,2,1,0:T(8,128)(2,1)S(1)}, u32[]{:S(2)}, u32[]{:S(2)}) %collective-permute-start.3) | collective-permute-done | bytes 262176 | tf_op jit(solution)/shard_map/ppermute | solution.py:213
  102.0 1.9 %collective-permute-start.5 = (bf16[2,4,128,128]{3,2,1,0:T(8,128)(2,1)S(1)}, bf16[2,4,128,128]{3,2,1,0:T(8,128)(2,1)S(1)}, u32[]{:S(2)}, u32[]{:S(2)}) collective-permute-start(bf16[2,4,128,128]{3,2,1,0:T(8,128)(2,1)S(1)} %collective-permute-done.3), channel_id=1, source_target_pairs={{0,64},{16,80},{32,96},{48,112},{64,128},{80,144},{96,160},{112,17... | collective-permute-start | bytes 786440 | tf_op jit(solution)/shard_map/ppermute | solution.py:213
  103.9 4.6 %collective-permute-start.6 = (bf16[2,4,128,128]{3,2,1,0:T(8,128)(2,1)S(1)}, bf16[2,4,128,128]{3,2,1,0:T(8,128)(2,1)S(1)}, u32[]{:S(2)}, u32[]{:S(2)}) collective-permute-start(bf16[2,4,128,128]{3,2,1,0:T(8,128)(2,1)S(1)} %collective-permute-done.4), channel_id=1, source_target_pairs={{0,448},{16,464},{32,480},{48,496},{64,0},{80,16},{96,32},{112,48}... | collective-permute-start | bytes 786440 | tf_op jit(solution)/shard_map/ppermute | solution.py:213
  108.6 9.1 %collective-permute-done.5 = bf16[2,4,128,128]{3,2,1,0:T(8,128)(2,1)S(1)} collective-permute-done((bf16[2,4,128,128]{3,2,1,0:T(8,128)(2,1)S(1)}, bf16[2,4,128,128]{3,2,1,0:T(8,128)(2,1)S(1)}, u32[]{:S(2)}, u32[]{:S(2)}) %collective-permute-start.5) | collective-permute-done | bytes 262176 | tf_op jit(solution)/shard_map/ppermute | solution.py:213
  117.7 1.9 %collective-permute-start.7 = (bf16[2,4,128,128]{3,2,1,0:T(8,128)(2,1)S(1)}, bf16[2,4,128,128]{3,2,1,0:T(8,128)(2,1)S(1)}, u32[]{:S(2)}, u32[]{:S(2)}) collective-permute-start(bf16[2,4,128,128]{3,2,1,0:T(8,128)(2,1)S(1)} %collective-permute-done.5), channel_id=1, source_target_pairs={{0,64},{16,80},{32,96},{48,112},{64,128},{80,144},{96,160},{112,17... | collective-permute-start | bytes 786440 | tf_op jit(solution)/shard_map/ppermute | solution.py:213
  119.6 4.6 %collective-permute-start.8 = (bf16[2,4,128,128]{3,2,1,0:T(8,128)(2,1)S(1)}, bf16[2,4,128,128]{3,2,1,0:T(8,128)(2,1)S(1)}, u32[]{:S(2)}, u32[]{:S(2)}) collective-permute-start(bf16[2,4,128,128]{3,2,1,0:T(8,128)(2,1)S(1)} %collective-permute-done.6), channel_id=1, source_target_pairs={{0,448},{16,464},{32,480},{48,496},{64,0},{80,16},{96,32},{112,48}... | collective-permute-start | bytes 786440 | tf_op jit(solution)/shard_map/ppermute | solution.py:213
  126.0 1.9 %collective-permute-start.9 = (bf16[2,4,128,128]{3,2,1,0:T(8,128)(2,1)S(1)}, bf16[2,4,128,128]{3,2,1,0:T(8,128)(2,1)S(1)}, u32[]{:S(2)}, u32[]{:S(2)}) collective-permute-start(bf16[2,4,128,128]{3,2,1,0:T(8,128)(2,1)S(1)} %collective-permute-done.7), channel_id=1, source_target_pairs={{0,64},{16,80},{32,96},{48,112},{64,128},{80,144},{96,160},{112,17... | collective-permute-start | bytes 786440 | tf_op jit(solution)/shard_map/ppermute | solution.py:213
  128.0 6.3 %collective-permute-done.9 = bf16[2,4,128,128]{3,2,1,0:T(8,128)(2,1)S(1)} collective-permute-done((bf16[2,4,128,128]{3,2,1,0:T(8,128)(2,1)S(1)}, bf16[2,4,128,128]{3,2,1,0:T(8,128)(2,1)S(1)}, u32[]{:S(2)}, u32[]{:S(2)}) %collective-permute-start.9) | collective-permute-done | bytes 262176 | tf_op jit(solution)/shard_map/ppermute | solution.py:213
  135.7 6.4 %hidden_grad.1 = (f32[128,768]{1,0:T(8,128)}, f32[128,768]{1,0:T(8,128)}) custom-call(s32[128]{0:T(128)} %get-tuple-element.9.table_ref, s32[2]{0:T(128)} %pad_add_fusion.core_ref, bf16[256,8192]{1,0:T(8,128)(2,1)} %bitcast.28, bf16[16,4,128,128]{3,2,1,0:T(8,128)(2,1)} %bitcast.29), custom_call_target="tpu_custom_call" | custom-call | flops 536870912 | bytes 6291456 | tf_op jit(solution)/shard_map/hidden_grad/pallas_call | solution.py:331
  142.2 7.1 %collective-permute-start.10 = (f32[128,768]{1,0:T(8,128)}, f32[128,768]{1,0:T(8,128)S(1)}, u32[]{:S(2)}, u32[]{:S(2)}) collective-permute-start(f32[128,768]{1,0:T(8,128)} %get-tuple-element.11), channel_id=1, source_target_pairs={{0,16},{16,0},{32,48},{48,32},{64,80},{80,64},{96,112},{112,96},{1... | collective-permute-start | bytes 1179656 | tf_op jit(solution)/shard_map/ppermute | solution.py:213
  150.3 4.5 %collective-permute-start.12 = (bf16[4,128,128]{2,1,0:T(8,128)(2,1)S(1)}, bf16[4,128,128]{2,1,0:T(8,128)(2,1)S(1)}, u32[]{:S(2)}, u32[]{:S(2)}) collective-permute-start(bf16[4,128,128]{2,1,0:T(8,128)(2,1)S(1)} %get-tuple-element.15), channel_id=1, source_target_pairs={{0,32},{16,48},{32,0},{48,16},{64,96},{80,112},{96,64},{112,80},{1... | collective-permute-start | bytes 393224 | tf_op jit(solution)/shard_map/ppermute | solution.py:213
  156.7 2.0 %collective-permute-done.12.other_ref = bf16[4,128,128]{2,1,0:T(8,128)(2,1)S(1)} collective-permute-done((bf16[4,128,128]{2,1,0:T(8,128)(2,1)S(1)}, bf16[4,128,128]{2,1,0:T(8,128)(2,1)S(1)}, u32[]{:S(2)}, u32[]{:S(2)}) %collective-permute-start.12) | collective-permute-done | bytes 131104 | tf_op jit(solution)/shard_map/ppermute | solution.py:213
  (45 shorter events, 15.8 us)
Async XLA Ops:
  7.2 62.1 %all-gather.2.cloned.1.call-start = ((), (), s32[]{:S(2)}) async-start(), calls=%async_computation.1 | async-start | bytes 4456448 | tf_op jit(solution)/shard_map/all_gather | solution.py:273
  7.2 8.5 %collective-permute-start.1 = (bf16[8,8192]{1,0:T(8,128)(2,1)}, bf16[8,8192]{1,0:T(8,128)(2,1)S(1)}, u32[]{:S(2)}, u32[]{:S(2)}) collective-permute-start(bf16[8,8192]{1,0:T(8,128)(2,1)} %own_ref.1), channel_id=1, source_target_pairs={{0,8},{1,9},{2,10},{3,11},{4,12},{5,13},{6,14},{7,15},{8,0},{9,1},... | collective-permute-start | bytes 393224 | tf_op jit(solution)/shard_map/ppermute | solution.py:216
  11.2 4.6 %collective-permute-start = (s32[1]{0:T(128)}, s32[1]{0:T(128)}, u32[]{:S(2)}, u32[]{:S(2)}) collective-permute-start(s32[1]{0:T(128)} %param.7), channel_id=1, source_target_pairs={{0,8},{1,9},{2,10},{3,11},{4,12},{5,13},{6,14},{7,15},{8,0},{9,1},... | collective-permute-start | bytes 20 | tf_op jit(solution)/shard_map/ppermute | solution.py:216
  15.7 0.9 copy-start.3
  18.1 131.2 %reduce-scatter.2.cloned.1.call-start = ((), (), s32[]{:S(2)}) async-start(), calls=%async_computation.2 | async-start | bytes 2359296 | tf_op jit(solution)/shard_map/reduce_scatter | solution.py:321
  20.5 9.0 %collective-permute-start.11 = (bf16[128,768]{1,0:T(8,128)(2,1)}, bf16[128,768]{1,0:T(8,128)(2,1)S(1)}, u32[]{:S(2)}, u32[]{:S(2)}) collective-permute-start(bf16[128,768]{1,0:T(8,128)(2,1)} %get-tuple-element.14.own_ref), channel_id=1, source_target_pairs={{0,16},{16,0},{32,48},{48,32},{64,80},{80,64},{96,112},{112,96},{1... | collective-permute-start | bytes 589832 | tf_op jit(solution)/shard_map/ppermute | solution.py:213
  29.5 0.7 copy-start.7
  75.9 16.6 %copy-start.6 = (bf16[4,128,128]{2,1,0:T(8,128)(2,1)S(1)}, bf16[4,128,128]{2,1,0:T(8,128)(2,1)}, u32[]{:S(2)}) copy-start(bf16[4,128,128]{2,1,0:T(8,128)(2,1)} %pack.1) | copy-start | bytes 393220
  75.9 8.5 %collective-permute-start.2 = (bf16[4,128,128]{2,1,0:T(8,128)(2,1)}, bf16[4,128,128]{2,1,0:T(8,128)(2,1)S(1)}, u32[]{:S(2)}, u32[]{:S(2)}) collective-permute-start(bf16[4,128,128]{2,1,0:T(8,128)(2,1)} %pack.1), channel_id=1, source_target_pairs={{0,32},{16,48},{32,0},{48,16},{64,96},{80,112},{96,64},{112,80},{1... | collective-permute-start | bytes 393224 | tf_op jit(solution)/shard_map/ppermute | solution.py:213
  85.4 16.6 %collective-permute-start.3 = (bf16[2,4,128,128]{3,2,1,0:T(8,128)(2,1)S(1)}, bf16[2,4,128,128]{3,2,1,0:T(8,128)(2,1)S(1)}, u32[]{:S(2)}, u32[]{:S(2)}) collective-permute-start(bf16[2,4,128,128]{3,2,1,0:T(8,128)(2,1)S(1)} %broadcast_select_fusion), channel_id=1, source_target_pairs={{0,64},{16,80},{32,96},{48,112},{64,128},{80,144},{96,160},{112,17... | collective-permute-start | bytes 786440 | tf_op jit(solution)/shard_map/ppermute | solution.py:213
  88.5 15.4 %collective-permute-start.4 = (bf16[2,4,128,128]{3,2,1,0:T(8,128)(2,1)S(1)}, bf16[2,4,128,128]{3,2,1,0:T(8,128)(2,1)S(1)}, u32[]{:S(2)}, u32[]{:S(2)}) collective-permute-start(bf16[2,4,128,128]{3,2,1,0:T(8,128)(2,1)S(1)} %broadcast_select_fusion), channel_id=1, source_target_pairs={{0,448},{16,464},{32,480},{48,496},{64,0},{80,16},{96,32},{112,48}... | collective-permute-start | bytes 786440 | tf_op jit(solution)/shard_map/ppermute | solution.py:213
  102.0 15.7 %collective-permute-start.5 = (bf16[2,4,128,128]{3,2,1,0:T(8,128)(2,1)S(1)}, bf16[2,4,128,128]{3,2,1,0:T(8,128)(2,1)S(1)}, u32[]{:S(2)}, u32[]{:S(2)}) collective-permute-start(bf16[2,4,128,128]{3,2,1,0:T(8,128)(2,1)S(1)} %collective-permute-done.3), channel_id=1, source_target_pairs={{0,64},{16,80},{32,96},{48,112},{64,128},{80,144},{96,160},{112,17... | collective-permute-start | bytes 786440 | tf_op jit(solution)/shard_map/ppermute | solution.py:213
  103.9 15.6 %collective-permute-start.6 = (bf16[2,4,128,128]{3,2,1,0:T(8,128)(2,1)S(1)}, bf16[2,4,128,128]{3,2,1,0:T(8,128)(2,1)S(1)}, u32[]{:S(2)}, u32[]{:S(2)}) collective-permute-start(bf16[2,4,128,128]{3,2,1,0:T(8,128)(2,1)S(1)} %collective-permute-done.4), channel_id=1, source_target_pairs={{0,448},{16,464},{32,480},{48,496},{64,0},{80,16},{96,32},{112,48}... | collective-permute-start | bytes 786440 | tf_op jit(solution)/shard_map/ppermute | solution.py:213
  117.7 8.3 %collective-permute-start.7 = (bf16[2,4,128,128]{3,2,1,0:T(8,128)(2,1)S(1)}, bf16[2,4,128,128]{3,2,1,0:T(8,128)(2,1)S(1)}, u32[]{:S(2)}, u32[]{:S(2)}) collective-permute-start(bf16[2,4,128,128]{3,2,1,0:T(8,128)(2,1)S(1)} %collective-permute-done.5), channel_id=1, source_target_pairs={{0,64},{16,80},{32,96},{48,112},{64,128},{80,144},{96,160},{112,17... | collective-permute-start | bytes 786440 | tf_op jit(solution)/shard_map/ppermute | solution.py:213
  119.6 8.4 %collective-permute-start.8 = (bf16[2,4,128,128]{3,2,1,0:T(8,128)(2,1)S(1)}, bf16[2,4,128,128]{3,2,1,0:T(8,128)(2,1)S(1)}, u32[]{:S(2)}, u32[]{:S(2)}) collective-permute-start(bf16[2,4,128,128]{3,2,1,0:T(8,128)(2,1)S(1)} %collective-permute-done.6), channel_id=1, source_target_pairs={{0,448},{16,464},{32,480},{48,496},{64,0},{80,16},{96,32},{112,48}... | collective-permute-start | bytes 786440 | tf_op jit(solution)/shard_map/ppermute | solution.py:213
  126.0 8.3 %collective-permute-start.9 = (bf16[2,4,128,128]{3,2,1,0:T(8,128)(2,1)S(1)}, bf16[2,4,128,128]{3,2,1,0:T(8,128)(2,1)S(1)}, u32[]{:S(2)}, u32[]{:S(2)}) collective-permute-start(bf16[2,4,128,128]{3,2,1,0:T(8,128)(2,1)S(1)} %collective-permute-done.7), channel_id=1, source_target_pairs={{0,64},{16,80},{32,96},{48,112},{64,128},{80,144},{96,160},{112,17... | collective-permute-start | bytes 786440 | tf_op jit(solution)/shard_map/ppermute | solution.py:213
  134.3 1.4 copy-start.5
  135.7 19.1 %copy-start = (bf16[128,768]{1,0:T(8,128)(2,1)S(1)}, bf16[128,768]{1,0:T(8,128)(2,1)}, u32[]{:S(2)}) copy-start(bf16[128,768]{1,0:T(8,128)(2,1)} %gate_ref.3) | copy-start | bytes 589828
  135.7 19.1 %copy-start.1 = (bf16[128,768]{1,0:T(8,128)(2,1)S(1)}, bf16[128,768]{1,0:T(8,128)(2,1)}, u32[]{:S(2)}) copy-start(bf16[128,768]{1,0:T(8,128)(2,1)} %up_ref.3) | copy-start | bytes 589828
  135.7 23.0 %copy-start.4 = (s32[6,64]{1,0:T(8,128)S(1)}, s32[6,64]{1,0:T(8,128)}, u32[]{:S(2)}) copy-start(s32[6,64]{1,0:T(8,128)} %mask_ref.5) | copy-start | bytes 4612
  142.2 12.6 %collective-permute-start.10 = (f32[128,768]{1,0:T(8,128)}, f32[128,768]{1,0:T(8,128)S(1)}, u32[]{:S(2)}, u32[]{:S(2)}) collective-permute-start(f32[128,768]{1,0:T(8,128)} %get-tuple-element.11), channel_id=1, source_target_pairs={{0,16},{16,0},{32,48},{48,32},{64,80},{80,64},{96,112},{112,96},{1... | collective-permute-start | bytes 1179656 | tf_op jit(solution)/shard_map/ppermute | solution.py:213
  150.3 8.4 %collective-permute-start.12 = (bf16[4,128,128]{2,1,0:T(8,128)(2,1)S(1)}, bf16[4,128,128]{2,1,0:T(8,128)(2,1)S(1)}, u32[]{:S(2)}, u32[]{:S(2)}) collective-permute-start(bf16[4,128,128]{2,1,0:T(8,128)(2,1)S(1)} %get-tuple-element.15), channel_id=1, source_target_pairs={{0,32},{16,48},{32,0},{48,16},{64,96},{80,112},{96,64},{112,80},{1... | collective-permute-start | bytes 393224 | tf_op jit(solution)/shard_map/ppermute | solution.py:213
  154.8 1.0 copy-start.2
Sparse Core Ops, SparseCore 0:
  18.2 51.0 all-gather.1
  74.2 47.4 reduce-scatter.1

commit v6 on v5

--- a/solution.py
+++ b/solution.py
@@ -29,14 +29,11 @@
     return jnp.swapaxes(x.reshape(rows // (2 * TOK), 2, TOK, width), 0, 1).reshape(rows, width)
 
 
-def mask_kernel(xl_ref, live_ref, live_other_ref, own_ref, other_ref, out_ref):
-    rows = lax.broadcasted_iota(jnp.int32, own_ref.shape, 0)
-    for at, live, ref in (
-        (xl_ref[0], live_ref[0], own_ref),
-        (1 - xl_ref[0], live_other_ref[0], other_ref),
-    ):
-        value = ref[...].astype(jnp.float32)
-        out_ref[at] = jnp.where(rows < live, value, 0.0).astype(jnp.bfloat16)
+def mask_kernel(xl_ref, live_ref, own_ref, other_ref, out_ref):
+    rows = lax.broadcasted_iota(jnp.int32, other_ref.shape, 0)
+    value = other_ref[...].astype(jnp.float32)
+    out_ref[xl_ref[0]] = own_ref[...]
+    out_ref[1 - xl_ref[0]] = jnp.where(rows < live_ref[0], value, 0.0).astype(jnp.bfloat16)
 
 
 def pack_kernel(f_ref, mask_ref, weight_ref, packed_ref):
@@ -254,15 +251,18 @@
         first = (jnp.arange(2) == index).reshape((2,) + (1,) * own.ndim)
         return jnp.where(first, own[None], other[None])
 
+    own_masked = jnp.where(
+        jnp.arange(tok)[:, None] < live_rows[0], out_grad, jnp.zeros((), jnp.bfloat16)
+    )
     masked = pl.pallas_call(
         mask_kernel,
         out_shape=shape((2, tok, width)),
-        in_specs=[SMEM, SMEM, SMEM, VMEM, VMEM],
+        in_specs=[SMEM, SMEM, VMEM, VMEM],
         out_specs=VMEM,
         name="mask",
         compiler_params=pltpu.CompilerParams(vmem_limit_bytes=16 << 20),
         cost_estimate=cost(1000, 1 << 20),
-    )(xl.reshape(1).astype(jnp.int32), live_rows, live_other, out_grad, grad_other)
+    )(xl.reshape(1).astype(jnp.int32), live_other, own_masked, grad_other)
 
     columns = [[k + 4 * i for i in range(ring_y)] for k in range(4)]
     chips = [
@@ -283,6 +283,7 @@
         in_specs=[SMEM, VMEM, VMEM],
         out_specs=VMEM,
         name="join",
+        compiler_params=pltpu.CompilerParams(vmem_limit_bytes=16 << 20),
         cost_estimate=cost(1000, 1 << 20),
     )(core_arr, hidden, hidden_other)
 
@@ -316,12 +317,14 @@
             ),
         ),
         name="partial",
+        compiler_params=pltpu.CompilerParams(vmem_limit_bytes=20 << 20),
         cost_estimate=cost(ring_y * 16 * BLK * BLK * 2 * rows, ring_y << 19),
     )(table, core_arr, hidden_pair, panel)
     sums = lax.psum_scatter(
         tiles, "fsdp", scatter_dimension=0, axis_index_groups=columns, tiled=True
     )[0]
-    own_sum, send_sum = sums[0].astype(jnp.float32), sums[1]
+    sums, send_sum = lax.optimization_barrier((sums, sums[1]))
+    own_sum = sums[0].astype(jnp.float32)
     other_sum = swap_xh(send_sum)
 
     groups = 4

time: 168 us -> 171 us (1.018)
  local copies, waits for them, and re-layouts: 4.76 us -> 7.87 us
  Pallas kernels: 21.2 us -> 18.4 us
  waiting for transfers between devices: 71.9 us -> 74.7 us
    ppermute x11, waiting for transfers between devices: 32.7 us -> 35.7 us  [over_f(): return lax.ppermute(x, 'fsdp', [(i, move(i)) for i in range(fsdp_count)])]
    unnamed x16 -> x20, local copies, waits for them, and re-layouts: 3.99 us -> 6.18 us
  transfers between devices with their start and end apart: 15 -> 15, of which waited for: 9 -> 10; matrix products, arithmetic and copies ran while one was open for 2% -> 2% of each run, Pallas kernels for 8% -> 7%
where the time goes in v6:
time: 171 us
  waiting for transfers between devices  74.7 us (44%)
  starting transfers between devices  51.3 us (30%)
  Pallas kernels  18.4 us (11%)
  between operations  15 us (9%)
  local copies, waits for them, and re-layouts  7.87 us (5%)
  other arithmetic  3.16 us (2%)
    ppermute x11, starting transfers between devices, over_f(): return lax.ppermute(x, 'fsdp', [(i, move(i)) for i in range(fsdp_count)])  45.4 us
    all_gather x1, waiting for transfers between devices, per_device(): lax.all_gather(masked, ('fsdp', 'tensor'), axis_index_groups=chips, tiled...  38.1 us
    ppermute x11, waiting for transfers between devices, over_f(): return lax.ppermute(x, 'fsdp', [(i, move(i)) for i in range(fsdp_count)])  35.7 us
    pallas_call x1, Pallas kernels, per_device(): pl.pallas_call(hidden_grad_kernel, out_shape=(shape((rows, units), jnp.fl...  6.39 us
    unnamed x20, local copies, waits for them, and re-layouts  6.18 us
    ppermute x2, starting transfers between devices, over_t(): lax.ppermute(x, 'tensor', [(i, move(i)) for i in range(tensor_count)])  5.86 us
  transfers between devices with their start and end apart: 15, of which 10 were waited for; matrix products, arithmetic and copies ran while one was open for 2% of the time, Pallas kernels for 7%

profile of v6, /device:TPU:1, one launch (start us, length us, event | category | flops | bytes accessed | tf_op | source)
XLA Modules:
  0.0 170.5 jit_solution(9899031593258320189)
XLA Ops:
  7.2 3.9 %collective-permute-start.1 = (bf16[8,8192]{1,0:T(8,128)(2,1)}, bf16[8,8192]{1,0:T(8,128)(2,1)S(1)}, u32[]{:S(2)}, u32[]{:S(2)}) collective-permute-start(bf16[8,8192]{1,0:T(8,128)(2,1)} %param.6), channel_id=1, source_target_pairs={{0,8},{1,9},{2,10},{3,11},{4,12},{5,13},{6,14},{7,15},{8,0},{9,1},... | collective-permute-start | bytes 393224 | tf_op jit(solution)/shard_map/ppermute | solution.py:213
  11.2 1.9 %collective-permute-start = (s32[1]{0:T(128)}, s32[1]{0:T(128)}, u32[]{:S(2)}, u32[]{:S(2)}) collective-permute-start(s32[1]{0:T(128)} %param.7), channel_id=1, source_target_pairs={{0,8},{1,9},{2,10},{3,11},{4,12},{5,13},{6,14},{7,15},{8,0},{9,1},... | collective-permute-start | bytes 20 | tf_op jit(solution)/shard_map/ppermute | solution.py:213
  17.0 2.3 %hidden.1 = (s32[128]{0:T(128)}, bf16[128,768]{1,0:T(8,128)(2,1)}) custom-call(s32[1]{0:T(128)} %bitcast.f_ref, s32[6,64]{1,0:T(8,128)} %mask_ref.5, bf16[128,768]{1,0:T(8,128)(2,1)} %gate_ref.3, bf16[128,768]{1,0:T(8,128)(2,1)} %up_ref.3), custom_call_target="tpu_custom_call" | custom-call | flops 1000 | bytes 1048576 | tf_op jit(solution)/shard_map/hidden/pallas_call | solution.py:240
  19.4 8.0 %collective-permute-start.11 = (bf16[128,768]{1,0:T(8,128)(2,1)}, bf16[128,768]{1,0:T(8,128)(2,1)S(1)}, u32[]{:S(2)}, u32[]{:S(2)}) collective-permute-start(bf16[128,768]{1,0:T(8,128)(2,1)} %get-tuple-element.16.own_ref), channel_id=1, source_target_pairs={{0,16},{16,0},{32,48},{48,32},{64,80},{80,64},{96,112},{112,96},{1... | collective-permute-start | bytes 589832 | tf_op jit(solution)/shard_map/ppermute | solution.py:210
  30.3 38.1 %all-gather.2.cloned.1.call-done = bf16[32,8,8192]{2,1,0:T(8,128)(2,1)} async-done(((bf16[2,8,8192]{2,1,0:T(8,128)(2,1)}), bf16[32,8,8192]{2,1,0:T(8,128)(2,1)}) %all-gather.2.cloned.1.call-update) | async-done | bytes 4194320 | tf_op jit(solution)/shard_map/all_gather | solution.py:273
  68.4 2.2 %copy-done = bf16[32,8,8192]{2,1,0:T(8,128)(2,1)S(1)} copy-done((bf16[32,8,8192]{2,1,0:T(8,128)(2,1)S(1)}, bf16[32,8,8192]{2,1,0:T(8,128)(2,1)}, u32[]{:S(2)}) %copy-start) | copy-done | bytes 4194328
  71.3 3.3 %partial.1 = bf16[8,2,4,128,128]{4,3,2,1,0:T(8,128)(2,1)} custom-call(s32[128]{0:T(128)S(1)} %copy-done.7, s32[2]{0:T(128)S(1)} %pad_add_fusion.core_ref, bf16[768,256]{1,0:T(8,128)(2,1)S(1)} %join.1.hidden_ref, bf16[256,8192]{1,0:T(8,128)(2,1)S(1)} %bitcast.29), custom_call_target="tpu_custom_call" | custom-call | flops 536870912 | bytes 4194304 | tf_op jit(solution)/shard_map/partial/pallas_call | solution.py:308
  74.6 1.8 %pack.1 = bf16[4,128,128]{2,1,0:T(8,128)(2,1)} custom-call(s32[1]{0:T(128)} %bitcast.f_ref, s32[6,64]{1,0:T(8,128)} %mask_ref.5, bf16[768,256]{1,0:T(8,128)(2,1)} %weight_ref.1), custom_call_target="tpu_custom_call" | custom-call | flops 1000 | bytes 1048576 | tf_op jit(solution)/shard_map/pack/pallas_call | solution.py:229
  76.5 4.7 %collective-permute-start.2 = (bf16[4,128,128]{2,1,0:T(8,128)(2,1)}, bf16[4,128,128]{2,1,0:T(8,128)(2,1)S(1)}, u32[]{:S(2)}, u32[]{:S(2)}) collective-permute-start(bf16[4,128,128]{2,1,0:T(8,128)(2,1)} %pack.1), channel_id=1, source_target_pairs={{0,32},{16,48},{32,0},{48,16},{64,96},{80,112},{96,64},{112,80},{1... | collective-permute-start | bytes 393224 | tf_op jit(solution)/shard_map/ppermute | solution.py:210
  81.2 3.7 %collective-permute-done.2 = bf16[4,128,128]{2,1,0:T(8,128)(2,1)S(1)} collective-permute-done((bf16[4,128,128]{2,1,0:T(8,128)(2,1)}, bf16[4,128,128]{2,1,0:T(8,128)(2,1)S(1)}, u32[]{:S(2)}, u32[]{:S(2)}) %collective-permute-start.2) | collective-permute-done | bytes 131104 | tf_op jit(solution)/shard_map/ppermute | solution.py:210
  86.0 3.1 %collective-permute-start.3 = (bf16[2,4,128,128]{3,2,1,0:T(8,128)(2,1)S(1)}, bf16[2,4,128,128]{3,2,1,0:T(8,128)(2,1)S(1)}, u32[]{:S(2)}, u32[]{:S(2)}) collective-permute-start(bf16[2,4,128,128]{3,2,1,0:T(8,128)(2,1)S(1)} %broadcast_select_fusion), channel_id=1, source_target_pairs={{0,64},{16,80},{32,96},{48,112},{64,128},{80,144},{96,160},{112,17... | collective-permute-start | bytes 786440 | tf_op jit(solution)/shard_map/ppermute | solution.py:210
  89.1 3.4 %collective-permute-start.4 = (bf16[2,4,128,128]{3,2,1,0:T(8,128)(2,1)S(1)}, bf16[2,4,128,128]{3,2,1,0:T(8,128)(2,1)S(1)}, u32[]{:S(2)}, u32[]{:S(2)}) collective-permute-start(bf16[2,4,128,128]{3,2,1,0:T(8,128)(2,1)S(1)} %broadcast_select_fusion), channel_id=1, source_target_pairs={{0,448},{16,464},{32,480},{48,496},{64,0},{80,16},{96,32},{112,48}... | collective-permute-start | bytes 786440 | tf_op jit(solution)/shard_map/ppermute | solution.py:210
  93.2 9.3 %collective-permute-done.3 = bf16[2,4,128,128]{3,2,1,0:T(8,128)(2,1)S(1)} collective-permute-done((bf16[2,4,128,128]{3,2,1,0:T(8,128)(2,1)S(1)}, bf16[2,4,128,128]{3,2,1,0:T(8,128)(2,1)S(1)}, u32[]{:S(2)}, u32[]{:S(2)}) %collective-permute-start.3) | collective-permute-done | bytes 262176 | tf_op jit(solution)/shard_map/ppermute | solution.py:210
  102.6 1.9 %collective-permute-start.5 = (bf16[2,4,128,128]{3,2,1,0:T(8,128)(2,1)S(1)}, bf16[2,4,128,128]{3,2,1,0:T(8,128)(2,1)S(1)}, u32[]{:S(2)}, u32[]{:S(2)}) collective-permute-start(bf16[2,4,128,128]{3,2,1,0:T(8,128)(2,1)S(1)} %collective-permute-done.3), channel_id=1, source_target_pairs={{0,64},{16,80},{32,96},{48,112},{64,128},{80,144},{96,160},{112,17... | collective-permute-start | bytes 786440 | tf_op jit(solution)/shard_map/ppermute | solution.py:210
  104.5 4.6 %collective-permute-start.6 = (bf16[2,4,128,128]{3,2,1,0:T(8,128)(2,1)S(1)}, bf16[2,4,128,128]{3,2,1,0:T(8,128)(2,1)S(1)}, u32[]{:S(2)}, u32[]{:S(2)}) collective-permute-start(bf16[2,4,128,128]{3,2,1,0:T(8,128)(2,1)S(1)} %collective-permute-done.4), channel_id=1, source_target_pairs={{0,448},{16,464},{32,480},{48,496},{64,0},{80,16},{96,32},{112,48}... | collective-permute-start | bytes 786440 | tf_op jit(solution)/shard_map/ppermute | solution.py:210
  109.2 9.4 %collective-permute-done.5 = bf16[2,4,128,128]{3,2,1,0:T(8,128)(2,1)S(1)} collective-permute-done((bf16[2,4,128,128]{3,2,1,0:T(8,128)(2,1)S(1)}, bf16[2,4,128,128]{3,2,1,0:T(8,128)(2,1)S(1)}, u32[]{:S(2)}, u32[]{:S(2)}) %collective-permute-start.5) | collective-permute-done | bytes 262176 | tf_op jit(solution)/shard_map/ppermute | solution.py:210
  118.5 1.9 %collective-permute-start.7 = (bf16[2,4,128,128]{3,2,1,0:T(8,128)(2,1)S(1)}, bf16[2,4,128,128]{3,2,1,0:T(8,128)(2,1)S(1)}, u32[]{:S(2)}, u32[]{:S(2)}) collective-permute-start(bf16[2,4,128,128]{3,2,1,0:T(8,128)(2,1)S(1)} %collective-permute-done.5), channel_id=1, source_target_pairs={{0,64},{16,80},{32,96},{48,112},{64,128},{80,144},{96,160},{112,17... | collective-permute-start | bytes 786440 | tf_op jit(solution)/shard_map/ppermute | solution.py:210
  120.5 4.6 %collective-permute-start.8 = (bf16[2,4,128,128]{3,2,1,0:T(8,128)(2,1)S(1)}, bf16[2,4,128,128]{3,2,1,0:T(8,128)(2,1)S(1)}, u32[]{:S(2)}, u32[]{:S(2)}) collective-permute-start(bf16[2,4,128,128]{3,2,1,0:T(8,128)(2,1)S(1)} %collective-permute-done.6), channel_id=1, source_target_pairs={{0,448},{16,464},{32,480},{48,496},{64,0},{80,16},{96,32},{112,48}... | collective-permute-start | bytes 786440 | tf_op jit(solution)/shard_map/ppermute | solution.py:210
  126.9 1.9 %collective-permute-start.9 = (bf16[2,4,128,128]{3,2,1,0:T(8,128)(2,1)S(1)}, bf16[2,4,128,128]{3,2,1,0:T(8,128)(2,1)S(1)}, u32[]{:S(2)}, u32[]{:S(2)}) collective-permute-start(bf16[2,4,128,128]{3,2,1,0:T(8,128)(2,1)S(1)} %collective-permute-done.7), channel_id=1, source_target_pairs={{0,64},{16,80},{32,96},{48,112},{64,128},{80,144},{96,160},{112,17... | collective-permute-start | bytes 786440 | tf_op jit(solution)/shard_map/ppermute | solution.py:210
  128.9 6.3 %collective-permute-done.9 = bf16[2,4,128,128]{3,2,1,0:T(8,128)(2,1)S(1)} collective-permute-done((bf16[2,4,128,128]{3,2,1,0:T(8,128)(2,1)S(1)}, bf16[2,4,128,128]{3,2,1,0:T(8,128)(2,1)S(1)}, u32[]{:S(2)}, u32[]{:S(2)}) %collective-permute-start.9) | collective-permute-done | bytes 262176 | tf_op jit(solution)/shard_map/ppermute | solution.py:210
  136.6 6.4 %hidden_grad.1 = (f32[128,768]{1,0:T(8,128)}, f32[128,768]{1,0:T(8,128)}) custom-call(s32[128]{0:T(128)} %get-tuple-element.11.table_ref, s32[2]{0:T(128)} %copy-done.6, bf16[256,8192]{1,0:T(8,128)(2,1)} %bitcast.28, bf16[16,4,128,128]{3,2,1,0:T(8,128)(2,1)} %bitcast.30), custom_call_target="tpu_custom_call" | custom-call | flops 536870912 | bytes 6291456 | tf_op jit(solution)/shard_map/hidden_grad/pallas_call | solution.py:334
  143.0 6.7 %collective-permute-start.10 = (f32[128,768]{1,0:T(8,128)}, f32[128,768]{1,0:T(8,128)S(1)}, u32[]{:S(2)}, u32[]{:S(2)}) collective-permute-start(f32[128,768]{1,0:T(8,128)} %get-tuple-element.13), channel_id=1, source_target_pairs={{0,16},{16,0},{32,48},{48,32},{64,80},{80,64},{96,112},{112,96},{1... | collective-permute-start | bytes 1179656 | tf_op jit(solution)/shard_map/ppermute | solution.py:210
  154.0 4.6 %collective-permute-start.12 = (bf16[4,128,128]{2,1,0:T(8,128)(2,1)S(1)}, bf16[4,128,128]{2,1,0:T(8,128)(2,1)S(1)}, u32[]{:S(2)}, u32[]{:S(2)}) collective-permute-start(bf16[4,128,128]{2,1,0:T(8,128)(2,1)S(1)} %slice_bitcast_fusion), channel_id=1, source_target_pairs={{0,32},{16,48},{32,0},{48,16},{64,96},{80,112},{96,64},{112,80},{1... | collective-permute-start | bytes 393224 | tf_op jit(solution)/shard_map/ppermute | solution.py:210
  159.6 2.5 %collective-permute-done.12.other_ref = bf16[4,128,128]{2,1,0:T(8,128)(2,1)S(1)} collective-permute-done((bf16[4,128,128]{2,1,0:T(8,128)(2,1)S(1)}, bf16[4,128,128]{2,1,0:T(8,128)(2,1)S(1)}, u32[]{:S(2)}, u32[]{:S(2)}) %collective-permute-start.12) | collective-permute-done | bytes 131104 | tf_op jit(solution)/shard_map/ppermute | solution.py:210
  (52 shorter events, 18.7 us)
Async XLA Ops:
  7.2 61.3 %all-gather.2.cloned.1.call-start = ((), (), s32[]{:S(2)}) async-start(), calls=%async_computation.1 | async-start | bytes 4456448 | tf_op jit(solution)/shard_map/all_gather | solution.py:273
  7.2 8.4 %collective-permute-start.1 = (bf16[8,8192]{1,0:T(8,128)(2,1)}, bf16[8,8192]{1,0:T(8,128)(2,1)S(1)}, u32[]{:S(2)}, u32[]{:S(2)}) collective-permute-start(bf16[8,8192]{1,0:T(8,128)(2,1)} %param.6), channel_id=1, source_target_pairs={{0,8},{1,9},{2,10},{3,11},{4,12},{5,13},{6,14},{7,15},{8,0},{9,1},... | collective-permute-start | bytes 393224 | tf_op jit(solution)/shard_map/ppermute | solution.py:213
  11.2 4.4 %collective-permute-start = (s32[1]{0:T(128)}, s32[1]{0:T(128)}, u32[]{:S(2)}, u32[]{:S(2)}) collective-permute-start(s32[1]{0:T(128)} %param.7), channel_id=1, source_target_pairs={{0,8},{1,9},{2,10},{3,11},{4,12},{5,13},{6,14},{7,15},{8,0},{9,1},... | collective-permute-start | bytes 20 | tf_op jit(solution)/shard_map/ppermute | solution.py:213
  17.0 136.2 %reduce-scatter.2.cloned.1.call-start = ((), (), s32[]{:S(2)}) async-start(), calls=%async_computation.2 | async-start | bytes 2359296 | tf_op jit(solution)/shard_map/reduce_scatter | solution.py:323
  19.4 9.3 %collective-permute-start.11 = (bf16[128,768]{1,0:T(8,128)(2,1)}, bf16[128,768]{1,0:T(8,128)(2,1)S(1)}, u32[]{:S(2)}, u32[]{:S(2)}) collective-permute-start(bf16[128,768]{1,0:T(8,128)(2,1)} %get-tuple-element.16.own_ref), channel_id=1, source_target_pairs={{0,16},{16,0},{32,48},{48,32},{64,80},{80,64},{96,112},{112,96},{1... | collective-permute-start | bytes 589832 | tf_op jit(solution)/shard_map/ppermute | solution.py:210
  27.5 47.1 %copy-start.6 = (s32[2]{0:T(128)}, s32[2]{0:T(128)S(1)}, u32[]{:S(2)}) copy-start(s32[2]{0:T(128)S(1)} %pad_add_fusion.core_ref) | copy-start | bytes 28
  28.7 0.9 copy-start.4
  68.4 2.2 %copy-start = (bf16[32,8,8192]{2,1,0:T(8,128)(2,1)S(1)}, bf16[32,8,8192]{2,1,0:T(8,128)(2,1)}, u32[]{:S(2)}) copy-start(bf16[32,8,8192]{2,1,0:T(8,128)(2,1)} %all-gather.2.cloned.1.call-done) | copy-start | bytes 12582916
  76.5 16.5 %copy-start.9 = (bf16[4,128,128]{2,1,0:T(8,128)(2,1)S(1)}, bf16[4,128,128]{2,1,0:T(8,128)(2,1)}, u32[]{:S(2)}) copy-start(bf16[4,128,128]{2,1,0:T(8,128)(2,1)} %pack.1) | copy-start | bytes 393220
  76.5 8.5 %collective-permute-start.2 = (bf16[4,128,128]{2,1,0:T(8,128)(2,1)}, bf16[4,128,128]{2,1,0:T(8,128)(2,1)S(1)}, u32[]{:S(2)}, u32[]{:S(2)}) collective-permute-start(bf16[4,128,128]{2,1,0:T(8,128)(2,1)} %pack.1), channel_id=1, source_target_pairs={{0,32},{16,48},{32,0},{48,16},{64,96},{80,112},{96,64},{112,80},{1... | collective-permute-start | bytes 393224 | tf_op jit(solution)/shard_map/ppermute | solution.py:210
  86.0 16.6 %collective-permute-start.3 = (bf16[2,4,128,128]{3,2,1,0:T(8,128)(2,1)S(1)}, bf16[2,4,128,128]{3,2,1,0:T(8,128)(2,1)S(1)}, u32[]{:S(2)}, u32[]{:S(2)}) collective-permute-start(bf16[2,4,128,128]{3,2,1,0:T(8,128)(2,1)S(1)} %broadcast_select_fusion), channel_id=1, source_target_pairs={{0,64},{16,80},{32,96},{48,112},{64,128},{80,144},{96,160},{112,17... | collective-permute-start | bytes 786440 | tf_op jit(solution)/shard_map/ppermute | solution.py:210
  89.1 15.4 %collective-permute-start.4 = (bf16[2,4,128,128]{3,2,1,0:T(8,128)(2,1)S(1)}, bf16[2,4,128,128]{3,2,1,0:T(8,128)(2,1)S(1)}, u32[]{:S(2)}, u32[]{:S(2)}) collective-permute-start(bf16[2,4,128,128]{3,2,1,0:T(8,128)(2,1)S(1)} %broadcast_select_fusion), channel_id=1, source_target_pairs={{0,448},{16,464},{32,480},{48,496},{64,0},{80,16},{96,32},{112,48}... | collective-permute-start | bytes 786440 | tf_op jit(solution)/shard_map/ppermute | solution.py:210
  102.6 16.0 %collective-permute-start.5 = (bf16[2,4,128,128]{3,2,1,0:T(8,128)(2,1)S(1)}, bf16[2,4,128,128]{3,2,1,0:T(8,128)(2,1)S(1)}, u32[]{:S(2)}, u32[]{:S(2)}) collective-permute-start(bf16[2,4,128,128]{3,2,1,0:T(8,128)(2,1)S(1)} %collective-permute-done.3), channel_id=1, source_target_pairs={{0,64},{16,80},{32,96},{48,112},{64,128},{80,144},{96,160},{112,17... | collective-permute-start | bytes 786440 | tf_op jit(solution)/shard_map/ppermute | solution.py:210
  104.5 16.0 %collective-permute-start.6 = (bf16[2,4,128,128]{3,2,1,0:T(8,128)(2,1)S(1)}, bf16[2,4,128,128]{3,2,1,0:T(8,128)(2,1)S(1)}, u32[]{:S(2)}, u32[]{:S(2)}) collective-permute-start(bf16[2,4,128,128]{3,2,1,0:T(8,128)(2,1)S(1)} %collective-permute-done.4), channel_id=1, source_target_pairs={{0,448},{16,464},{32,480},{48,496},{64,0},{80,16},{96,32},{112,48}... | collective-permute-start | bytes 786440 | tf_op jit(solution)/shard_map/ppermute | solution.py:210
  118.5 8.3 %collective-permute-start.7 = (bf16[2,4,128,128]{3,2,1,0:T(8,128)(2,1)S(1)}, bf16[2,4,128,128]{3,2,1,0:T(8,128)(2,1)S(1)}, u32[]{:S(2)}, u32[]{:S(2)}) collective-permute-start(bf16[2,4,128,128]{3,2,1,0:T(8,128)(2,1)S(1)} %collective-permute-done.5), channel_id=1, source_target_pairs={{0,64},{16,80},{32,96},{48,112},{64,128},{80,144},{96,160},{112,17... | collective-permute-start | bytes 786440 | tf_op jit(solution)/shard_map/ppermute | solution.py:210
  120.5 8.4 %collective-permute-start.8 = (bf16[2,4,128,128]{3,2,1,0:T(8,128)(2,1)S(1)}, bf16[2,4,128,128]{3,2,1,0:T(8,128)(2,1)S(1)}, u32[]{:S(2)}, u32[]{:S(2)}) collective-permute-start(bf16[2,4,128,128]{3,2,1,0:T(8,128)(2,1)S(1)} %collective-permute-done.6), channel_id=1, source_target_pairs={{0,448},{16,464},{32,480},{48,496},{64,0},{80,16},{96,32},{112,48}... | collective-permute-start | bytes 786440 | tf_op jit(solution)/shard_map/ppermute | solution.py:210
  126.9 8.3 %collective-permute-start.9 = (bf16[2,4,128,128]{3,2,1,0:T(8,128)(2,1)S(1)}, bf16[2,4,128,128]{3,2,1,0:T(8,128)(2,1)S(1)}, u32[]{:S(2)}, u32[]{:S(2)}) collective-permute-start(bf16[2,4,128,128]{3,2,1,0:T(8,128)(2,1)S(1)} %collective-permute-done.7), channel_id=1, source_target_pairs={{0,64},{16,80},{32,96},{48,112},{64,128},{80,144},{96,160},{112,17... | collective-permute-start | bytes 786440 | tf_op jit(solution)/shard_map/ppermute | solution.py:210
  135.2 1.4 copy-start.8
  136.6 14.6 %copy-start.1 = (bf16[128,768]{1,0:T(8,128)(2,1)S(1)}, bf16[128,768]{1,0:T(8,128)(2,1)}, u32[]{:S(2)}) copy-start(bf16[128,768]{1,0:T(8,128)(2,1)} %gate_ref.3) | copy-start | bytes 589828
  136.6 14.6 %copy-start.2 = (bf16[128,768]{1,0:T(8,128)(2,1)S(1)}, bf16[128,768]{1,0:T(8,128)(2,1)}, u32[]{:S(2)}) copy-start(bf16[128,768]{1,0:T(8,128)(2,1)} %up_ref.3) | copy-start | bytes 589828
  136.6 25.5 %copy-start.5 = (s32[6,64]{1,0:T(8,128)S(1)}, s32[6,64]{1,0:T(8,128)}, u32[]{:S(2)}) copy-start(s32[6,64]{1,0:T(8,128)} %mask_ref.5) | copy-start | bytes 4612
  143.0 8.2 %collective-permute-start.10 = (f32[128,768]{1,0:T(8,128)}, f32[128,768]{1,0:T(8,128)S(1)}, u32[]{:S(2)}, u32[]{:S(2)}) collective-permute-start(f32[128,768]{1,0:T(8,128)} %get-tuple-element.13), channel_id=1, source_target_pairs={{0,16},{16,0},{32,48},{48,32},{64,80},{80,64},{96,112},{112,96},{1... | collective-permute-start | bytes 1179656 | tf_op jit(solution)/shard_map/ppermute | solution.py:210
  151.2 1.0 copy-start.3
  154.0 8.1 %collective-permute-start.12 = (bf16[4,128,128]{2,1,0:T(8,128)(2,1)S(1)}, bf16[4,128,128]{2,1,0:T(8,128)(2,1)S(1)}, u32[]{:S(2)}, u32[]{:S(2)}) collective-permute-start(bf16[4,128,128]{2,1,0:T(8,128)(2,1)S(1)} %slice_bitcast_fusion), channel_id=1, source_target_pairs={{0,32},{16,48},{32,0},{48,16},{64,96},{80,112},{96,64},{112,80},{1... | collective-permute-start | bytes 393224 | tf_op jit(solution)/shard_map/ppermute | solution.py:210
  (1 other events, 0.7 us)
Sparse Core Ops, SparseCore 0:
  17.1 51.3 all-gather.1
  74.8 47.5 reduce-scatter.1
